TPU v7x, 512 devices: a whole 4x8x8 slice. The times are simulated.
512 devices in a mesh: gz: 8 (over x, core), gy: 8 (over z), gx: 8 (over y).
Axes of the slice: x: 4, y: 8, z: 8, core: 2. Of those that a mesh axis runs over, the one named last changes fastest.
Arguments:
- source: float32 [2, 64, 256, 1024], P(None, 'gz', 'gy', 'gx'), may hold values from -6 to 6
- adjoint_start: float32 [2, 64, 256, 1024], P(None, 'gz', 'gy', 'gx'), may hold values from -4 to 4
- couple: float32 [6, 64, 256, 1024], P(None, 'gz', 'gy', 'gx'), may hold values from 0.15 to 2.4
- diag_inverse: float32 [2, 64, 256, 1024], P(None, 'gz', 'gy', 'gx'), may hold values from 0.1 to 0.16
- cross_inverse: float32 [2, 64, 256, 1024], P(None, 'gz', 'gy', 'gx'), may hold values from -0.04 to 0.04
- perf_row: int32 [8, 8, 8, 64], P('gz', 'gy', 'gx'), may hold values from 0 to 255, as said below
- well_owner: int32 [8, 8, 8, 64, 1], P('gz', 'gy', 'gx'), may hold values from 0 to 63; in each aligned block of 64 rows (0 to 63, 64 to 127, ..., all dimensions but the last counted through in order) at most 2 rows name the same one
- well_slot: int32 [8, 8, 8, 64], P('gz', 'gy', 'gx'), may hold values from 0 to 3
- well_block: bfloat16 [8, 8, 8, 4, 256, 256], P('gz', 'gy', 'gx'), may hold values from -0.375 to 0.375
- cross_block: bfloat16 [8, 8, 8, 4, 256, 256], P('gz', 'gy', 'gx'), may hold values from -0.09375 to 0.09375
Outputs:
- adjoint: float32 [2, 64, 256, 1024], P(None, 'gz', 'gy', 'gx')
Inputs may be any that keep to these rules, and one draw needn't show every extreme that they name: `perf_row`: the 64 rows of one device are distinct. `well_owner`: at most 2 of one device's panels name the same owner.
All inputs are finite; a program needn't handle non-finite values.
Results may differ from a plain program's by a relative error of at most 0.0015.
Values may be sent and summed in bfloat16 or wider, within the bound.
No kernel may reach another device: no remote copies, remote signals or barrier semaphores. Data moves between devices by JAX's collectives and lax.ppermute only.
A program may use at most 64 MiB of HBM per device.

v0:
```python
import jax
import jax.numpy as jnp
from jax import lax
from jax.sharding import PartitionSpec as P

SWEEPS = 4
OUTER = 2


def padded_2(block, sides, width):
    for axis, dim in sides:
        count = lax.axis_size(axis)
        forward = [(i, i + 1) for i in range(count - 1)]
        backward = [(target, source) for source, target in forward]
        low = lax.ppermute(
            lax.slice_in_dim(block, block.shape[dim] - width, None, axis=dim), axis, forward
        )
        high = lax.ppermute(lax.slice_in_dim(block, 0, width, axis=dim), axis, backward)
        block = jnp.concatenate([low, block, high], axis=dim)
    return block


def neighbours(padded, couple):
    summed = couple[0] * padded[:, 2:, 1:-1, 1:-1]
    summed = summed + couple[1] * padded[:, :-2, 1:-1, 1:-1]
    summed = summed + couple[2] * padded[:, 1:-1, 2:, 1:-1]
    summed = summed + couple[3] * padded[:, 1:-1, :-2, 1:-1]
    summed = summed + couple[4] * padded[:, 1:-1, 1:-1, 2:]
    summed = summed + couple[5] * padded[:, 1:-1, 1:-1, :-2]
    return summed


def jacobi_sweep(padded, right_side, couple, diag_inverse, cross_inverse):
    inflow = right_side + neighbours(padded, couple)
    first_comp = diag_inverse[0] * inflow[0] + cross_inverse[0] * inflow[1]
    second_comp = cross_inverse[1] * inflow[0] + diag_inverse[1] * inflow[1]
    return jnp.stack([first_comp, second_comp])


def gather_panels(adjoint, perf_rows):
    block_rows = adjoint.reshape(2, -1, adjoint.shape[3])
    picked = jnp.take(block_rows, perf_rows, axis=1)
    return picked.transpose(1, 0, 2).reshape(perf_rows.shape[0], -1).astype(jnp.bfloat16)


def owner_work(arrived, arrived_ids, well_mats, cross_mats):
    well_count = well_mats.shape[0]
    labels = jnp.arange(well_count, dtype=jnp.int32).astype(jnp.bfloat16)
    select = arrived_ids[None, :] == labels[:, None]
    totals = jnp.dot(
        select.astype(jnp.bfloat16), arrived, preferred_element_type=jnp.float32
    ).astype(jnp.bfloat16)
    own_term = jnp.einsum("sd,wde->wse", arrived, well_mats, preferred_element_type=jnp.float32)
    crossed = jnp.einsum("wd,wde->we", totals, cross_mats, preferred_element_type=jnp.float32)
    weights = select.astype(jnp.float32)[:, :, None]
    mixed_out = jnp.sum(weights * (own_term + crossed[:, None, :]), axis=0)
    return mixed_out.astype(jnp.bfloat16)


def per_device(
    source,
    adjoint_start,
    couple,
    diag_inverse,
    cross_inverse,
    perf_row,
    well_owner,
    well_slot,
    well_block,
    cross_block,
):
    rows_y = lax.axis_size("gy")
    cols_x = lax.axis_size("gx")
    owners = rows_y * cols_x
    perf_rows = perf_row.reshape(-1)
    panel_count = perf_rows.shape[0]
    capacity = max(2, 2 * panel_count // owners)
    targets = well_owner.reshape(-1)
    slot_ids = well_slot.reshape(-1)
    matches = (targets[:, None] == jnp.arange(owners, dtype=jnp.int32)[None, :]).astype(jnp.int32)
    slot_rank = jnp.sum((jnp.cumsum(matches, axis=0) - 1) * matches, axis=1)
    destination = targets * capacity + slot_rank
    well_mats = well_block.reshape(well_block.shape[3], well_block.shape[4], well_block.shape[5])
    cross_mats = cross_block.reshape(
        cross_block.shape[3], cross_block.shape[4], cross_block.shape[5]
    )
    panel_width = well_mats.shape[1]
    ids_sent = (
        jnp.full((owners * capacity,), -1.0, jnp.bfloat16)
        .at[destination]
        .set(slot_ids.astype(jnp.bfloat16))
    )
    layers_dev = adjoint_start.shape[1]
    rows_dev = adjoint_start.shape[2]
    cols_dev = adjoint_start.shape[3]
    adjoint = adjoint_start
    for outer_step in range(OUTER):
        panels = gather_panels(adjoint, perf_rows)
        outgoing = (
            jnp.zeros((owners * capacity, panel_width), jnp.bfloat16).at[destination].set(panels)
        )
        arrived, arrived_ids = (
            lax.all_to_all(
                outgoing.reshape(owners, capacity, panel_width),
                ("gy", "gx"),
                split_axis=0,
                concat_axis=0,
                tiled=True,
            ),
            lax.all_to_all(
                ids_sent.reshape(owners, capacity),
                ("gy", "gx"),
                split_axis=0,
                concat_axis=0,
                tiled=True,
            ),
        )
        mixed_out = owner_work(
            arrived.reshape(-1, panel_width), arrived_ids.reshape(-1), well_mats, cross_mats
        )
        returned = lax.all_to_all(
            mixed_out.reshape(owners, capacity, panel_width),
            ("gy", "gx"),
            split_axis=0,
            concat_axis=0,
            tiled=True,
        )
        values = returned.reshape(owners * capacity, panel_width)[destination].astype(jnp.float32)
        placed = (
            jnp.zeros((layers_dev * rows_dev, 2, cols_dev), jnp.float32)
            .at[perf_rows]
            .set(values.reshape(-1, 2, cols_dev))
        )
        right_side = source + placed.transpose(1, 0, 2).reshape(2, layers_dev, rows_dev, cols_dev)
        for sweep_step in range(SWEEPS):
            padded = padded_2(adjoint, (("gz", 1), ("gy", 2), ("gx", 3)), 1)
            adjoint = jacobi_sweep(padded, right_side, couple, diag_inverse, cross_inverse)
    return adjoint


def solution(mesh):
    placed = (
        P(None, "gz", "gy", "gx"),
        P(None, "gz", "gy", "gx"),
        P(None, "gz", "gy", "gx"),
        P(None, "gz", "gy", "gx"),
        P(None, "gz", "gy", "gx"),
        P("gz", "gy", "gx", None),
        P("gz", "gy", "gx", None, None),
        P("gz", "gy", "gx", None),
        P("gz", "gy", "gx", None, None, None),
        P("gz", "gy", "gx", None, None, None),
    )
    return jax.shard_map(
        per_device, mesh=mesh, in_specs=placed, out_specs=P(None, "gz", "gy", "gx"), check_vma=False
    )
```

profile of v0, /device:TPU:1, one launch (start us, length us, event | category | flops | bytes accessed | tf_op | source)
XLA Modules:
  0.0 326.0 jit_solution(471143538459804983)
XLA Ops:
  3.5 17.1 %all-to-all-start = ((bf16[64,1,2]{2,1,0:T(2,128)(2,1)}), bf16[64,1,2]{2,1,0:T(2,128)(2,1)S(1)}, u32[]{:S(2)}, u32[]{:S(2)}) async-start(bf16[64,1,2]{2,1,0:T(2,128)(2,1)} %all_to_all.25), calls=%async_computation | async-start | bytes 65536 | tf_op jit(solution)/shard_map/all_to_all | solution.py:110
  31.5 12.2 %all-to-all-start.1 = ((bf16[64,2,256]{2,1,0:T(2,128)(2,1)}), bf16[64,2,256]{2,1,0:T(2,128)(2,1)S(1)}, u32[]{:S(2)}, u32[]{:S(2)}) async-start(bf16[64,2,256]{2,1,0:T(2,128)(2,1)} %reshape.169), calls=%async_computation.1 | async-start | bytes 131072 | tf_op jit(solution)/shard_map/all_to_all | solution.py:103
  56.1 9.9 %all-to-all-start.2 = ((bf16[64,2,256]{2,1,0:T(2,128)(2,1)}), bf16[64,2,256]{2,1,0:T(2,128)(2,1)S(1)}, u32[]{:S(2)}, u32[]{:S(2)}) async-start(bf16[64,2,256]{2,1,0:T(2,128)(2,1)} %convert_element_type.89), calls=%async_computation.2 | async-start | bytes 131072 | tf_op jit(solution)/shard_map/all_to_all | solution.py:121
  68.4 4.7 %collective-permute-start.5 = (f32[2,10,34,1]{3,2,1,0:T(8,128)}, f32[2,10,34,1]{3,2,1,0:T(8,128)}, u32[]{:S(2)}, u32[]{:S(2)}) collective-permute-start(f32[2,10,34,1]{3,2,1,0:T(8,128)} %get-tuple-element.47), channel_id=1, source_target_pairs={{0,1},{1,2},{2,3},{3,4},{4,5},{5,6},{6,7},{8,9},{9,10},{10,11},{11... | collective-permute-start | bytes 8168 | tf_op jit(solution)/shard_map/ppermute | solution.py:15
  73.1 4.1 %all-to-all-done.2 = bf16[64,2,256]{2,1,0:T(2,128)(2,1)S(1)} async-done(((bf16[64,2,256]{2,1,0:T(2,128)(2,1)}), bf16[64,2,256]{2,1,0:T(2,128)(2,1)S(1)}, u32[]{:S(2)}, u32[]{:S(2)}) %all-to-all-start.2) | async-done | bytes 65568 | tf_op jit(solution)/shard_map/all_to_all | solution.py:121
  86.2 5.7 %collective-permute-start.7 = (f32[2,1,32,128]{3,2,1,0:T(8,128)S(1)}, f32[2,1,32,128]{3,2,1,0:T(8,128)S(1)}, u32[]{:S(2)}, u32[]{:S(2)}) collective-permute-start(f32[2,1,32,128]{3,2,1,0:T(8,128)S(1)} %get-tuple-element.76), channel_id=1, source_target_pairs={{0,64},{64,128},{128,192},{192,256},{256,320},{320,384},{384,448},... | collective-permute-start | bytes 98312 | tf_op jit(solution)/shard_map/ppermute | solution.py:15
  100.5 4.0 %collective-permute-start.11 = (f32[2,10,34,1]{3,2,1,0:T(8,128)S(1)}, f32[2,10,34,1]{3,2,1,0:T(8,128)S(1)}, u32[]{:S(2)}, u32[]{:S(2)}) collective-permute-start(f32[2,10,34,1]{3,2,1,0:T(8,128)S(1)} %get-tuple-element.45), channel_id=1, source_target_pairs={{0,1},{1,2},{2,3},{3,4},{4,5},{5,6},{6,7},{8,9},{9,10},{10,11},{11... | collective-permute-start | bytes 8168 | tf_op jit(solution)/shard_map/ppermute | solution.py:15
  104.6 6.1 %collective-permute-done.10 = f32[2,10,34,1]{3,2,1,0:T(8,128)S(1)} collective-permute-done((f32[2,10,34,1]{3,2,1,0:T(8,128)S(1)}, f32[2,10,34,1]{3,2,1,0:T(8,128)S(1)}, u32[]{:S(2)}, u32[]{:S(2)}) %collective-permute-start.10) | collective-permute-done | bytes 2752 | tf_op jit(solution)/shard_map/ppermute | solution.py:18
  114.8 4.8 %collective-permute-start.13 = (f32[2,1,32,128]{3,2,1,0:T(8,128)S(1)}, f32[2,1,32,128]{3,2,1,0:T(8,128)S(1)}, u32[]{:S(2)}, u32[]{:S(2)}) collective-permute-start(f32[2,1,32,128]{3,2,1,0:T(8,128)S(1)} %get-tuple-element.74), channel_id=1, source_target_pairs={{0,64},{64,128},{128,192},{192,256},{256,320},{320,384},{384,448},... | collective-permute-start | bytes 98312 | tf_op jit(solution)/shard_map/ppermute | solution.py:15
  121.9 4.2 %collective-permute-start.15 = (f32[2,10,1,128]{3,2,1,0:T(1,128)S(1)}, f32[2,10,1,128]{3,2,1,0:T(1,128)S(1)}, u32[]{:S(2)}, u32[]{:S(2)}) collective-permute-start(f32[2,10,1,128]{3,2,1,0:T(1,128)S(1)} %get-tuple-element.58), channel_id=1, source_target_pairs={{0,8},{8,16},{16,24},{24,32},{32,40},{40,48},{48,56},{1,9},{9,17},... | collective-permute-start | bytes 30728 | tf_op jit(solution)/shard_map/ppermute | solution.py:15
  128.5 4.8 %collective-permute-start.17 = (f32[2,10,34,1]{3,2,1,0:T(8,128)S(1)}, f32[2,10,34,1]{3,2,1,0:T(8,128)S(1)}, u32[]{:S(2)}, u32[]{:S(2)}) collective-permute-start(f32[2,10,34,1]{3,2,1,0:T(8,128)S(1)} %get-tuple-element.43), channel_id=1, source_target_pairs={{0,1},{1,2},{2,3},{3,4},{4,5},{5,6},{6,7},{8,9},{9,10},{10,11},{11... | collective-permute-start | bytes 8168 | tf_op jit(solution)/shard_map/ppermute | solution.py:15
  133.3 6.4 %collective-permute-done.16 = f32[2,10,34,1]{3,2,1,0:T(8,128)S(1)} collective-permute-done((f32[2,10,34,1]{3,2,1,0:T(8,128)S(1)}, f32[2,10,34,1]{3,2,1,0:T(8,128)S(1)}, u32[]{:S(2)}, u32[]{:S(2)}) %collective-permute-start.16) | collective-permute-done | bytes 2752 | tf_op jit(solution)/shard_map/ppermute | solution.py:18
  143.9 4.2 %collective-permute-start.19 = (f32[2,1,32,128]{3,2,1,0:T(8,128)S(1)}, f32[2,1,32,128]{3,2,1,0:T(8,128)S(1)}, u32[]{:S(2)}, u32[]{:S(2)}) collective-permute-start(f32[2,1,32,128]{3,2,1,0:T(8,128)S(1)} %get-tuple-element.72), channel_id=1, source_target_pairs={{0,64},{64,128},{128,192},{192,256},{256,320},{320,384},{384,448},... | collective-permute-start | bytes 98312 | tf_op jit(solution)/shard_map/ppermute | solution.py:15
  150.4 4.5 %collective-permute-start.21 = (f32[2,10,1,128]{3,2,1,0:T(1,128)S(1)}, f32[2,10,1,128]{3,2,1,0:T(1,128)S(1)}, u32[]{:S(2)}, u32[]{:S(2)}) collective-permute-start(f32[2,10,1,128]{3,2,1,0:T(1,128)S(1)} %get-tuple-element.56), channel_id=1, source_target_pairs={{0,8},{8,16},{16,24},{24,32},{32,40},{40,48},{48,56},{1,9},{9,17},... | collective-permute-start | bytes 30728 | tf_op jit(solution)/shard_map/ppermute | solution.py:15
  157.3 4.8 %collective-permute-start.23 = (f32[2,10,34,1]{3,2,1,0:T(8,128)S(1)}, f32[2,10,34,1]{3,2,1,0:T(8,128)S(1)}, u32[]{:S(2)}, u32[]{:S(2)}) collective-permute-start(f32[2,10,34,1]{3,2,1,0:T(8,128)S(1)} %get-tuple-element.41), channel_id=1, source_target_pairs={{0,1},{1,2},{2,3},{3,4},{4,5},{5,6},{6,7},{8,9},{9,10},{10,11},{11... | collective-permute-start | bytes 8168 | tf_op jit(solution)/shard_map/ppermute | solution.py:15
  162.0 7.2 %collective-permute-done.22 = f32[2,10,34,1]{3,2,1,0:T(8,128)S(1)} collective-permute-done((f32[2,10,34,1]{3,2,1,0:T(8,128)S(1)}, f32[2,10,34,1]{3,2,1,0:T(8,128)S(1)}, u32[]{:S(2)}, u32[]{:S(2)}) %collective-permute-start.22) | collective-permute-done | bytes 2752 | tf_op jit(solution)/shard_map/ppermute | solution.py:18
  179.4 4.4 %collective-permute-start.27 = (f32[2,10,1,128]{3,2,1,0:T(1,128)S(1)}, f32[2,10,1,128]{3,2,1,0:T(1,128)S(1)}, u32[]{:S(2)}, u32[]{:S(2)}) collective-permute-start(f32[2,10,1,128]{3,2,1,0:T(1,128)S(1)} %get-tuple-element.54), channel_id=1, source_target_pairs={{0,8},{8,16},{16,24},{24,32},{32,40},{40,48},{48,56},{1,9},{9,17},... | collective-permute-start | bytes 30728 | tf_op jit(solution)/shard_map/ppermute | solution.py:15
  185.6 17.9 %all-to-all-start.3 = ((bf16[64,2,256]{2,1,0:T(2,128)(2,1)}), bf16[64,2,256]{2,1,0:T(2,128)(2,1)S(1)}, u32[]{:S(2)}, u32[]{:S(2)}) async-start(bf16[64,2,256]{2,1,0:T(2,128)(2,1)} %reshape.175), calls=%async_computation.3 | async-start | bytes 131072 | tf_op jit(solution)/shard_map/all_to_all | solution.py:103
  203.7 11.0 %all-to-all-done.3 = bf16[64,2,256]{2,1,0:T(2,128)(2,1)S(1)} async-done(((bf16[64,2,256]{2,1,0:T(2,128)(2,1)}), bf16[64,2,256]{2,1,0:T(2,128)(2,1)S(1)}, u32[]{:S(2)}, u32[]{:S(2)}) %all-to-all-start.3) | async-done | bytes 65568 | tf_op jit(solution)/shard_map/all_to_all | solution.py:103
  216.7 4.6 %all-to-all-start.4 = ((bf16[64,2,256]{2,1,0:T(2,128)(2,1)}), bf16[64,2,256]{2,1,0:T(2,128)(2,1)S(1)}, u32[]{:S(2)}, u32[]{:S(2)}) async-start(bf16[64,2,256]{2,1,0:T(2,128)(2,1)} %convert_element_type.97), calls=%async_computation.4 | async-start | bytes 131072 | tf_op jit(solution)/shard_map/all_to_all | solution.py:121
  223.6 4.7 %collective-permute-start.29 = (f32[2,10,34,1]{3,2,1,0:T(8,128)}, f32[2,10,34,1]{3,2,1,0:T(8,128)}, u32[]{:S(2)}, u32[]{:S(2)}) collective-permute-start(f32[2,10,34,1]{3,2,1,0:T(8,128)} %get-tuple-element.39), channel_id=1, source_target_pairs={{0,1},{1,2},{2,3},{3,4},{4,5},{5,6},{6,7},{8,9},{9,10},{10,11},{11... | collective-permute-start | bytes 8168 | tf_op jit(solution)/shard_map/ppermute | solution.py:15
  228.4 4.0 %all-to-all-done.4 = bf16[64,2,256]{2,1,0:T(2,128)(2,1)S(1)} async-done(((bf16[64,2,256]{2,1,0:T(2,128)(2,1)}), bf16[64,2,256]{2,1,0:T(2,128)(2,1)S(1)}, u32[]{:S(2)}, u32[]{:S(2)}) %all-to-all-start.4) | async-done | bytes 65568 | tf_op jit(solution)/shard_map/all_to_all | solution.py:121
  237.8 5.3 %collective-permute-start.30 = (f32[2,1,32,128]{3,2,1,0:T(8,128)S(1)}, f32[2,1,32,128]{3,2,1,0:T(8,128)S(1)}, u32[]{:S(2)}, u32[]{:S(2)}) collective-permute-start(f32[2,1,32,128]{3,2,1,0:T(8,128)S(1)} %get-tuple-element.69), channel_id=1, source_target_pairs={{64,0},{128,64},{192,128},{256,192},{320,256},{384,320},{448,384},... | collective-permute-start | bytes 98312 | tf_op jit(solution)/shard_map/ppermute | solution.py:18
  243.1 4.0 %collective-permute-start.31 = (f32[2,1,32,128]{3,2,1,0:T(8,128)S(1)}, f32[2,1,32,128]{3,2,1,0:T(8,128)S(1)}, u32[]{:S(2)}, u32[]{:S(2)}) collective-permute-start(f32[2,1,32,128]{3,2,1,0:T(8,128)S(1)} %get-tuple-element.68), channel_id=1, source_target_pairs={{0,64},{64,128},{128,192},{192,256},{256,320},{320,384},{384,448},... | collective-permute-start | bytes 98312 | tf_op jit(solution)/shard_map/ppermute | solution.py:15
  255.8 4.0 %collective-permute-start.35 = (f32[2,10,34,1]{3,2,1,0:T(8,128)S(1)}, f32[2,10,34,1]{3,2,1,0:T(8,128)S(1)}, u32[]{:S(2)}, u32[]{:S(2)}) collective-permute-start(f32[2,10,34,1]{3,2,1,0:T(8,128)S(1)} %get-tuple-element.37), channel_id=1, source_target_pairs={{0,1},{1,2},{2,3},{3,4},{4,5},{5,6},{6,7},{8,9},{9,10},{10,11},{11... | collective-permute-start | bytes 8168 | tf_op jit(solution)/shard_map/ppermute | solution.py:15
  259.8 7.8 %collective-permute-done.34 = f32[2,10,34,1]{3,2,1,0:T(8,128)S(1)} collective-permute-done((f32[2,10,34,1]{3,2,1,0:T(8,128)S(1)}, f32[2,10,34,1]{3,2,1,0:T(8,128)S(1)}, u32[]{:S(2)}, u32[]{:S(2)}) %collective-permute-start.34) | collective-permute-done | bytes 2752 | tf_op jit(solution)/shard_map/ppermute | solution.py:18
  277.3 4.0 %collective-permute-start.39 = (f32[2,10,1,128]{3,2,1,0:T(1,128)S(1)}, f32[2,10,1,128]{3,2,1,0:T(1,128)S(1)}, u32[]{:S(2)}, u32[]{:S(2)}) collective-permute-start(f32[2,10,1,128]{3,2,1,0:T(1,128)S(1)} %get-tuple-element.50), channel_id=1, source_target_pairs={{0,8},{8,16},{16,24},{24,32},{32,40},{40,48},{48,56},{1,9},{9,17},... | collective-permute-start | bytes 30728 | tf_op jit(solution)/shard_map/ppermute | solution.py:15
  283.7 4.8 %collective-permute-start.41 = (f32[2,10,34,1]{3,2,1,0:T(8,128)S(1)}, f32[2,10,34,1]{3,2,1,0:T(8,128)S(1)}, u32[]{:S(2)}, u32[]{:S(2)}) collective-permute-start(f32[2,10,34,1]{3,2,1,0:T(8,128)S(1)} %get-tuple-element.35), channel_id=1, source_target_pairs={{0,1},{1,2},{2,3},{3,4},{4,5},{5,6},{6,7},{8,9},{9,10},{10,11},{11... | collective-permute-start | bytes 8168 | tf_op jit(solution)/shard_map/ppermute | solution.py:15
  288.5 7.7 %collective-permute-done.40 = f32[2,10,34,1]{3,2,1,0:T(8,128)S(1)} collective-permute-done((f32[2,10,34,1]{3,2,1,0:T(8,128)S(1)}, f32[2,10,34,1]{3,2,1,0:T(8,128)S(1)}, u32[]{:S(2)}, u32[]{:S(2)}) %collective-permute-start.40) | collective-permute-done | bytes 2752 | tf_op jit(solution)/shard_map/ppermute | solution.py:18
  305.5 4.2 %collective-permute-start.45 = (f32[2,10,1,128]{3,2,1,0:T(1,128)S(1)}, f32[2,10,1,128]{3,2,1,0:T(1,128)S(1)}, u32[]{:S(2)}, u32[]{:S(2)}) collective-permute-start(f32[2,10,1,128]{3,2,1,0:T(1,128)S(1)} %get-tuple-element.48), channel_id=1, source_target_pairs={{0,8},{8,16},{16,24},{24,32},{32,40},{40,48},{48,56},{1,9},{9,17},... | collective-permute-start | bytes 30728 | tf_op jit(solution)/shard_map/ppermute | solution.py:15
  312.0 4.8 %collective-permute-start.47 = (f32[2,10,34,1]{3,2,1,0:T(8,128)S(1)}, f32[2,10,34,1]{3,2,1,0:T(8,128)S(1)}, u32[]{:S(2)}, u32[]{:S(2)}) collective-permute-start(f32[2,10,34,1]{3,2,1,0:T(8,128)S(1)} %get-tuple-element.33), channel_id=1, source_target_pairs={{0,1},{1,2},{2,3},{3,4},{4,5},{5,6},{6,7},{8,9},{9,10},{10,11},{11... | collective-permute-start | bytes 8168 | tf_op jit(solution)/shard_map/ppermute | solution.py:15
  316.7 7.2 %collective-permute-done.46 = f32[2,10,34,1]{3,2,1,0:T(8,128)S(1)} collective-permute-done((f32[2,10,34,1]{3,2,1,0:T(8,128)S(1)}, f32[2,10,34,1]{3,2,1,0:T(8,128)S(1)}, u32[]{:S(2)}, u32[]{:S(2)}) %collective-permute-start.46) | collective-permute-done | bytes 2752 | tf_op jit(solution)/shard_map/ppermute | solution.py:18
  (223 shorter events, 119.4 us)
Async XLA Ops:
  3.5 28.0 %all-to-all-start = ((bf16[64,1,2]{2,1,0:T(2,128)(2,1)}), bf16[64,1,2]{2,1,0:T(2,128)(2,1)S(1)}, u32[]{:S(2)}, u32[]{:S(2)}) async-start(bf16[64,1,2]{2,1,0:T(2,128)(2,1)} %all_to_all.25), calls=%async_computation | async-start | bytes 65536 | tf_op jit(solution)/shard_map/all_to_all | solution.py:110
  21.4 22.5 %collective-permute-start.1 = (f32[2,1,32,128]{3,2,1,0:T(8,128)S(1)}, f32[2,1,32,128]{3,2,1,0:T(8,128)S(1)}, u32[]{:S(2)}, u32[]{:S(2)}) collective-permute-start(f32[2,1,32,128]{3,2,1,0:T(8,128)S(1)} %get-tuple-element.79), channel_id=1, source_target_pairs={{0,64},{64,128},{128,192},{192,256},{256,320},{320,384},{384,448},... | collective-permute-start | bytes 98312 | tf_op jit(solution)/shard_map/ppermute | solution.py:15
  25.4 18.6 %collective-permute-start = (f32[2,1,32,128]{3,2,1,0:T(8,128)S(1)}, f32[2,1,32,128]{3,2,1,0:T(8,128)S(1)}, u32[]{:S(2)}, u32[]{:S(2)}) collective-permute-start(f32[2,1,32,128]{3,2,1,0:T(8,128)S(1)} %get-tuple-element.78), channel_id=1, source_target_pairs={{64,0},{128,64},{192,128},{256,192},{320,256},{384,320},{448,384},... | collective-permute-start | bytes 98312 | tf_op jit(solution)/shard_map/ppermute | solution.py:18
  31.5 23.3 %all-to-all-start.1 = ((bf16[64,2,256]{2,1,0:T(2,128)(2,1)}), bf16[64,2,256]{2,1,0:T(2,128)(2,1)S(1)}, u32[]{:S(2)}, u32[]{:S(2)}) async-start(bf16[64,2,256]{2,1,0:T(2,128)(2,1)} %reshape.169), calls=%async_computation.1 | async-start | bytes 131072 | tf_op jit(solution)/shard_map/all_to_all | solution.py:103
  56.1 21.1 %all-to-all-start.2 = ((bf16[64,2,256]{2,1,0:T(2,128)(2,1)}), bf16[64,2,256]{2,1,0:T(2,128)(2,1)S(1)}, u32[]{:S(2)}, u32[]{:S(2)}) async-start(bf16[64,2,256]{2,1,0:T(2,128)(2,1)} %convert_element_type.89), calls=%async_computation.2 | async-start | bytes 131072 | tf_op jit(solution)/shard_map/all_to_all | solution.py:121
  67.1 13.5 %collective-permute-start.4 = (f32[2,10,34,1]{3,2,1,0:T(8,128)}, f32[2,10,34,1]{3,2,1,0:T(8,128)S(1)}, u32[]{:S(2)}, u32[]{:S(2)}) collective-permute-start(f32[2,10,34,1]{3,2,1,0:T(8,128)} %get-tuple-element.46), channel_id=1, source_target_pairs={{1,0},{2,1},{3,2},{4,3},{5,4},{6,5},{7,6},{9,8},{10,9},{11,10},{12... | collective-permute-start | bytes 8168 | tf_op jit(solution)/shard_map/ppermute | solution.py:18
  68.4 13.0 %collective-permute-start.5 = (f32[2,10,34,1]{3,2,1,0:T(8,128)}, f32[2,10,34,1]{3,2,1,0:T(8,128)}, u32[]{:S(2)}, u32[]{:S(2)}) collective-permute-start(f32[2,10,34,1]{3,2,1,0:T(8,128)} %get-tuple-element.47), channel_id=1, source_target_pairs={{0,1},{1,2},{2,3},{3,4},{4,5},{5,6},{6,7},{8,9},{9,10},{10,11},{11... | collective-permute-start | bytes 8168 | tf_op jit(solution)/shard_map/ppermute | solution.py:15
  83.0 8.9 %collective-permute-start.6 = (f32[2,1,32,128]{3,2,1,0:T(8,128)S(1)}, f32[2,1,32,128]{3,2,1,0:T(8,128)S(1)}, u32[]{:S(2)}, u32[]{:S(2)}) collective-permute-start(f32[2,1,32,128]{3,2,1,0:T(8,128)S(1)} %get-tuple-element.77), channel_id=1, source_target_pairs={{64,0},{128,64},{192,128},{256,192},{320,256},{384,320},{448,384},... | collective-permute-start | bytes 98312 | tf_op jit(solution)/shard_map/ppermute | solution.py:18
  86.2 6.7 %collective-permute-start.7 = (f32[2,1,32,128]{3,2,1,0:T(8,128)S(1)}, f32[2,1,32,128]{3,2,1,0:T(8,128)S(1)}, u32[]{:S(2)}, u32[]{:S(2)}) collective-permute-start(f32[2,1,32,128]{3,2,1,0:T(8,128)S(1)} %get-tuple-element.76), channel_id=1, source_target_pairs={{0,64},{64,128},{128,192},{192,256},{256,320},{320,384},{384,448},... | collective-permute-start | bytes 98312 | tf_op jit(solution)/shard_map/ppermute | solution.py:15
  99.2 11.4 %collective-permute-start.10 = (f32[2,10,34,1]{3,2,1,0:T(8,128)S(1)}, f32[2,10,34,1]{3,2,1,0:T(8,128)S(1)}, u32[]{:S(2)}, u32[]{:S(2)}) collective-permute-start(f32[2,10,34,1]{3,2,1,0:T(8,128)S(1)} %get-tuple-element.44), channel_id=1, source_target_pairs={{1,0},{2,1},{3,2},{4,3},{5,4},{6,5},{7,6},{9,8},{10,9},{11,10},{12... | collective-permute-start | bytes 8168 | tf_op jit(solution)/shard_map/ppermute | solution.py:18
  100.5 11.9 %collective-permute-start.11 = (f32[2,10,34,1]{3,2,1,0:T(8,128)S(1)}, f32[2,10,34,1]{3,2,1,0:T(8,128)S(1)}, u32[]{:S(2)}, u32[]{:S(2)}) collective-permute-start(f32[2,10,34,1]{3,2,1,0:T(8,128)S(1)} %get-tuple-element.45), channel_id=1, source_target_pairs={{0,1},{1,2},{2,3},{3,4},{4,5},{5,6},{6,7},{8,9},{9,10},{10,11},{11... | collective-permute-start | bytes 8168 | tf_op jit(solution)/shard_map/ppermute | solution.py:15
  112.9 6.7 %collective-permute-start.12 = (f32[2,1,32,128]{3,2,1,0:T(8,128)S(1)}, f32[2,1,32,128]{3,2,1,0:T(8,128)S(1)}, u32[]{:S(2)}, u32[]{:S(2)}) collective-permute-start(f32[2,1,32,128]{3,2,1,0:T(8,128)S(1)} %get-tuple-element.75), channel_id=1, source_target_pairs={{64,0},{128,64},{192,128},{256,192},{320,256},{384,320},{448,384},... | collective-permute-start | bytes 98312 | tf_op jit(solution)/shard_map/ppermute | solution.py:18
  127.2 12.5 %collective-permute-start.16 = (f32[2,10,34,1]{3,2,1,0:T(8,128)S(1)}, f32[2,10,34,1]{3,2,1,0:T(8,128)S(1)}, u32[]{:S(2)}, u32[]{:S(2)}) collective-permute-start(f32[2,10,34,1]{3,2,1,0:T(8,128)S(1)} %get-tuple-element.42), channel_id=1, source_target_pairs={{1,0},{2,1},{3,2},{4,3},{5,4},{6,5},{7,6},{9,8},{10,9},{11,10},{12... | collective-permute-start | bytes 8168 | tf_op jit(solution)/shard_map/ppermute | solution.py:18
  128.5 12.9 %collective-permute-start.17 = (f32[2,10,34,1]{3,2,1,0:T(8,128)S(1)}, f32[2,10,34,1]{3,2,1,0:T(8,128)S(1)}, u32[]{:S(2)}, u32[]{:S(2)}) collective-permute-start(f32[2,10,34,1]{3,2,1,0:T(8,128)S(1)} %get-tuple-element.43), channel_id=1, source_target_pairs={{0,1},{1,2},{2,3},{3,4},{4,5},{5,6},{6,7},{8,9},{9,10},{10,11},{11... | collective-permute-start | bytes 8168 | tf_op jit(solution)/shard_map/ppermute | solution.py:15
  141.9 6.1 %collective-permute-start.18 = (f32[2,1,32,128]{3,2,1,0:T(8,128)S(1)}, f32[2,1,32,128]{3,2,1,0:T(8,128)S(1)}, u32[]{:S(2)}, u32[]{:S(2)}) collective-permute-start(f32[2,1,32,128]{3,2,1,0:T(8,128)S(1)} %get-tuple-element.73), channel_id=1, source_target_pairs={{64,0},{128,64},{192,128},{256,192},{320,256},{384,320},{448,384},... | collective-permute-start | bytes 98312 | tf_op jit(solution)/shard_map/ppermute | solution.py:18
  149.1 5.8 %collective-permute-start.20 = (f32[2,10,1,128]{3,2,1,0:T(1,128)S(1)}, f32[2,10,1,128]{3,2,1,0:T(1,128)S(1)}, u32[]{:S(2)}, u32[]{:S(2)}) collective-permute-start(f32[2,10,1,128]{3,2,1,0:T(1,128)S(1)} %get-tuple-element.57), channel_id=1, source_target_pairs={{8,0},{16,8},{24,16},{32,24},{40,32},{48,40},{56,48},{9,1},{17,9},... | collective-permute-start | bytes 30728 | tf_op jit(solution)/shard_map/ppermute | solution.py:18
  156.0 13.3 %collective-permute-start.22 = (f32[2,10,34,1]{3,2,1,0:T(8,128)S(1)}, f32[2,10,34,1]{3,2,1,0:T(8,128)S(1)}, u32[]{:S(2)}, u32[]{:S(2)}) collective-permute-start(f32[2,10,34,1]{3,2,1,0:T(8,128)S(1)} %get-tuple-element.40), channel_id=1, source_target_pairs={{1,0},{2,1},{3,2},{4,3},{5,4},{6,5},{7,6},{9,8},{10,9},{11,10},{12... | collective-permute-start | bytes 8168 | tf_op jit(solution)/shard_map/ppermute | solution.py:18
  157.3 13.8 %collective-permute-start.23 = (f32[2,10,34,1]{3,2,1,0:T(8,128)S(1)}, f32[2,10,34,1]{3,2,1,0:T(8,128)S(1)}, u32[]{:S(2)}, u32[]{:S(2)}) collective-permute-start(f32[2,10,34,1]{3,2,1,0:T(8,128)S(1)} %get-tuple-element.41), channel_id=1, source_target_pairs={{0,1},{1,2},{2,3},{3,4},{4,5},{5,6},{6,7},{8,9},{9,10},{10,11},{11... | collective-permute-start | bytes 8168 | tf_op jit(solution)/shard_map/ppermute | solution.py:15
  171.5 6.5 %collective-permute-start.24 = (f32[2,1,32,128]{3,2,1,0:T(8,128)S(1)}, f32[2,1,32,128]{3,2,1,0:T(8,128)S(1)}, u32[]{:S(2)}, u32[]{:S(2)}) collective-permute-start(f32[2,1,32,128]{3,2,1,0:T(8,128)S(1)} %get-tuple-element.71), channel_id=1, source_target_pairs={{64,0},{128,64},{192,128},{256,192},{320,256},{384,320},{448,384},... | collective-permute-start | bytes 98312 | tf_op jit(solution)/shard_map/ppermute | solution.py:18
  178.1 25.5 %collective-permute-start.26 = (f32[2,10,1,128]{3,2,1,0:T(1,128)S(1)}, f32[2,10,1,128]{3,2,1,0:T(1,128)S(1)}, u32[]{:S(2)}, u32[]{:S(2)}) collective-permute-start(f32[2,10,1,128]{3,2,1,0:T(1,128)S(1)} %get-tuple-element.55), channel_id=1, source_target_pairs={{8,0},{16,8},{24,16},{32,24},{40,32},{48,40},{56,48},{9,1},{17,9},... | collective-permute-start | bytes 30728 | tf_op jit(solution)/shard_map/ppermute | solution.py:18
  179.4 24.2 %collective-permute-start.27 = (f32[2,10,1,128]{3,2,1,0:T(1,128)S(1)}, f32[2,10,1,128]{3,2,1,0:T(1,128)S(1)}, u32[]{:S(2)}, u32[]{:S(2)}) collective-permute-start(f32[2,10,1,128]{3,2,1,0:T(1,128)S(1)} %get-tuple-element.54), channel_id=1, source_target_pairs={{0,8},{8,16},{16,24},{24,32},{32,40},{40,48},{48,56},{1,9},{9,17},... | collective-permute-start | bytes 30728 | tf_op jit(solution)/shard_map/ppermute | solution.py:15
  185.6 29.0 %all-to-all-start.3 = ((bf16[64,2,256]{2,1,0:T(2,128)(2,1)}), bf16[64,2,256]{2,1,0:T(2,128)(2,1)S(1)}, u32[]{:S(2)}, u32[]{:S(2)}) async-start(bf16[64,2,256]{2,1,0:T(2,128)(2,1)} %reshape.175), calls=%async_computation.3 | async-start | bytes 131072 | tf_op jit(solution)/shard_map/all_to_all | solution.py:103
  216.7 15.7 %all-to-all-start.4 = ((bf16[64,2,256]{2,1,0:T(2,128)(2,1)}), bf16[64,2,256]{2,1,0:T(2,128)(2,1)S(1)}, u32[]{:S(2)}, u32[]{:S(2)}) async-start(bf16[64,2,256]{2,1,0:T(2,128)(2,1)} %convert_element_type.97), calls=%async_computation.4 | async-start | bytes 131072 | tf_op jit(solution)/shard_map/all_to_all | solution.py:121
  222.3 14.1 %collective-permute-start.28 = (f32[2,10,34,1]{3,2,1,0:T(8,128)}, f32[2,10,34,1]{3,2,1,0:T(8,128)S(1)}, u32[]{:S(2)}, u32[]{:S(2)}) collective-permute-start(f32[2,10,34,1]{3,2,1,0:T(8,128)} %get-tuple-element.38), channel_id=1, source_target_pairs={{1,0},{2,1},{3,2},{4,3},{5,4},{6,5},{7,6},{9,8},{10,9},{11,10},{12... | collective-permute-start | bytes 8168 | tf_op jit(solution)/shard_map/ppermute | solution.py:18
  223.6 12.8 %collective-permute-start.29 = (f32[2,10,34,1]{3,2,1,0:T(8,128)}, f32[2,10,34,1]{3,2,1,0:T(8,128)}, u32[]{:S(2)}, u32[]{:S(2)}) collective-permute-start(f32[2,10,34,1]{3,2,1,0:T(8,128)} %get-tuple-element.39), channel_id=1, source_target_pairs={{0,1},{1,2},{2,3},{3,4},{4,5},{5,6},{6,7},{8,9},{9,10},{10,11},{11... | collective-permute-start | bytes 8168 | tf_op jit(solution)/shard_map/ppermute | solution.py:15
  237.8 9.3 %collective-permute-start.30 = (f32[2,1,32,128]{3,2,1,0:T(8,128)S(1)}, f32[2,1,32,128]{3,2,1,0:T(8,128)S(1)}, u32[]{:S(2)}, u32[]{:S(2)}) collective-permute-start(f32[2,1,32,128]{3,2,1,0:T(8,128)S(1)} %get-tuple-element.69), channel_id=1, source_target_pairs={{64,0},{128,64},{192,128},{256,192},{320,256},{384,320},{448,384},... | collective-permute-start | bytes 98312 | tf_op jit(solution)/shard_map/ppermute | solution.py:18
  254.5 13.1 %collective-permute-start.34 = (f32[2,10,34,1]{3,2,1,0:T(8,128)S(1)}, f32[2,10,34,1]{3,2,1,0:T(8,128)S(1)}, u32[]{:S(2)}, u32[]{:S(2)}) collective-permute-start(f32[2,10,34,1]{3,2,1,0:T(8,128)S(1)} %get-tuple-element.36), channel_id=1, source_target_pairs={{1,0},{2,1},{3,2},{4,3},{5,4},{6,5},{7,6},{9,8},{10,9},{11,10},{12... | collective-permute-start | bytes 8168 | tf_op jit(solution)/shard_map/ppermute | solution.py:18
  255.8 13.1 %collective-permute-start.35 = (f32[2,10,34,1]{3,2,1,0:T(8,128)S(1)}, f32[2,10,34,1]{3,2,1,0:T(8,128)S(1)}, u32[]{:S(2)}, u32[]{:S(2)}) collective-permute-start(f32[2,10,34,1]{3,2,1,0:T(8,128)S(1)} %get-tuple-element.37), channel_id=1, source_target_pairs={{0,1},{1,2},{2,3},{3,4},{4,5},{5,6},{6,7},{8,9},{9,10},{10,11},{11... | collective-permute-start | bytes 8168 | tf_op jit(solution)/shard_map/ppermute | solution.py:15
  282.4 13.8 %collective-permute-start.40 = (f32[2,10,34,1]{3,2,1,0:T(8,128)S(1)}, f32[2,10,34,1]{3,2,1,0:T(8,128)S(1)}, u32[]{:S(2)}, u32[]{:S(2)}) collective-permute-start(f32[2,10,34,1]{3,2,1,0:T(8,128)S(1)} %get-tuple-element.34), channel_id=1, source_target_pairs={{1,0},{2,1},{3,2},{4,3},{5,4},{6,5},{7,6},{9,8},{10,9},{11,10},{12... | collective-permute-start | bytes 8168 | tf_op jit(solution)/shard_map/ppermute | solution.py:18
  283.7 13.4 %collective-permute-start.41 = (f32[2,10,34,1]{3,2,1,0:T(8,128)S(1)}, f32[2,10,34,1]{3,2,1,0:T(8,128)S(1)}, u32[]{:S(2)}, u32[]{:S(2)}) collective-permute-start(f32[2,10,34,1]{3,2,1,0:T(8,128)S(1)} %get-tuple-element.35), channel_id=1, source_target_pairs={{0,1},{1,2},{2,3},{3,4},{4,5},{5,6},{6,7},{8,9},{9,10},{10,11},{11... | collective-permute-start | bytes 8168 | tf_op jit(solution)/shard_map/ppermute | solution.py:15
  310.7 13.3 %collective-permute-start.46 = (f32[2,10,34,1]{3,2,1,0:T(8,128)S(1)}, f32[2,10,34,1]{3,2,1,0:T(8,128)S(1)}, u32[]{:S(2)}, u32[]{:S(2)}) collective-permute-start(f32[2,10,34,1]{3,2,1,0:T(8,128)S(1)} %get-tuple-element.32), channel_id=1, source_target_pairs={{1,0},{2,1},{3,2},{4,3},{5,4},{6,5},{7,6},{9,8},{10,9},{11,10},{12... | collective-permute-start | bytes 8168 | tf_op jit(solution)/shard_map/ppermute | solution.py:18
  312.0 12.8 %collective-permute-start.47 = (f32[2,10,34,1]{3,2,1,0:T(8,128)S(1)}, f32[2,10,34,1]{3,2,1,0:T(8,128)S(1)}, u32[]{:S(2)}, u32[]{:S(2)}) collective-permute-start(f32[2,10,34,1]{3,2,1,0:T(8,128)S(1)} %get-tuple-element.33), channel_id=1, source_target_pairs={{0,1},{1,2},{2,3},{3,4},{4,5},{5,6},{6,7},{8,9},{9,10},{10,11},{11... | collective-permute-start | bytes 8168 | tf_op jit(solution)/shard_map/ppermute | solution.py:15
  (44 other events, 410.9 us)
where the time goes:
time: 330 us; the launch traced here: 326 us
  starting transfers between devices  206 us (62%)
  waiting for transfers between devices  86.3 us (26%)
  local copies, waits for them, and re-layouts  22.5 us (7%)
  other arithmetic  8.72 us (3%)
    ppermute x24, starting transfers between devices, padded_2(): lax.ppermute(lax.slice_in_dim(block, block.shape[dim] - width, None, axis...  102 us
    ppermute x24, waiting for transfers between devices, padded_2(): lax.ppermute(lax.slice_in_dim(block, 0, width, axis=dim), axis, backward)  42.5 us
    ppermute x24, starting transfers between devices, padded_2(): lax.ppermute(lax.slice_in_dim(block, 0, width, axis=dim), axis, backward)  42.4 us
    all_to_all x2, starting transfers between devices, per_device(): lax.all_to_all(outgoing.reshape(owners, capacity, panel_width), ('gy', 'g...  30.2 us
    ppermute x24, waiting for transfers between devices, padded_2(): lax.ppermute(lax.slice_in_dim(block, block.shape[dim] - width, None, axis...  20.6 us
    all_to_all x1, starting transfers between devices, per_device(): lax.all_to_all(ids_sent.reshape(owners, capacity), ('gy', 'gx'), split_ax...  17.1 us
    all_to_all x2, waiting for transfers between devices, per_device(): lax.all_to_all(outgoing.reshape(owners, capacity, panel_width), ('gy', 'g...  14.9 us
    all_to_all x2, starting transfers between devices, per_device(): lax.all_to_all(mixed_out.reshape(owners, capacity, panel_width), ('gy', '...  14.5 us
  transfers between devices with their start and end apart: 53, of which 32 were waited for; matrix products, arithmetic and copies ran while one was open for 5% of the time, Pallas kernels for 0%

commit v1 on v0

v1 whole, which is shorter than its diff:
```python
import jax
import jax.numpy as jnp
from jax import lax
from jax.experimental import pallas as pl
from jax.experimental.pallas import tpu as pltpu
from jax.sharding import PartitionSpec as P

SWEEPS = 4
OUTER = 2
F32 = jnp.float32
BF16 = jnp.bfloat16
NZ, NY, NX = 8, 32, 128
EZ, EY, EX = 16, 40, 256
OWNERS = 64
SLOTS = 128
COEFS = 12
CZ = 14


def iota(shape, dim):
    return lax.broadcasted_iota(jnp.int32, shape, dim)


def call(body, out_shape, scratch=(), limit=32):
    return pl.pallas_call(
        body,
        out_shape=out_shape,
        scratch_shapes=list(scratch),
        compiler_params=pltpu.CompilerParams(vmem_limit_bytes=limit * 1024 * 1024),
    )


def dot(a, b):
    return jnp.dot(a.astype(BF16), b.astype(BF16), preferred_element_type=F32)


def panels_body(adj, perf, owner, slot, out, sc):
    own = owner[...].astype(F32)
    i0, i1 = iota((64, 64), 0), iota((64, 64), 1)
    wide = jnp.broadcast_to(own, (64, 64))
    tall = jnp.sum(jnp.where(i0 == i1, wide, 0.0), axis=1, keepdims=True)
    rank = jnp.sum(jnp.where((tall == wide) & (i0 < i1), 1.0, 0.0), axis=0, keepdims=True)
    dest = rank * float(OWNERS) + own
    hit = iota((SLOTS, 64), 0).astype(F32) == dest
    row_code = jnp.sum(jnp.where(hit, perf[...].astype(F32) + 1.0, 0.0), axis=1, keepdims=True)
    slot_code = jnp.sum(jnp.where(hit, slot[...].astype(F32) + 1.0, 0.0), axis=1, keepdims=True)
    pick = jnp.where(row_code == (iota((SLOTS, 256), 1) + 1).astype(F32), 1.0, 0.0)
    lane = iota((SLOTS, 128), 1)
    meta = jnp.where(lane == 0, slot_code, jnp.where(lane == 1, row_code, 0.0))
    for c in range(2):
        picked = dot(pick, adj[c].reshape(NZ * NY, NX))
        for k in range(2):
            sc[pl.ds(2 * c + k, 64, stride=8), :] = picked[k * 64 : (k + 1) * 64]
    zero = jnp.zeros((64, 128), F32)
    for k in range(2):
        sc[pl.ds(4 + k, 64, stride=8), :] = meta[k * 64 : (k + 1) * 64]
        sc[pl.ds(6 + k, 64, stride=8), :] = zero
    out[...] = sc[...].astype(BF16)


def panels(adj, perf, owner, slot):
    return call(
        panels_body,
        jax.ShapeDtypeStruct((512, 128), BF16),
        [pltpu.VMEM((512, 128), F32)],
    )(adj, perf, owner, slot)


def owner_body(arrived, well, cross, out, sx, rq):
    sx[...] = arrived[...].astype(F32)

    def rows(i):
        return jnp.concatenate(
            [sx[pl.ds(i, 64, stride=8), :], sx[pl.ds(i + 1, 64, stride=8), :]], axis=0
        )

    meta = rows(4)
    ident, row_code = meta[:, 0:1], meta[:, 1:2]
    panel = jnp.concatenate([rows(0), rows(2)], axis=1)
    i0, i1 = iota((SLOTS, SLOTS), 0), iota((SLOTS, SLOTS), 1)
    across = jnp.sum(jnp.where(i0 == i1, ident, 0.0), axis=0, keepdims=True)
    same = jnp.where(ident == across, 1.0, 0.0)
    totals = dot(same, panel).astype(BF16).astype(F32)
    mixed = jnp.zeros((SLOTS, 256), F32)
    for w in range(4):
        mine = ident == float(w + 1)
        mixed = mixed + dot(jnp.where(mine, panel, 0.0), well[w])
        mixed = mixed + dot(jnp.where(mine, totals, 0.0), cross[w])
    mixed = mixed.astype(BF16).astype(F32)
    tag = jnp.where(iota((SLOTS, 128), 1) == 96, row_code, 0.0)
    for k in range(2):
        part = slice(k * 64, (k + 1) * 64)
        for c in range(2):
            rq[pl.ds(2 * c + k, 64, stride=8), :] = mixed[part, c * 128 : (c + 1) * 128]
        rq[pl.ds(4 + k, 64, stride=8), :] = tag[part]
        rq[pl.ds(6 + k, 64, stride=8), :] = jnp.zeros((64, 128), F32)
    full = rq[...].reshape(64, 8, 128)
    sub, lane = iota((64, 8, 128), 1), iota((64, 8, 128), 2)

    def from_y(v, step):
        gap = jnp.zeros((8, 8, 128), F32)
        return jnp.concatenate([gap, v[:-8]] if step < 0 else [v[8:], gap], axis=0)

    def from_x(v, step):
        v = v.reshape(8, 8, 8, 128)
        gap = jnp.zeros((8, 1, 8, 128), F32)
        v = jnp.concatenate([gap, v[:, :-1]] if step < 0 else [v[:, 1:], gap], axis=1)
        return v.reshape(64, 8, 128)

    def turn(v, by):
        return pltpu.roll(v, by, 2)

    def half(v):
        return pltpu.roll(v, 4, 1)

    below, above = from_y(full, -1), from_y(full, 1)
    edge = jnp.where(lane >= 125, from_x(full, -1), jnp.where(lane < 3, from_x(full, 1), 0.0))
    edges = edge + turn(from_y(edge, -1), 32) + turn(from_y(edge, 1), 64)
    tags = jnp.where((sub >= 4) & (lane == 96), full, 0.0)
    tags = tags + turn(from_y(tags, -1), 1) + turn(from_y(tags, 1), 2)
    tags = tags + turn(from_x(tags, -1), 3) + turn(from_x(tags, 1), 6)
    first = jnp.where(sub < 4, full, half(below))
    second = jnp.where(sub < 4, above, half(jnp.where(sub < 4, edges, 0.0)) + tags)
    out[...] = jnp.concatenate([first, second], axis=1).astype(BF16)


def owner_work(arrived, well, cross):
    return call(
        owner_body,
        jax.ShapeDtypeStruct((64, 16, 128), BF16),
        [pltpu.VMEM((512, 128), F32), pltpu.VMEM((512, 128), F32)],
    )(arrived, well, cross)


def place_body(arrived, ws, up, down, sx):
    sx[...] = arrived[...].reshape(1024, 128).astype(F32)

    def rows(i):
        return jnp.concatenate(
            [sx[pl.ds(i, 64, stride=16), :], sx[pl.ds(i + 1, 64, stride=16), :]], axis=0
        )

    def both(i):
        return jnp.concatenate([rows(i), rows(i + 2)], axis=1)

    codes = rows(12).T

    def code(n):
        return codes[96 + n : 97 + n, :]

    def place(want, n, values):
        return dot(jnp.where(want == code(n), 1.0, 0.0), values)

    lane = jnp.bitwise_and(iota((SLOTS, 256), 1), 127)

    def sides(by):
        v = jnp.concatenate(
            [pltpu.roll(rows(12), by, 1) if by else rows(12), pltpu.roll(rows(14), by, 1) if by else rows(14)],
            axis=1,
        )
        return jnp.where(lane >= 125, v, 0.0), jnp.where(lane < 3, v, 0.0)

    own = (iota((256, SLOTS), 0) + 1).astype(F32)
    g = iota((64, SLOTS), 0)
    j = jnp.bitwise_and(g, 7)
    base = (g - j) * 4 + j + 1
    high = jnp.where(j < 3, base, -1).astype(F32)
    low = jnp.where(j >= 5, base + 24, -1).astype(F32)
    main = place(own, 0, both(0))
    halo = place(low, 1, both(4)) + place(high, 2, both(8))
    minus, plus = sides(0)
    side = place(own, 3, minus) + place(own, 6, plus)
    minus, plus = sides(96)
    corner = place(low, 4, minus) + place(low, 7, plus)
    minus, plus = sides(64)
    corner = corner + place(high, 5, minus) + place(high, 8, plus)
    for c in range(2):
        part = slice(c * 128, (c + 1) * 128)
        ws[c, :, 0:32, 0:128] = main[:, part].reshape(8, 32, 128)
        ws[c, :, 32:40, 0:128] = halo[:, part].reshape(8, 8, 128)
        ws[c, :, 0:32, 128:256] = side[:, part].reshape(8, 32, 128)
        ws[c, :, 32:40, 128:256] = corner[:, part].reshape(8, 8, 128)
        up[c] = ws[c, 5:8].astype(BF16)
        down[c] = ws[c, 0:3].astype(BF16)


def place(arrived):
    return call(
        place_body,
        (
            jax.ShapeDtypeStruct((2, NZ, EY, EX), F32),
            jax.ShapeDtypeStruct((2, 3, EY, EX), BF16),
            jax.ShapeDtypeStruct((2, 3, EY, EX), BF16),
        ),
        [pltpu.VMEM((1024, 128), F32)],
    )(arrived)


def fields_of(refs):
    couple, diag, cross, source = refs
    return [(couple, i) for i in range(6)] + [(r, i) for r in (diag, cross, source) for i in range(2)]


def zsend_body(*refs):
    ins, (up, down) = refs[:-2], refs[-2:]
    adj = ins[0]
    for c in range(2):
        up[4 * c : 4 * c + 4] = adj[c, 4:8].astype(BF16)
        down[4 * c : 4 * c + 4] = adj[c, 0:4].astype(BF16)
    if len(ins) > 1:
        for n, (ref, i) in enumerate(fields_of(ins[1:])):
            up[8 + 3 * n : 11 + 3 * n] = ref[i, 5:8].astype(BF16)
            down[8 + 3 * n : 11 + 3 * n] = ref[i, 0:3].astype(BF16)


def zsend(*ins):
    planes = 44 if len(ins) > 1 else 8
    shape = jax.ShapeDtypeStruct((planes, NY, NX), BF16)
    return call(zsend_body, (shape, shape))(*ins)


def adj_plane(adj, zlo, zhi, c, z):
    if z < 4:
        return zlo[4 * c + z].astype(F32)
    if z >= 12:
        return zhi[4 * c + z - 12].astype(F32)
    return adj[c, z - 4]


def coef_plane(ref, i, n, zlo, zhi, e):
    if e < 3:
        return zlo[8 + 3 * n + e].astype(F32)
    if e >= 11:
        return zhi[8 + 3 * n + e - 11].astype(F32)
    return ref[i, e - 3]


def ysend_body(*refs):
    ins, (zlo, zhi, up, down) = refs[:-4], refs[-4:]
    low = iota((8, 128), 0) < 4

    def pack(index, even, odd):
        up[index] = jnp.where(low, pltpu.roll(even[24:32], 4, 0), odd[24:32]).astype(BF16)
        down[index] = jnp.where(low, even[0:8], pltpu.roll(odd[0:8], 4, 0)).astype(BF16)

    for c in range(2):
        for h in range(8):
            pack(8 * c + h, *[adj_plane(ins[0], zlo, zhi, c, 2 * h + o) for o in range(2)])
    if len(ins) > 1:
        for n, (ref, i) in enumerate(fields_of(ins[1:])):
            for h in range(7):
                pack(16 + 7 * n + h, *[coef_plane(ref, i, n, zlo, zhi, 2 * h + o) for o in range(2)])


def ysend(*ins):
    tiles = 100 if len(ins) > 3 else 16
    shape = jax.ShapeDtypeStruct((tiles, 8, 128), BF16)
    return call(ysend_body, (shape, shape))(*ins)


def y_tiles(ylo, yhi, index):
    low = iota((8, 128), 0) < 4
    a, b = ylo[index].astype(F32), yhi[index].astype(F32)
    even = jnp.where(low, b, pltpu.roll(a, 4, 0))
    odd = jnp.where(low, pltpu.roll(b, 4, 0), a)
    return even, odd


def xsend_body(*refs):
    ins, (zlo, zhi, ylo, yhi, out) = refs[:-5], refs[-5:]
    group = lax.shift_right_logical(iota((8, 128), 1), 3)
    group4 = lax.shift_right_logical(iota((32, 128), 1), 3)

    def pack(index, count, plane, tile_at):
        acc = jnp.zeros((32, 128), F32)
        edge = jnp.zeros((8, 128), F32)
        for h in range(count // 2):
            tiles = y_tiles(ylo, yhi, tile_at + h)
            for o in range(2):
                z = 2 * h + o
                acc = jnp.where(group4 == z, pltpu.roll(plane(z), 8 * z + 4 if z < 15 else 124, 1), acc)
                edge = jnp.where(group == z, pltpu.roll(tiles[o], 8 * z + 4, 1), edge)
        out[index, 0:32] = acc.astype(BF16)
        out[index, 32:40] = edge.astype(BF16)

    for c in range(2):
        pack(c, EZ, lambda z, c=c: adj_plane(ins[0], zlo, zhi, c, z), 8 * c)
    if len(ins) > 1:
        for n, (ref, i) in enumerate(fields_of(ins[1:])):
            pack(
                2 + n,
                CZ,
                lambda e, n=n, ref=ref, i=i: coef_plane(ref, i, n, zlo, zhi, e),
                16 + 7 * n,
            )


def xsend(*ins):
    fields = 14 if len(ins) > 5 else 2
    return call(xsend_body, jax.ShapeDtypeStruct((fields, EY, 128), BF16))(*ins)


def sweeps_body(
    adj, couple, diag, cross, source,
    azlo, azhi, aylo, ayhi, axlo, axhi,
    czlo, czhi, cylo, cyhi, cxlo, cxhi,
    ws, wlo, whi,
    out, field, bufs, rhs,
):
    lane = iota((EY, 128), 1)
    from_low = jnp.bitwise_and(lane, 7) < 4
    keep = (lane < 4) | (lane >= 124)

    def columns(xlo, xhi, index):
        return jnp.where(from_low, xlo[index].astype(F32), xhi[index].astype(F32))

    def spread(packed, z):
        return jnp.where(keep, pltpu.roll(packed, (124 - 8 * z) % 128, 1), 0.0)

    for c in range(2):
        packed = columns(axlo, axhi, c)
        for h in range(8):
            tiles = y_tiles(aylo, ayhi, 8 * c + h)
            for o in range(2):
                z = 2 * h + o
                bufs[0, c, z, 0:32, 0:128] = adj_plane(adj, azlo, azhi, c, z)
                bufs[0, c, z, 32:40, 0:128] = tiles[o]
                bufs[0, c, z, :, 128:256] = spread(packed, z)
    for n, (ref, i) in enumerate(fields_of((couple, diag, cross, source))):
        packed = columns(cxlo, cxhi, 2 + n)
        for h in range(7):
            tiles = y_tiles(cylo, cyhi, 16 + 7 * n + h)
            for o in range(2):
                e = 2 * h + o
                field[n, e, 0:32, 0:128] = coef_plane(ref, i, n, czlo, czhi, e)
                field[n, e, 32:40, 0:128] = tiles[o]
                field[n, e, :, 128:256] = spread(packed, e)
    for c in range(2):
        for e in range(CZ):
            if e < 3:
                extra = wlo[c, e].astype(F32)
            elif e >= 11:
                extra = whi[c, e - 11].astype(F32)
            else:
                extra = ws[c, e - 3]
            rhs[c, e] = field[10 + c, e] + extra

    for s in range(SWEEPS):
        last = s == SWEEPS - 1
        rows, lanes = (NY, NX) if last else (EY, EX)

        def layer(z, carry, s=s, last=last, rows=rows, lanes=lanes):
            e = z - 1
            src = s % 2

            def co(n):
                return field[n, e, 0:rows, 0:lanes]

            inflow = []
            for c in range(2):
                here = bufs[src, c, z]
                total = rhs[c, e, 0:rows, 0:lanes]
                total = total + co(0) * bufs[src, c, z + 1, 0:rows, 0:lanes]
                total = total + co(1) * bufs[src, c, z - 1, 0:rows, 0:lanes]
                total = total + co(2) * pltpu.roll(here, EY - 1, 0)[0:rows, 0:lanes]
                total = total + co(3) * pltpu.roll(here, 1, 0)[0:rows, 0:lanes]
                total = total + co(4) * pltpu.roll(here, EX - 1, 1)[0:rows, 0:lanes]
                total = total + co(5) * pltpu.roll(here, 1, 1)[0:rows, 0:lanes]
                inflow.append(total)
            new0 = co(6) * inflow[0] + co(8) * inflow[1]
            new1 = co(9) * inflow[0] + co(7) * inflow[1]
            if last:
                out[0, z - 4] = new0
                out[1, z - 4] = new1
            else:
                bufs[1 - src, 0, z] = new0
                bufs[1 - src, 1, z] = new1
            return carry

        lax.fori_loop(1 + s, EZ - 1 - s, layer, 0)


def sweeps(*ins):
    return call(
        sweeps_body,
        jax.ShapeDtypeStruct((2, NZ, NY, NX), F32),
        [
            pltpu.VMEM((COEFS, CZ, EY, EX), F32),
            pltpu.VMEM((2, 2, EZ, EY, EX), F32),
            pltpu.VMEM((2, CZ, EY, EX), F32),
        ],
    )(*ins)


def exchange(up, down, axis):
    count = lax.axis_size(axis)
    forward = [(i, i + 1) for i in range(count - 1)]
    backward = [(i + 1, i) for i in range(count - 1)]
    return lax.ppermute(up, axis, forward), lax.ppermute(down, axis, backward)


def per_device(
    source,
    adjoint_start,
    couple,
    diag_inverse,
    cross_inverse,
    perf_row,
    well_owner,
    well_slot,
    well_block,
    cross_block,
):
    perf = perf_row.reshape(1, -1)
    owner = well_owner.reshape(1, -1)
    slot = well_slot.reshape(1, -1)
    well = well_block.reshape(well_block.shape[3:])
    cross_mats = cross_block.reshape(cross_block.shape[3:])
    fields = (couple, diag_inverse, cross_inverse, source)
    adjoint = adjoint_start
    kept = None
    for outer_step in range(OUTER):
        more = fields if outer_step == 0 else ()
        sent = panels(adjoint, perf, owner, slot)
        arrived = lax.all_to_all(sent, ("gy", "gx"), split_axis=0, concat_axis=0, tiled=True)
        zlo, zhi = exchange(*zsend(adjoint, *more), "gz")
        ylo, yhi = exchange(*ysend(adjoint, *more, zlo, zhi), "gy")
        packed = xsend(adjoint, *more, zlo, zhi, ylo, yhi)
        xlo, xhi = exchange(packed, packed, "gx")
        halo = (zlo, zhi, ylo, yhi, xlo, xhi)
        kept = halo if kept is None else kept
        answers = owner_work(arrived, well, cross_mats)
        returned = lax.all_to_all(answers, ("gy", "gx"), split_axis=0, concat_axis=0, tiled=True)
        ws, up, down = place(returned)
        wlo, whi = exchange(up, down, "gz")
        adjoint = sweeps(adjoint, *fields, *halo, *kept, ws, wlo, whi)
    return adjoint


def solution(mesh):
    placed = (
        P(None, "gz", "gy", "gx"),
        P(None, "gz", "gy", "gx"),
        P(None, "gz", "gy", "gx"),
        P(None, "gz", "gy", "gx"),
        P(None, "gz", "gy", "gx"),
        P("gz", "gy", "gx", None),
        P("gz", "gy", "gx", None, None),
        P("gz", "gy", "gx", None),
        P("gz", "gy", "gx", None, None, None),
        P("gz", "gy", "gx", None, None, None),
    )
    return jax.shard_map(
        per_device, mesh=mesh, in_specs=placed, out_specs=P(None, "gz", "gy", "gx"), check_vma=False
    )
```

time: 330 us -> 167 us (0.51)
  starting transfers between devices: 206 us -> 70.7 us
  waiting for transfers between devices: 86.3 us -> 24.2 us
  blocking collectives: 0 us -> 41.8 us
  Pallas kernels: 0 us -> 24 us
  local copies, waits for them, and re-layouts: 22.5 us -> 4.69 us
  other arithmetic: 8.72 us -> 0 us
    ppermute x48 -> x16, starting transfers between devices: 144 us -> 42.4 us  [exchange(): return (lax.ppermute(up, axis, forward), lax.ppermute(down, axis, backward))]
    all_to_all x0 -> x2, blocking collectives: none -> 41.8 us  [the longest x1 23.9 us: per_device(): lax.all_to_all(sent, ('gy', 'gx'), split_axis=0, concat_axis=0, tiled=True)]
    ppermute x48 -> x16, waiting for transfers between devices: 63.1 us -> 22.5 us  [exchange(): return (lax.ppermute(up, axis, forward), lax.ppermute(down, axis, backward))]
    all_to_all x5 -> x2, starting transfers between devices: 61.8 us -> 28.3 us  [the longest x1 17.1 us: per_device(): lax.all_to_all(sent, ('gy', 'gx'), split_axis=0, concat_axis=0, tiled=True)]
    pallas_call x0 -> x14, Pallas kernels: none -> 24 us  [the longest x2 15.7 us: sweeps(): call(sweeps_body, jax.ShapeDtypeStruct((2, NZ, NY, NX), F32), [pltpu.VMEM...]
    all_to_all x5 -> x2, waiting for transfers between devices: 23.2 us -> 1.65 us  [the longest x1 1.65 us: per_device(): lax.all_to_all(sent, ('gy', 'gx'), split_axis=0, concat_axis=0, tiled=True)]
    scatter x5 -> x0, local copies, waits for them, and re-layouts: 7.61 us -> none  [the longest x2 4.86 us: per_device(): placed = jnp.zeros((layers_dev * rows_dev, 2, cols_dev), jnp.float32).at[...]
    add x16 -> x0, other arithmetic: 5.68 us -> none  [the longest x8 5.14 us: jacobi_sweep(): inflow = right_side + neighbours(padded, couple)]
  transfers between devices with their start and end apart: 53 -> 18, of which waited for: 32 -> 7; matrix products, arithmetic and copies ran while one was open for 5% -> 0% of each run, Pallas kernels for 0% -> 3%
where the time goes in v1:
time: 167 us; the launch traced here: 166 us
  starting transfers between devices  70.7 us (42%)
  blocking collectives  41.8 us (25%)
  waiting for transfers between devices  24.2 us (14%)
  Pallas kernels  24 us (14%)
  local copies, waits for them, and re-layouts  4.69 us (3%)
    ppermute x16, starting transfers between devices, exchange(): return (lax.ppermute(up, axis, forward), lax.ppermute(down, axis, backward))  42.4 us
    all_to_all x1, blocking collectives, per_device(): lax.all_to_all(sent, ('gy', 'gx'), split_axis=0, concat_axis=0, tiled=True)  23.9 us
    ppermute x16, waiting for transfers between devices, exchange(): return (lax.ppermute(up, axis, forward), lax.ppermute(down, axis, backward))  22.5 us
    all_to_all x1, blocking collectives, per_device(): lax.all_to_all(answers, ('gy', 'gx'), split_axis=0, concat_axis=0, tiled=...  17.9 us
    all_to_all x1, starting transfers between devices, per_device(): lax.all_to_all(sent, ('gy', 'gx'), split_axis=0, concat_axis=0, tiled=True)  17.1 us
    pallas_call x2, Pallas kernels, sweeps(): call(sweeps_body, jax.ShapeDtypeStruct((2, NZ, NY, NX), F32), [pltpu.VMEM...  15.7 us
    all_to_all x1, starting transfers between devices, per_device(): lax.all_to_all(answers, ('gy', 'gx'), split_axis=0, concat_axis=0, tiled=...  11.2 us
    unnamed x30, local copies, waits for them, and re-layouts  4.69 us
  transfers between devices with their start and end apart: 18, of which 7 were waited for; matrix products, arithmetic and copies ran while one was open for 0% of the time, Pallas kernels for 3%

profile of v1, /device:TPU:1, one launch (start us, length us, event | category | flops | bytes accessed | tf_op | source)
XLA Modules:
  0.0 165.8 jit_solution(2448013644926736823)
XLA Ops:
  2.7 17.1 %all-to-all-start = ((bf16[64,8,128]{2,1,0:T(8,128)(2,1)}), bf16[64,8,128]{2,1,0:T(8,128)(2,1)S(1)}, u32[]{:S(2)}, u32[]{:S(2)}) async-start(bf16[64,8,128]{2,1,0:T(8,128)(2,1)} %bitcast.3), calls=%async_computation | async-start | bytes 262144 | tf_op jit(solution)/shard_map/all_to_all | solution.py:425
  23.8 3.9 %collective-permute-start = (bf16[44,32,128]{2,1,0:T(8,128)(2,1)}, bf16[44,32,128]{2,1,0:T(8,128)(2,1)S(1)}, u32[]{:S(2)}, u32[]{:S(2)}) collective-permute-start(bf16[44,32,128]{2,1,0:T(8,128)(2,1)} %get-tuple-element.19), channel_id=1, source_target_pairs={{0,64},{64,128},{128,192},{192,256},{256,320},{320,384},{384,448},... | collective-permute-start | bytes 1081352 | tf_op jit(solution)/shard_map/ppermute | solution.py:399
  27.8 1.9 %collective-permute-start.1 = (bf16[44,32,128]{2,1,0:T(8,128)(2,1)}, bf16[44,32,128]{2,1,0:T(8,128)(2,1)S(1)}, u32[]{:S(2)}, u32[]{:S(2)}) collective-permute-start(bf16[44,32,128]{2,1,0:T(8,128)(2,1)} %get-tuple-element.20), channel_id=1, source_target_pairs={{64,0},{128,64},{192,128},{256,192},{320,256},{384,320},{448,384},... | collective-permute-start | bytes 1081352 | tf_op jit(solution)/shard_map/ppermute | solution.py:399
  29.7 1.7 all-to-all-done
  31.4 1.7 %shard_map.104 = bf16[64,16,128]{2,1,0:T(8,128)(2,1)} custom-call(bf16[512,128]{1,0:T(8,128)(2,1)S(1)} %bitcast.14, bf16[4,256,256]{2,1,0:T(8,128)(2,1)S(1)} %bitcast.9, bf16[4,256,256]{2,1,0:T(8,128)(2,1)S(1)} %bitcast.11), custom_call_target="tpu_custom_call" | custom-call | tf_op jit(solution)/shard_map/pallas_call | solution.py:128
  33.0 11.2 %all-to-all-start.1 = ((bf16[64,16,128]{2,1,0:T(8,128)(2,1)}), bf16[64,16,128]{2,1,0:T(8,128)(2,1)}, u32[]{:S(2)}, u32[]{:S(2)}) async-start(bf16[64,16,128]{2,1,0:T(8,128)(2,1)} %shard_map.104), calls=%async_computation.1 | async-start | bytes 524288 | tf_op jit(solution)/shard_map/all_to_all | solution.py:433
  44.4 2.9 %collective-permute-start.2 = (bf16[100,8,128]{2,1,0:T(8,128)(2,1)S(1)}, bf16[100,8,128]{2,1,0:T(8,128)(2,1)S(1)}, u32[]{:S(2)}, u32[]{:S(2)}) collective-permute-start(bf16[100,8,128]{2,1,0:T(8,128)(2,1)S(1)} %get-tuple-element.21), channel_id=1, source_target_pairs={{0,8},{8,16},{16,24},{24,32},{32,40},{40,48},{48,56},{1,9},{9,17},... | collective-permute-start | bytes 614408 | tf_op jit(solution)/shard_map/ppermute | solution.py:399
  47.3 1.3 collective-permute-start.3
  48.6 6.5 %collective-permute-done.2.refs_7_.aylo.cylo = bf16[100,8,128]{2,1,0:T(8,128)(2,1)S(1)} collective-permute-done((bf16[100,8,128]{2,1,0:T(8,128)(2,1)S(1)}, bf16[100,8,128]{2,1,0:T(8,128)(2,1)S(1)}, u32[]{:S(2)}, u32[]{:S(2)}) %collective-permute-start.2) | collective-permute-done | bytes 204832 | tf_op jit(solution)/shard_map/ppermute | solution.py:399
  55.0 1.5 collective-permute-done.3.refs_8_.ayhi.cyhi
  56.6 1.3 shard_map.102
  57.8 3.6 %collective-permute-start.4 = (bf16[14,40,128]{2,1,0:T(8,128)(2,1)}, bf16[14,40,128]{2,1,0:T(8,128)(2,1)}, u32[]{:S(2)}, u32[]{:S(2)}) collective-permute-start(bf16[14,40,128]{2,1,0:T(8,128)(2,1)} %shard_map.102), channel_id=1, source_target_pairs={{0,1},{1,2},{2,3},{3,4},{4,5},{5,6},{6,7},{8,9},{9,10},{10,11},{11... | collective-permute-start | bytes 430088 | tf_op jit(solution)/shard_map/ppermute | solution.py:399
  61.4 1.3 collective-permute-start.5
  62.7 1.4 shard_map.105
  64.1 5.4 %collective-permute-start.6 = (bf16[2,3,40,256]{3,2,1,0:T(8,128)(2,1)S(1)}, bf16[2,3,40,256]{3,2,1,0:T(8,128)(2,1)S(1)}, u32[]{:S(2)}, u32[]{:S(2)}) collective-permute-start(bf16[2,3,40,256]{3,2,1,0:T(8,128)(2,1)S(1)} %get-tuple-element.24), channel_id=1, source_target_pairs={{0,64},{64,128},{128,192},{192,256},{256,320},{320,384},{384,448},... | collective-permute-start | bytes 368648 | tf_op jit(solution)/shard_map/ppermute | solution.py:399
  69.4 1.9 %collective-permute-start.7 = (bf16[2,3,40,256]{3,2,1,0:T(8,128)(2,1)S(1)}, bf16[2,3,40,256]{3,2,1,0:T(8,128)(2,1)S(1)}, u32[]{:S(2)}, u32[]{:S(2)}) collective-permute-start(bf16[2,3,40,256]{3,2,1,0:T(8,128)(2,1)S(1)} %get-tuple-element.25), channel_id=1, source_target_pairs={{64,0},{128,64},{192,128},{256,192},{320,256},{384,320},{448,384},... | collective-permute-start | bytes 368648 | tf_op jit(solution)/shard_map/ppermute | solution.py:399
  71.4 4.2 %collective-permute-done.7.whi = bf16[2,3,40,256]{3,2,1,0:T(8,128)(2,1)S(1)} collective-permute-done((bf16[2,3,40,256]{3,2,1,0:T(8,128)(2,1)S(1)}, bf16[2,3,40,256]{3,2,1,0:T(8,128)(2,1)S(1)}, u32[]{:S(2)}, u32[]{:S(2)}) %collective-permute-start.7) | collective-permute-done | bytes 122912 | tf_op jit(solution)/shard_map/ppermute | solution.py:399
  75.6 7.6 %shard_map.106.refs_0_.adj = f32[2,8,32,128]{3,2,1,0:T(8,128)S(1)} custom-call(f32[2,8,32,128]{3,2,1,0:T(8,128)S(1)} %copy-done.3, f32[6,8,32,128]{3,2,1,0:T(8,128)S(1)} %copy-done.1, f32[2,8,32,128]{3,2,1,0:T(8,128)S(1)} %copy-done.4, f32[2,8,32,128]{3,2,1,0:T(8,128)S(1)} %copy-done.6, f32[2,8,32,128]{3,2,1,0:T(8,128)S(1)} %copy-done.8, ...), custom_call_target="tpu_custom_call" | custom-call | tf_op jit(solution)/shard_map/pallas_call | solution.py:384
  83.6 23.9 %all_to_all.32 = bf16[64,8,128]{2,1,0:T(8,128)(2,1)S(1)} all-to-all(bf16[64,8,128]{2,1,0:T(8,128)(2,1)S(1)} %bitcast.13), channel_id=1, replica_groups=mesh['gz'=8,'gy'=8,'gx'=8] {'gy','gx'}, dimensions={0} | all-to-all | bytes 262144 | tf_op jit(solution)/shard_map/all_to_all | solution.py:425
  108.5 17.9 %all_to_all.33.arrived = bf16[64,16,128]{2,1,0:T(8,128)(2,1)S(1)} all-to-all(bf16[64,16,128]{2,1,0:T(8,128)(2,1)S(1)} %shard_map.111), channel_id=1, replica_groups=mesh['gz'=8,'gy'=8,'gx'=8] {'gy','gx'}, dimensions={0} | all-to-all | bytes 524288 | tf_op jit(solution)/shard_map/all_to_all | solution.py:433
  126.8 5.3 %collective-permute-start.14 = (bf16[2,3,40,256]{3,2,1,0:T(8,128)(2,1)S(1)}, bf16[2,3,40,256]{3,2,1,0:T(8,128)(2,1)S(1)}, u32[]{:S(2)}, u32[]{:S(2)}) collective-permute-start(bf16[2,3,40,256]{3,2,1,0:T(8,128)(2,1)S(1)} %get-tuple-element.31), channel_id=1, source_target_pairs={{0,64},{64,128},{128,192},{192,256},{256,320},{320,384},{384,448},... | collective-permute-start | bytes 368648 | tf_op jit(solution)/shard_map/ppermute | solution.py:399
  132.1 1.9 %collective-permute-start.15 = (bf16[2,3,40,256]{3,2,1,0:T(8,128)(2,1)S(1)}, bf16[2,3,40,256]{3,2,1,0:T(8,128)(2,1)S(1)}, u32[]{:S(2)}, u32[]{:S(2)}) collective-permute-start(bf16[2,3,40,256]{3,2,1,0:T(8,128)(2,1)S(1)} %get-tuple-element.32), channel_id=1, source_target_pairs={{64,0},{128,64},{192,128},{256,192},{320,256},{384,320},{448,384},... | collective-permute-start | bytes 368648 | tf_op jit(solution)/shard_map/ppermute | solution.py:399
  134.0 3.6 %collective-permute-start.8 = (bf16[8,32,128]{2,1,0:T(8,128)(2,1)S(1)}, bf16[8,32,128]{2,1,0:T(8,128)(2,1)S(1)}, u32[]{:S(2)}, u32[]{:S(2)}) collective-permute-start(bf16[8,32,128]{2,1,0:T(8,128)(2,1)S(1)} %get-tuple-element.26), channel_id=1, source_target_pairs={{0,64},{64,128},{128,192},{192,256},{256,320},{320,384},{384,448},... | collective-permute-start | bytes 196616 | tf_op jit(solution)/shard_map/ppermute | solution.py:399
  137.7 1.9 %collective-permute-start.9 = (bf16[8,32,128]{2,1,0:T(8,128)(2,1)S(1)}, bf16[8,32,128]{2,1,0:T(8,128)(2,1)S(1)}, u32[]{:S(2)}, u32[]{:S(2)}) collective-permute-start(bf16[8,32,128]{2,1,0:T(8,128)(2,1)S(1)} %get-tuple-element.27), channel_id=1, source_target_pairs={{64,0},{128,64},{192,128},{256,192},{320,256},{384,320},{448,384},... | collective-permute-start | bytes 196616 | tf_op jit(solution)/shard_map/ppermute | solution.py:399
  139.6 3.6 %collective-permute-done.9.refs_2_.azhi = bf16[8,32,128]{2,1,0:T(8,128)(2,1)S(1)} collective-permute-done((bf16[8,32,128]{2,1,0:T(8,128)(2,1)S(1)}, bf16[8,32,128]{2,1,0:T(8,128)(2,1)S(1)}, u32[]{:S(2)}, u32[]{:S(2)}) %collective-permute-start.9) | collective-permute-done | bytes 65568 | tf_op jit(solution)/shard_map/ppermute | solution.py:399
  143.3 2.3 %collective-permute-start.10 = (bf16[16,8,128]{2,1,0:T(8,128)(2,1)S(1)}, bf16[16,8,128]{2,1,0:T(8,128)(2,1)S(1)}, u32[]{:S(2)}, u32[]{:S(2)}) collective-permute-start(bf16[16,8,128]{2,1,0:T(8,128)(2,1)S(1)} %get-tuple-element.28), channel_id=1, source_target_pairs={{0,8},{8,16},{16,24},{24,32},{32,40},{40,48},{48,56},{1,9},{9,17},... | collective-permute-start | bytes 98312 | tf_op jit(solution)/shard_map/ppermute | solution.py:399
  145.6 1.3 collective-permute-start.11
  146.9 3.3 %collective-permute-done.11.refs_4_.ayhi = bf16[16,8,128]{2,1,0:T(8,128)(2,1)S(1)} collective-permute-done((bf16[16,8,128]{2,1,0:T(8,128)(2,1)S(1)}, bf16[16,8,128]{2,1,0:T(8,128)(2,1)S(1)}, u32[]{:S(2)}, u32[]{:S(2)}) %collective-permute-start.11) | collective-permute-done | bytes 32800 | tf_op jit(solution)/shard_map/ppermute | solution.py:399
  150.4 2.7 %collective-permute-start.12 = (bf16[2,40,128]{2,1,0:T(8,128)(2,1)S(1)}, bf16[2,40,128]{2,1,0:T(8,128)(2,1)S(1)}, u32[]{:S(2)}, u32[]{:S(2)}) collective-permute-start(bf16[2,40,128]{2,1,0:T(8,128)(2,1)S(1)} %shard_map.109), channel_id=1, source_target_pairs={{0,1},{1,2},{2,3},{3,4},{4,5},{5,6},{6,7},{8,9},{9,10},{10,11},{11... | collective-permute-start | bytes 61448 | tf_op jit(solution)/shard_map/ppermute | solution.py:399
  153.1 1.3 collective-permute-start.13
  154.4 3.3 %collective-permute-done.13.axhi = bf16[2,40,128]{2,1,0:T(8,128)(2,1)S(1)} collective-permute-done((bf16[2,40,128]{2,1,0:T(8,128)(2,1)S(1)}, bf16[2,40,128]{2,1,0:T(8,128)(2,1)S(1)}, u32[]{:S(2)}, u32[]{:S(2)}) %collective-permute-start.13) | collective-permute-done | bytes 20512 | tf_op jit(solution)/shard_map/ppermute | solution.py:399
  157.6 8.1 %shard_map.113 = f32[2,8,32,128]{3,2,1,0:T(8,128)} custom-call(f32[2,8,32,128]{3,2,1,0:T(8,128)S(1)} %shard_map.106.refs_0_.adj, f32[6,8,32,128]{3,2,1,0:T(8,128)S(1)} %copy-done.1, f32[2,8,32,128]{3,2,1,0:T(8,128)S(1)} %copy-done.4, f32[2,8,32,128]{3,2,1,0:T(8,128)S(1)} %copy-done.6, f32[2,8,32,128]{3,2,1,0:T(8,128)S(1)} %copy-done.8, ...), custom_call_target="tpu_custom_call" | custom-call | tf_op jit(solution)/shard_map/pallas_call | solution.py:384
  (50 shorter events, 8.7 us)
Async XLA Ops:
  0.0 0.7 copy-start.13
  0.0 0.7 copy-start.14
  0.7 0.9 copy-start.2
  1.6 18.2 %copy-start.3 = (f32[2,8,32,128]{3,2,1,0:T(8,128)S(1)}, f32[2,8,32,128]{3,2,1,0:T(8,128)}, u32[]{:S(2)}) copy-start(f32[2,8,32,128]{3,2,1,0:T(8,128)} %adj.3) | copy-start | bytes 786436
  1.6 18.2 %copy-start.4 = (f32[2,8,32,128]{3,2,1,0:T(8,128)S(1)}, f32[2,8,32,128]{3,2,1,0:T(8,128)}, u32[]{:S(2)}) copy-start(f32[2,8,32,128]{3,2,1,0:T(8,128)} %diag.3) | copy-start | bytes 786436
  2.7 28.7 %all-to-all-start = ((bf16[64,8,128]{2,1,0:T(8,128)(2,1)}), bf16[64,8,128]{2,1,0:T(8,128)(2,1)S(1)}, u32[]{:S(2)}, u32[]{:S(2)}) async-start(bf16[64,8,128]{2,1,0:T(8,128)(2,1)} %bitcast.3), calls=%async_computation | async-start | bytes 262144 | tf_op jit(solution)/shard_map/all_to_all | solution.py:425
  19.8 1.1 copy-start
  21.0 0.9 copy-start.5
  21.9 0.9 copy-start.7
  22.9 8.5 %copy-start.9 = (bf16[1,1,1,4,256,256]{5,4,3,2,1,0:T(8,128)(2,1)S(1)}, bf16[1,1,1,4,256,256]{5,4,3,2,1,0:T(8,128)(2,1)}, u32[]{:S(2)}) copy-start(bf16[1,1,1,4,256,256]{5,4,3,2,1,0:T(8,128)(2,1)} %param.18) | copy-start | bytes 1572868
  22.9 8.5 %copy-start.10 = (bf16[1,1,1,4,256,256]{5,4,3,2,1,0:T(8,128)(2,1)S(1)}, bf16[1,1,1,4,256,256]{5,4,3,2,1,0:T(8,128)(2,1)}, u32[]{:S(2)}) copy-start(bf16[1,1,1,4,256,256]{5,4,3,2,1,0:T(8,128)(2,1)} %param.19) | copy-start | bytes 1572868
  23.8 20.4 %collective-permute-start = (bf16[44,32,128]{2,1,0:T(8,128)(2,1)}, bf16[44,32,128]{2,1,0:T(8,128)(2,1)S(1)}, u32[]{:S(2)}, u32[]{:S(2)}) collective-permute-start(bf16[44,32,128]{2,1,0:T(8,128)(2,1)} %get-tuple-element.19), channel_id=1, source_target_pairs={{0,64},{64,128},{128,192},{192,256},{256,320},{320,384},{384,448},... | collective-permute-start | bytes 1081352 | tf_op jit(solution)/shard_map/ppermute | solution.py:399
  27.8 16.5 %collective-permute-start.1 = (bf16[44,32,128]{2,1,0:T(8,128)(2,1)}, bf16[44,32,128]{2,1,0:T(8,128)(2,1)S(1)}, u32[]{:S(2)}, u32[]{:S(2)}) collective-permute-start(bf16[44,32,128]{2,1,0:T(8,128)(2,1)} %get-tuple-element.20), channel_id=1, source_target_pairs={{64,0},{128,64},{192,128},{256,192},{320,256},{384,320},{448,384},... | collective-permute-start | bytes 1081352 | tf_op jit(solution)/shard_map/ppermute | solution.py:399
  31.4 12.9 %copy-start.1 = (f32[6,8,32,128]{3,2,1,0:T(8,128)S(1)}, f32[6,8,32,128]{3,2,1,0:T(8,128)}, u32[]{:S(2)}) copy-start(f32[6,8,32,128]{3,2,1,0:T(8,128)} %couple.3) | copy-start | bytes 2359300
  33.0 11.2 %copy-start.6 = (f32[2,8,32,128]{3,2,1,0:T(8,128)S(1)}, f32[2,8,32,128]{3,2,1,0:T(8,128)}, u32[]{:S(2)}) copy-start(f32[2,8,32,128]{3,2,1,0:T(8,128)} %cross.3) | copy-start | bytes 786436
  33.0 11.2 %copy-start.8 = (f32[2,8,32,128]{3,2,1,0:T(8,128)S(1)}, f32[2,8,32,128]{3,2,1,0:T(8,128)}, u32[]{:S(2)}) copy-start(f32[2,8,32,128]{3,2,1,0:T(8,128)} %source.3) | copy-start | bytes 786436
  33.0 29.7 %all-to-all-start.1 = ((bf16[64,16,128]{2,1,0:T(8,128)(2,1)}), bf16[64,16,128]{2,1,0:T(8,128)(2,1)}, u32[]{:S(2)}, u32[]{:S(2)}) async-start(bf16[64,16,128]{2,1,0:T(8,128)(2,1)} %shard_map.104), calls=%async_computation.1 | async-start | bytes 524288 | tf_op jit(solution)/shard_map/all_to_all | solution.py:433
  44.4 10.6 %collective-permute-start.2 = (bf16[100,8,128]{2,1,0:T(8,128)(2,1)S(1)}, bf16[100,8,128]{2,1,0:T(8,128)(2,1)S(1)}, u32[]{:S(2)}, u32[]{:S(2)}) collective-permute-start(bf16[100,8,128]{2,1,0:T(8,128)(2,1)S(1)} %get-tuple-element.21), channel_id=1, source_target_pairs={{0,8},{8,16},{16,24},{24,32},{32,40},{40,48},{48,56},{1,9},{9,17},... | collective-permute-start | bytes 614408 | tf_op jit(solution)/shard_map/ppermute | solution.py:399
  47.3 9.3 %collective-permute-start.3 = (bf16[100,8,128]{2,1,0:T(8,128)(2,1)S(1)}, bf16[100,8,128]{2,1,0:T(8,128)(2,1)S(1)}, u32[]{:S(2)}, u32[]{:S(2)}) collective-permute-start(bf16[100,8,128]{2,1,0:T(8,128)(2,1)S(1)} %get-tuple-element.22), channel_id=1, source_target_pairs={{8,0},{16,8},{24,16},{32,24},{40,32},{48,40},{56,48},{9,1},{17,9},... | collective-permute-start | bytes 614408 | tf_op jit(solution)/shard_map/ppermute | solution.py:399
  57.8 13.5 %collective-permute-start.4 = (bf16[14,40,128]{2,1,0:T(8,128)(2,1)}, bf16[14,40,128]{2,1,0:T(8,128)(2,1)}, u32[]{:S(2)}, u32[]{:S(2)}) collective-permute-start(bf16[14,40,128]{2,1,0:T(8,128)(2,1)} %shard_map.102), channel_id=1, source_target_pairs={{0,1},{1,2},{2,3},{3,4},{4,5},{5,6},{6,7},{8,9},{9,10},{10,11},{11... | collective-permute-start | bytes 430088 | tf_op jit(solution)/shard_map/ppermute | solution.py:399
  61.4 10.0 %collective-permute-start.5 = (bf16[14,40,128]{2,1,0:T(8,128)(2,1)}, bf16[14,40,128]{2,1,0:T(8,128)(2,1)}, u32[]{:S(2)}, u32[]{:S(2)}) collective-permute-start(bf16[14,40,128]{2,1,0:T(8,128)(2,1)} %shard_map.102), channel_id=1, source_target_pairs={{1,0},{2,1},{3,2},{4,3},{5,4},{6,5},{7,6},{9,8},{10,9},{11,10},{12... | collective-permute-start | bytes 430088 | tf_op jit(solution)/shard_map/ppermute | solution.py:399
  64.1 7.3 %collective-permute-start.6 = (bf16[2,3,40,256]{3,2,1,0:T(8,128)(2,1)S(1)}, bf16[2,3,40,256]{3,2,1,0:T(8,128)(2,1)S(1)}, u32[]{:S(2)}, u32[]{:S(2)}) collective-permute-start(bf16[2,3,40,256]{3,2,1,0:T(8,128)(2,1)S(1)} %get-tuple-element.24), channel_id=1, source_target_pairs={{0,64},{64,128},{128,192},{192,256},{256,320},{320,384},{384,448},... | collective-permute-start | bytes 368648 | tf_op jit(solution)/shard_map/ppermute | solution.py:399
  69.4 6.2 %collective-permute-start.7 = (bf16[2,3,40,256]{3,2,1,0:T(8,128)(2,1)S(1)}, bf16[2,3,40,256]{3,2,1,0:T(8,128)(2,1)S(1)}, u32[]{:S(2)}, u32[]{:S(2)}) collective-permute-start(bf16[2,3,40,256]{3,2,1,0:T(8,128)(2,1)S(1)} %get-tuple-element.25), channel_id=1, source_target_pairs={{64,0},{128,64},{192,128},{256,192},{320,256},{384,320},{448,384},... | collective-permute-start | bytes 368648 | tf_op jit(solution)/shard_map/ppermute | solution.py:399
  83.2 24.3 %copy-start.11 = (bf16[1,1,1,4,256,256]{5,4,3,2,1,0:T(8,128)(2,1)S(1)}, bf16[1,1,1,4,256,256]{5,4,3,2,1,0:T(8,128)(2,1)}, u32[]{:S(2)}) copy-start(bf16[1,1,1,4,256,256]{5,4,3,2,1,0:T(8,128)(2,1)} %param.19) | copy-start | bytes 1572868
  126.8 30.8 %collective-permute-start.14 = (bf16[2,3,40,256]{3,2,1,0:T(8,128)(2,1)S(1)}, bf16[2,3,40,256]{3,2,1,0:T(8,128)(2,1)S(1)}, u32[]{:S(2)}, u32[]{:S(2)}) collective-permute-start(bf16[2,3,40,256]{3,2,1,0:T(8,128)(2,1)S(1)} %get-tuple-element.31), channel_id=1, source_target_pairs={{0,64},{64,128},{128,192},{192,256},{256,320},{320,384},{384,448},... | collective-permute-start | bytes 368648 | tf_op jit(solution)/shard_map/ppermute | solution.py:399
  132.1 25.6 %collective-permute-start.15 = (bf16[2,3,40,256]{3,2,1,0:T(8,128)(2,1)S(1)}, bf16[2,3,40,256]{3,2,1,0:T(8,128)(2,1)S(1)}, u32[]{:S(2)}, u32[]{:S(2)}) collective-permute-start(bf16[2,3,40,256]{3,2,1,0:T(8,128)(2,1)S(1)} %get-tuple-element.32), channel_id=1, source_target_pairs={{64,0},{128,64},{192,128},{256,192},{320,256},{384,320},{448,384},... | collective-permute-start | bytes 368648 | tf_op jit(solution)/shard_map/ppermute | solution.py:399
  134.0 5.6 %collective-permute-start.8 = (bf16[8,32,128]{2,1,0:T(8,128)(2,1)S(1)}, bf16[8,32,128]{2,1,0:T(8,128)(2,1)S(1)}, u32[]{:S(2)}, u32[]{:S(2)}) collective-permute-start(bf16[8,32,128]{2,1,0:T(8,128)(2,1)S(1)} %get-tuple-element.26), channel_id=1, source_target_pairs={{0,64},{64,128},{128,192},{192,256},{256,320},{320,384},{384,448},... | collective-permute-start | bytes 196616 | tf_op jit(solution)/shard_map/ppermute | solution.py:399
  137.7 5.6 %collective-permute-start.9 = (bf16[8,32,128]{2,1,0:T(8,128)(2,1)S(1)}, bf16[8,32,128]{2,1,0:T(8,128)(2,1)S(1)}, u32[]{:S(2)}, u32[]{:S(2)}) collective-permute-start(bf16[8,32,128]{2,1,0:T(8,128)(2,1)S(1)} %get-tuple-element.27), channel_id=1, source_target_pairs={{64,0},{128,64},{192,128},{256,192},{320,256},{384,320},{448,384},... | collective-permute-start | bytes 196616 | tf_op jit(solution)/shard_map/ppermute | solution.py:399
  143.3 3.6 %collective-permute-start.10 = (bf16[16,8,128]{2,1,0:T(8,128)(2,1)S(1)}, bf16[16,8,128]{2,1,0:T(8,128)(2,1)S(1)}, u32[]{:S(2)}, u32[]{:S(2)}) collective-permute-start(bf16[16,8,128]{2,1,0:T(8,128)(2,1)S(1)} %get-tuple-element.28), channel_id=1, source_target_pairs={{0,8},{8,16},{16,24},{24,32},{32,40},{40,48},{48,56},{1,9},{9,17},... | collective-permute-start | bytes 98312 | tf_op jit(solution)/shard_map/ppermute | solution.py:399
  145.6 4.7 %collective-permute-start.11 = (bf16[16,8,128]{2,1,0:T(8,128)(2,1)S(1)}, bf16[16,8,128]{2,1,0:T(8,128)(2,1)S(1)}, u32[]{:S(2)}, u32[]{:S(2)}) collective-permute-start(bf16[16,8,128]{2,1,0:T(8,128)(2,1)S(1)} %get-tuple-element.29), channel_id=1, source_target_pairs={{8,0},{16,8},{24,16},{32,24},{40,32},{48,40},{56,48},{9,1},{17,9},... | collective-permute-start | bytes 98312 | tf_op jit(solution)/shard_map/ppermute | solution.py:399
  150.4 4.0 %collective-permute-start.12 = (bf16[2,40,128]{2,1,0:T(8,128)(2,1)S(1)}, bf16[2,40,128]{2,1,0:T(8,128)(2,1)S(1)}, u32[]{:S(2)}, u32[]{:S(2)}) collective-permute-start(bf16[2,40,128]{2,1,0:T(8,128)(2,1)S(1)} %shard_map.109), channel_id=1, source_target_pairs={{0,1},{1,2},{2,3},{3,4},{4,5},{5,6},{6,7},{8,9},{9,10},{10,11},{11... | collective-permute-start | bytes 61448 | tf_op jit(solution)/shard_map/ppermute | solution.py:399
  153.1 4.6 %collective-permute-start.13 = (bf16[2,40,128]{2,1,0:T(8,128)(2,1)S(1)}, bf16[2,40,128]{2,1,0:T(8,128)(2,1)S(1)}, u32[]{:S(2)}, u32[]{:S(2)}) collective-permute-start(bf16[2,40,128]{2,1,0:T(8,128)(2,1)S(1)} %shard_map.109), channel_id=1, source_target_pairs={{1,0},{2,1},{3,2},{4,3},{5,4},{6,5},{7,6},{9,8},{10,9},{11,10},{12... | collective-permute-start | bytes 61448 | tf_op jit(solution)/shard_map/ppermute | solution.py:399
  (1 other events, 0.7 us)

commit v2 on v1

v2 whole, which is shorter than its diff:
```python
import jax
import jax.numpy as jnp
from jax import lax
from jax.experimental import pallas as pl
from jax.experimental.pallas import tpu as pltpu
from jax.sharding import PartitionSpec as P

SWEEPS = 4
OUTER = 2
F32 = jnp.float32
BF16 = jnp.bfloat16
NZ, NY, NX = 8, 32, 128
EZ, EY = 16, 40
OWNERS = 64
SLOTS = 128
CZ = 14


def iota(shape, dim):
    return lax.broadcasted_iota(jnp.int32, shape, dim)


def call(body, out_shape, scratch=(), limit=32):
    return pl.pallas_call(
        body,
        out_shape=out_shape,
        scratch_shapes=list(scratch),
        compiler_params=pltpu.CompilerParams(vmem_limit_bytes=limit * 1024 * 1024),
    )


def dot(a, b):
    return jnp.dot(a.astype(BF16), b.astype(BF16), preferred_element_type=F32)


def y_tiles(ylo, yhi, index):
    low = iota((8, 128), 0) < 4
    a, b = ylo[index].astype(F32), yhi[index].astype(F32)
    even = jnp.where(low, b, pltpu.roll(a, 4, 0))
    odd = jnp.where(low, pltpu.roll(b, 4, 0), a)
    return even, odd


def columns(xlo, xhi, index):
    low = jnp.bitwise_and(iota((EY, 128), 1), 7) < 4
    return jnp.where(low, xlo[index].astype(F32), xhi[index].astype(F32))


def lane_group():
    return lax.shift_right_logical(iota((EY, 128), 1), 3)


def to_strip(plane, z, strip):
    return jnp.where(lane_group() == z, pltpu.roll(plane, 8 * z + 4, 1), strip)


def tall(main, tile):
    return jnp.concatenate([main, tile], axis=0)


def panels_body(adj, perf, owner, slot, out, sc):
    own = owner[...].astype(F32)
    i0, i1 = iota((64, 64), 0), iota((64, 64), 1)
    wide = jnp.broadcast_to(own, (64, 64))
    down = jnp.sum(jnp.where(i0 == i1, wide, 0.0), axis=1, keepdims=True)
    rank = jnp.sum(jnp.where((down == wide) & (i0 < i1), 1.0, 0.0), axis=0, keepdims=True)
    dest = rank * float(OWNERS) + own
    hit = iota((SLOTS, 64), 0).astype(F32) == dest
    row_code = jnp.sum(jnp.where(hit, perf[...].astype(F32) + 1.0, 0.0), axis=1, keepdims=True)
    slot_code = jnp.sum(jnp.where(hit, slot[...].astype(F32) + 1.0, 0.0), axis=1, keepdims=True)
    pick = jnp.where(row_code == (iota((SLOTS, 256), 1) + 1).astype(F32), 1.0, 0.0)
    lane = iota((SLOTS, 128), 1)
    meta = jnp.where(lane == 0, slot_code, jnp.where(lane == 1, row_code, 0.0))
    for c in range(2):
        picked = dot(pick, adj[c].reshape(NZ * NY, NX))
        for k in range(2):
            sc[pl.ds(2 * c + k, 64, stride=8), :] = picked[k * 64 : (k + 1) * 64]
    zero = jnp.zeros((64, 128), F32)
    for k in range(2):
        sc[pl.ds(4 + k, 64, stride=8), :] = meta[k * 64 : (k + 1) * 64]
        sc[pl.ds(6 + k, 64, stride=8), :] = zero
    out[...] = sc[...].astype(BF16)


def panels(adj, perf, owner, slot):
    return call(
        panels_body,
        jax.ShapeDtypeStruct((512, 128), BF16),
        [pltpu.VMEM((512, 128), F32)],
    )(adj, perf, owner, slot)


def owner_body(arrived, well, cross, out, sx, rq):
    sx[...] = arrived[...].astype(F32)

    def rows(i):
        return jnp.concatenate(
            [sx[pl.ds(i, 64, stride=8), :], sx[pl.ds(i + 1, 64, stride=8), :]], axis=0
        )

    meta = rows(4)
    ident, row_code = meta[:, 0:1], meta[:, 1:2]
    panel = jnp.concatenate([rows(0), rows(2)], axis=1)
    i0, i1 = iota((SLOTS, SLOTS), 0), iota((SLOTS, SLOTS), 1)
    across = jnp.sum(jnp.where(i0 == i1, ident, 0.0), axis=0, keepdims=True)
    same = jnp.where(ident == across, 1.0, 0.0)
    totals = dot(same, panel).astype(BF16).astype(F32)
    mixed = jnp.zeros((SLOTS, 256), F32)
    for w in range(4):
        mine = ident == float(w + 1)
        mixed = mixed + dot(jnp.where(mine, panel, 0.0), well[w])
        mixed = mixed + dot(jnp.where(mine, totals, 0.0), cross[w])
    mixed = mixed.astype(BF16).astype(F32)
    tag = jnp.where(iota((SLOTS, 128), 1) == 96, row_code, 0.0)
    for k in range(2):
        part = slice(k * 64, (k + 1) * 64)
        for c in range(2):
            rq[pl.ds(2 * c + k, 64, stride=8), :] = mixed[part, c * 128 : (c + 1) * 128]
        rq[pl.ds(4 + k, 64, stride=8), :] = tag[part]
        rq[pl.ds(6 + k, 64, stride=8), :] = jnp.zeros((64, 128), F32)
    full = rq[...].reshape(64, 8, 128)
    sub, lane = iota((64, 8, 128), 1), iota((64, 8, 128), 2)

    def from_y(v, step):
        gap = jnp.zeros((8, 8, 128), F32)
        return jnp.concatenate([gap, v[:-8]] if step < 0 else [v[8:], gap], axis=0)

    def from_x(v, step):
        v = v.reshape(8, 8, 8, 128)
        gap = jnp.zeros((8, 1, 8, 128), F32)
        v = jnp.concatenate([gap, v[:, :-1]] if step < 0 else [v[:, 1:], gap], axis=1)
        return v.reshape(64, 8, 128)

    def turn(v, by):
        return pltpu.roll(v, by, 2)

    def half(v):
        return pltpu.roll(v, 4, 1)

    below, above = from_y(full, -1), from_y(full, 1)
    edge = jnp.where(lane >= 125, from_x(full, -1), jnp.where(lane < 3, from_x(full, 1), 0.0))
    edges = edge + turn(from_y(edge, -1), 32) + turn(from_y(edge, 1), 64)
    tags = jnp.where((sub >= 4) & (lane == 96), full, 0.0)
    tags = tags + turn(from_y(tags, -1), 1) + turn(from_y(tags, 1), 2)
    tags = tags + turn(from_x(tags, -1), 3) + turn(from_x(tags, 1), 6)
    first = jnp.where(sub < 4, full, half(below))
    second = jnp.where(sub < 4, above, half(jnp.where(sub < 4, edges, 0.0)) + tags)
    out[...] = jnp.concatenate([first, second], axis=1).astype(BF16)


def owner_work(arrived, well, cross):
    return call(
        owner_body,
        jax.ShapeDtypeStruct((64, 16, 128), BF16),
        [pltpu.VMEM((512, 128), F32), pltpu.VMEM((512, 128), F32)],
    )(arrived, well, cross)


def place_body(arrived, *refs):
    ins, (ws, wx, up, down, sx) = refs[:-5], refs[-5:]
    sx[...] = arrived[...].reshape(1024, 128).astype(F32)

    def rows(i):
        return jnp.concatenate(
            [sx[pl.ds(i, 64, stride=16), :], sx[pl.ds(i + 1, 64, stride=16), :]], axis=0
        )

    def both(i):
        return jnp.concatenate([rows(i), rows(i + 2)], axis=1)

    codes = rows(12).T

    def code(n):
        return codes[96 + n : 97 + n, :]

    def place(want, n, values):
        return dot(jnp.where(want == code(n), 1.0, 0.0), values)

    lane = jnp.bitwise_and(iota((SLOTS, 256), 1), 127)

    def sides(by):
        v = jnp.concatenate(
            [pltpu.roll(rows(12), by, 1) if by else rows(12), pltpu.roll(rows(14), by, 1) if by else rows(14)],
            axis=1,
        )
        return jnp.where(lane >= 125, v, 0.0), jnp.where(lane < 3, v, 0.0)

    own = (iota((256, SLOTS), 0) + 1).astype(F32)
    g = iota((64, SLOTS), 0)
    j = jnp.bitwise_and(g, 7)
    base = (g - j) * 4 + j + 1
    high = jnp.where(j < 3, base, -1).astype(F32)
    low = jnp.where(j >= 5, base + 24, -1).astype(F32)
    main = place(own, 0, both(0))
    halo = place(low, 1, both(4)) + place(high, 2, both(8))
    minus, plus = sides(0)
    side = place(own, 3, minus) + place(own, 6, plus)
    minus, plus = sides(96)
    corner = place(low, 4, minus) + place(low, 7, plus)
    minus, plus = sides(64)
    corner = corner + place(high, 5, minus) + place(high, 8, plus)
    for c in range(2):
        part = slice(c * 128, (c + 1) * 128)
        main_c = main[:, part].reshape(8, 32, 128)
        halo_c = halo[:, part].reshape(8, 8, 128)
        side_c = side[:, part].reshape(8, 32, 128)
        corner_c = corner[:, part].reshape(8, 8, 128)
        strip = jnp.zeros((EY, 128), F32)
        for z in range(NZ):
            ws[c, z] = tall(main_c[z], halo_c[z])
            strip = to_strip(tall(side_c[z], corner_c[z]), z + 4, strip)
        wx[c] = strip
        first = 4 if ins else 0
        for ref, z0, w0 in ((up, 4, 5), (down, 0, 0)):
            packed = jnp.where(
                (lane_group() >= first) & (lane_group() < first + 3),
                pltpu.roll(strip, (8 * (first - w0 - 4)) % 128, 1),
                0.0,
            )
            if ins:
                adj, ylo, yhi, xlo, xhi = ins
                cols = columns(xlo, xhi, c)
                cols = pltpu.roll(cols, 128 - 8 * z0, 1) if z0 else cols
                packed = jnp.where(lane_group() < 4, cols, packed)
                for h in range(2):
                    tiles = y_tiles(ylo, yhi, 4 * c + z0 // 2 + h)
                    for o in range(2):
                        ref[c, 2 * h + o] = tall(adj[c, z0 + 2 * h + o], tiles[o]).astype(BF16)
            for j in range(3):
                ref[c, first + j] = tall(main_c[w0 + j], halo_c[w0 + j]).astype(BF16)
            ref[c, first + 3] = packed.astype(BF16)


def place(arrived, *ins):
    sent = jax.ShapeDtypeStruct((2, 8 if ins else 4, EY, 128), BF16)
    return call(
        place_body,
        (
            jax.ShapeDtypeStruct((2, NZ, EY, 128), F32),
            jax.ShapeDtypeStruct((2, EY, 128), F32),
            sent,
            sent,
        ),
        [pltpu.VMEM((1024, 128), F32)],
    )(arrived, *ins)


def fields_of(refs):
    out = [(refs[0], 0), (refs[0], 1)]
    if len(refs) > 1:
        out += [(refs[1], i) for i in range(6)]
        out += [(r, i) for r in refs[2:5] for i in range(2)]
    return out


def ysend_body(*refs):
    ins, (up, down) = refs[:-2], refs[-2:]
    low = iota((8, 128), 0) < 4
    for f, (ref, i) in enumerate(fields_of(ins)):
        for h in range(4):
            z = 2 * h
            up[4 * f + h] = jnp.where(
                low, pltpu.roll(ref[i, z, 24:32], 4, 0), ref[i, z + 1, 24:32]
            ).astype(BF16)
            down[4 * f + h] = jnp.where(
                low, ref[i, z, 0:8], pltpu.roll(ref[i, z + 1, 0:8], 4, 0)
            ).astype(BF16)


def ysend(*ins):
    shape = jax.ShapeDtypeStruct((56 if len(ins) > 1 else 8, 8, 128), BF16)
    return call(ysend_body, (shape, shape))(*ins)


def block_planes(ref, i, f, ylo, yhi):
    planes = []
    for h in range(4):
        tiles = y_tiles(ylo, yhi, 4 * f + h)
        planes += [tall(ref[i, 2 * h + o], tiles[o]) for o in range(2)]
    return planes


def z_slot(f):
    return (4 * f, 4) if f < 2 else (3 * f + 2, 3)


def zsend_body(*refs):
    ins, (ylo, yhi, up, down) = refs[:-4], refs[-4:]
    for f, (ref, i) in enumerate(fields_of(ins)):
        planes = block_planes(ref, i, f, ylo, yhi)
        at, deep = z_slot(f)
        for j in range(deep):
            up[at + j] = planes[NZ - deep + j].astype(BF16)
            down[at + j] = planes[j].astype(BF16)


def zsend(*ins):
    shape = jax.ShapeDtypeStruct((44, EY, NX), BF16)
    return call(zsend_body, (shape, shape))(*ins)


def field_planes(ref, i, f, ylo, yhi, zlo, zhi):
    at, deep = z_slot(f)
    low = [zlo[at + j].astype(F32) for j in range(deep)]
    high = [zhi[at + j].astype(F32) for j in range(deep)]
    return low + block_planes(ref, i, f, ylo, yhi) + high


def xsend_body(*refs):
    if len(refs) == 4:
        adj, ylo, yhi, out = refs
        for c in range(2):
            strip = jnp.zeros((EY, 128), F32)
            for z, plane in enumerate(block_planes(adj, c, c, ylo, yhi)):
                strip = to_strip(plane, z, strip)
            out[c] = strip.astype(BF16)
        return
    ins, (ylo, yhi, zlo, zhi, out) = refs[:-5], refs[-5:]
    for f, (ref, i) in enumerate(fields_of(ins)):
        strip = jnp.zeros((EY, 128), F32)
        for z, plane in enumerate(field_planes(ref, i, f, ylo, yhi, zlo, zhi)):
            strip = to_strip(plane, z + (f >= 2), strip)
        out[f] = strip.astype(BF16)


def xsend(*ins):
    fields = 14 if len(ins) > 3 else 2
    return call(xsend_body, jax.ShapeDtypeStruct((fields, EY, 128), BF16))(*ins)


def sweeps_body(*refs):
    ins, ylo, yhi, zlo, zhi, xlo, xhi = refs[:5], *refs[5:11]
    out, field, fstrip, buf0, buf1, overs, rhs, rstrip = refs[-8:]
    ws, wx, wlo, whi = refs[-12:-8]
    later = refs[11:-12]
    bufs = (buf0, buf1)
    strips = []
    skip = 4 if later else 0
    group = lane_group()
    lane = iota((EY, 128), 1)
    column = jnp.bitwise_and(lane, 7)

    for c in range(2):
        ends = [r[c, skip + 3].astype(F32) for r in (wlo, whi)]
        if later:
            yl, yh, xl, xh = later
            planes = [wlo[c, j].astype(F32) for j in range(4)]
            planes += block_planes(ins[0], c, c, yl, yh)
            planes += [whi[c, j].astype(F32) for j in range(4)]
            strip = pltpu.roll(columns(xl, xh, c), 32, 1)
            strip = jnp.where(group < 4, ends[0], strip)
            strip = jnp.where(group >= 12, pltpu.roll(ends[1], 96, 1), strip)
        else:
            planes = field_planes(ins[0], c, c, ylo, yhi, zlo, zhi)
            strip = columns(xlo, xhi, c)
        for z, plane in enumerate(planes):
            buf0[c, z] = plane
        strips.append(strip)
        side = wx[c]
        side = jnp.where(group < 4, pltpu.roll(ends[0], (8 - 8 * skip) % 128, 1), side)
        side = jnp.where(group >= 12, pltpu.roll(ends[1], 96 - 8 * skip, 1), side)
        rstrip[c] = side + columns(xlo, xhi, 12 + c)
        for e, plane in enumerate(field_planes(ins[4], c, 12 + c, ylo, yhi, zlo, zhi)):
            if e < 3:
                extra = wlo[c, skip + e].astype(F32)
            elif e >= 11:
                extra = whi[c, skip + e - 11].astype(F32)
            else:
                extra = ws[c, e - 3]
            rhs[c, e] = plane + extra
    for n, (ref, i) in enumerate(fields_of(ins)[2:12]):
        for e, plane in enumerate(field_planes(ref, i, n + 2, ylo, yhi, zlo, zhi)):
            field[n, e] = plane
        fstrip[n] = columns(xlo, xhi, n + 2)

    def mix(co, inflow):
        return co(6) * inflow[0] + co(8) * inflow[1], co(9) * inflow[0] + co(7) * inflow[1]

    for s in range(SWEEPS):
        last = s == SWEEPS - 1
        src, dst = bufs[s % 2], bufs[1 - s % 2]
        rows = NY if last else EY
        layers = range(1 + s, EZ - 1 - s)
        edges = []
        for c in range(2):
            edge = jnp.zeros((EY, 128), F32)
            for z in layers:
                overs[c, z] = pltpu.roll(strips[c], 124 - 8 * z, 1)
                if not last:
                    edge = to_strip(src[c, z], z, edge)
            edges.append(edge)

        for z in layers:

            def co(n):
                return field[n, z - 1, 0:rows]

            inflow = []
            for c in range(2):
                here, over = src[c, z], overs[c, z]
                right = pltpu.roll(jnp.where(lane == 0, over, here), 127, 1)
                left = pltpu.roll(jnp.where(lane == 127, over, here), 1, 1)
                total = rhs[c, z - 1, 0:rows]
                total = total + co(0) * src[c, z + 1, 0:rows]
                total = total + co(1) * src[c, z - 1, 0:rows]
                total = total + co(2) * pltpu.roll(here, EY - 1, 0)[0:rows]
                total = total + co(3) * pltpu.roll(here, 1, 0)[0:rows]
                total = total + co(4) * right[0:rows]
                total = total + co(5) * left[0:rows]
                inflow.append(total)
            for c, new in enumerate(mix(co, inflow)):
                if last:
                    out[c, z - 4] = new
                else:
                    dst[c, z] = new
        if last:
            continue

        def co(n):
            return fstrip[n]

        inflow = []
        for c in range(2):
            here, edge = strips[c], edges[c]
            right = pltpu.roll(jnp.where(column == 4, edge, here), 127, 1)
            left = pltpu.roll(jnp.where(column == 3, edge, here), 1, 1)
            total = rstrip[c]
            total = total + co(0) * pltpu.roll(here, 120, 1) + co(1) * pltpu.roll(here, 8, 1)
            total = total + co(2) * pltpu.roll(here, EY - 1, 0) + co(3) * pltpu.roll(here, 1, 0)
            total = total + co(4) * right + co(5) * left
            inflow.append(total)
        strips = list(mix(co, inflow))


def sweeps(*ins):
    return call(
        sweeps_body,
        jax.ShapeDtypeStruct((2, NZ, NY, NX), F32),
        [
            pltpu.VMEM((10, CZ, EY, 128), F32),
            pltpu.VMEM((10, EY, 128), F32),
            pltpu.VMEM((2, EZ, EY, 128), F32),
            pltpu.VMEM((2, EZ, EY, 128), F32),
            pltpu.VMEM((2, EZ, EY, 128), F32),
            pltpu.VMEM((2, CZ, EY, 128), F32),
            pltpu.VMEM((2, EY, 128), F32),
        ],
    )(*ins)


def exchange(up, down, axis):
    count = lax.axis_size(axis)
    forward = [(i, i + 1) for i in range(count - 1)]
    backward = [(i + 1, i) for i in range(count - 1)]
    return lax.ppermute(up, axis, forward), lax.ppermute(down, axis, backward)


def per_device(
    source,
    adjoint_start,
    couple,
    diag_inverse,
    cross_inverse,
    perf_row,
    well_owner,
    well_slot,
    well_block,
    cross_block,
):
    perf = perf_row.reshape(1, -1)
    owner = well_owner.reshape(1, -1)
    slot = well_slot.reshape(1, -1)
    well = well_block.reshape(well_block.shape[3:])
    cross_mats = cross_block.reshape(cross_block.shape[3:])
    fields = (couple, diag_inverse, cross_inverse, source)
    start = (adjoint_start, *fields)
    sent = panels(adjoint_start, perf, owner, slot)
    arrived = lax.all_to_all(sent, ("gy", "gx"), split_axis=0, concat_axis=0, tiled=True)
    ylo, yhi = exchange(*ysend(*start), "gy")
    zlo, zhi = exchange(*zsend(*start, ylo, yhi), "gz")
    packed = xsend(*start, ylo, yhi, zlo, zhi)
    kept = (*fields, ylo, yhi, zlo, zhi, *exchange(packed, packed, "gx"))
    answers = owner_work(arrived, well, cross_mats)
    returned = lax.all_to_all(answers, ("gy", "gx"), split_axis=0, concat_axis=0, tiled=True)
    ws, wx, up, down = place(returned)
    adjoint = sweeps(adjoint_start, *kept, ws, wx, *exchange(up, down, "gz"))

    for _ in range(OUTER - 1):
        sent = panels(adjoint, perf, owner, slot)
        arrived = lax.all_to_all(sent, ("gy", "gx"), split_axis=0, concat_axis=0, tiled=True)
        ylo, yhi = exchange(*ysend(adjoint), "gy")
        arrived, ylo, yhi = lax.optimization_barrier((arrived, ylo, yhi))
        packed = xsend(adjoint, ylo, yhi)
        answers = owner_work(arrived, well, cross_mats)
        returned = lax.all_to_all(answers, ("gy", "gx"), split_axis=0, concat_axis=0, tiled=True)
        halo = (ylo, yhi, *exchange(packed, packed, "gx"))
        ws, wx, up, down = place(returned, adjoint, *halo)
        adjoint = sweeps(adjoint, *kept, *halo, ws, wx, *exchange(up, down, "gz"))
    return adjoint


def solution(mesh):
    placed = (
        P(None, "gz", "gy", "gx"),
        P(None, "gz", "gy", "gx"),
        P(None, "gz", "gy", "gx"),
        P(None, "gz", "gy", "gx"),
        P(None, "gz", "gy", "gx"),
        P("gz", "gy", "gx", None),
        P("gz", "gy", "gx", None, None),
        P("gz", "gy", "gx", None),
        P("gz", "gy", "gx", None, None, None),
        P("gz", "gy", "gx", None, None, None),
    )
    return jax.shard_map(
        per_device, mesh=mesh, in_specs=placed, out_specs=P(None, "gz", "gy", "gx"), check_vma=False
    )
```

time: 167 us -> 147 us (0.88)
  blocking collectives: 41.8 us -> 0 us
  starting transfers between devices: 70.7 us -> 86.4 us
  waiting for transfers between devices: 24.2 us -> 35.5 us
  Pallas kernels: 24 us -> 16.2 us
  local copies, waits for them, and re-layouts: 4.69 us -> 7.31 us
    all_to_all x2 -> x0, blocking collectives: 41.8 us -> none  [the longest x1 23.9 us: per_device(): lax.all_to_all(sent, ('gy', 'gx'), split_axis=0, concat_axis=0, tiled=True)]
    all_to_all x1 -> x2, starting transfers between devices: 17.1 us -> 28.8 us  [per_device(): lax.all_to_all(sent, ('gy', 'gx'), split_axis=0, concat_axis=0, tiled=True)]
    pallas_call x2, Pallas kernels: 15.7 us -> 7.12 us  [sweeps(): call(sweeps_body, jax.ShapeDtypeStruct((2, NZ, NY, NX), F32), [pltpu.VMEM...]
    all_to_all x1 -> x2, starting transfers between devices: 11.2 us -> 19.2 us  [per_device(): lax.all_to_all(answers, ('gy', 'gx'), split_axis=0, concat_axis=0, tiled=...]
    all_to_all x1 -> x2, waiting for transfers between devices: 1.65 us -> 7.88 us  [per_device(): lax.all_to_all(sent, ('gy', 'gx'), split_axis=0, concat_axis=0, tiled=True)]
    all_to_all x1 -> x2, waiting for transfers between devices: 0.01 us -> 6.23 us  [per_device(): lax.all_to_all(answers, ('gy', 'gx'), split_axis=0, concat_axis=0, tiled=...]
    ppermute x16 -> x14, starting transfers between devices: 42.4 us -> 38.3 us  [exchange(): return (lax.ppermute(up, axis, forward), lax.ppermute(down, axis, backward))]
    unnamed x30 -> x48, local copies, waits for them, and re-layouts: 4.69 us -> 7.31 us
  transfers between devices with their start and end apart: 18 -> 18, of which waited for: 7 -> 10; matrix products, arithmetic and copies ran while one was open for 0% -> 0% of each run, Pallas kernels for 3% -> 3%
where the time goes in v2:
time: 147 us; the launch traced here: 146 us
  starting transfers between devices  86.4 us (59%)
  waiting for transfers between devices  35.5 us (24%)
  Pallas kernels  16.2 us (11%)
  local copies, waits for them, and re-layouts  7.31 us (5%)
    ppermute x14, starting transfers between devices, exchange(): return (lax.ppermute(up, axis, forward), lax.ppermute(down, axis, backward))  38.3 us
    all_to_all x2, starting transfers between devices, per_device(): lax.all_to_all(sent, ('gy', 'gx'), split_axis=0, concat_axis=0, tiled=True)  28.8 us
    ppermute x14, waiting for transfers between devices, exchange(): return (lax.ppermute(up, axis, forward), lax.ppermute(down, axis, backward))  21.4 us
    all_to_all x2, starting transfers between devices, per_device(): lax.all_to_all(answers, ('gy', 'gx'), split_axis=0, concat_axis=0, tiled=...  19.2 us
    all_to_all x2, waiting for transfers between devices, per_device(): lax.all_to_all(sent, ('gy', 'gx'), split_axis=0, concat_axis=0, tiled=True)  7.88 us
    unnamed x48, local copies, waits for them, and re-layouts  7.31 us
    pallas_call x2, Pallas kernels, sweeps(): call(sweeps_body, jax.ShapeDtypeStruct((2, NZ, NY, NX), F32), [pltpu.VMEM...  7.12 us
    all_to_all x2, waiting for transfers between devices, per_device(): lax.all_to_all(answers, ('gy', 'gx'), split_axis=0, concat_axis=0, tiled=...  6.23 us
  transfers between devices with their start and end apart: 18, of which 10 were waited for; matrix products, arithmetic and copies ran while one was open for 0% of the time, Pallas kernels for 3%

profile of v2, /device:TPU:1, one launch (start us, length us, event | category | flops | bytes accessed | tf_op | source)
XLA Modules:
  0.0 145.7 jit_solution(1042470585928996050)
XLA Ops:
  2.7 17.1 %all-to-all-start = ((bf16[64,8,128]{2,1,0:T(8,128)(2,1)}), bf16[64,8,128]{2,1,0:T(8,128)(2,1)S(1)}, u32[]{:S(2)}, u32[]{:S(2)}) async-start(bf16[64,8,128]{2,1,0:T(8,128)(2,1)} %bitcast.3), calls=%async_computation | async-start | bytes 262144 | tf_op jit(solution)/shard_map/all_to_all | solution.py:478
  22.9 3.1 %collective-permute-start = (bf16[56,8,128]{2,1,0:T(8,128)(2,1)S(1)}, bf16[56,8,128]{2,1,0:T(8,128)(2,1)S(1)}, u32[]{:S(2)}, u32[]{:S(2)}) collective-permute-start(bf16[56,8,128]{2,1,0:T(8,128)(2,1)S(1)} %get-tuple-element.22), channel_id=1, source_target_pairs={{0,8},{8,16},{16,24},{24,32},{32,40},{40,48},{48,56},{1,9},{9,17},... | collective-permute-start | bytes 344072 | tf_op jit(solution)/shard_map/ppermute | solution.py:455
  26.0 1.3 collective-permute-start.1
  27.3 4.0 %all-to-all-done = bf16[64,8,128]{2,1,0:T(8,128)(2,1)S(1)} async-done(((bf16[64,8,128]{2,1,0:T(8,128)(2,1)}), bf16[64,8,128]{2,1,0:T(8,128)(2,1)S(1)}, u32[]{:S(2)}, u32[]{:S(2)}) %all-to-all-start) | async-done | bytes 131104 | tf_op jit(solution)/shard_map/all_to_all | solution.py:478
  31.4 1.7 %shard_map.104 = bf16[64,16,128]{2,1,0:T(8,128)(2,1)} custom-call(bf16[512,128]{1,0:T(8,128)(2,1)S(1)} %bitcast.14, bf16[4,256,256]{2,1,0:T(8,128)(2,1)S(1)} %bitcast.9, bf16[4,256,256]{2,1,0:T(8,128)(2,1)S(1)} %bitcast.11), custom_call_target="tpu_custom_call" | custom-call | tf_op jit(solution)/shard_map/pallas_call | solution.py:152
  33.0 10.8 %all-to-all-start.1 = ((bf16[64,16,128]{2,1,0:T(8,128)(2,1)}), bf16[64,16,128]{2,1,0:T(8,128)(2,1)}, u32[]{:S(2)}, u32[]{:S(2)}) async-start(bf16[64,16,128]{2,1,0:T(8,128)(2,1)} %shard_map.104), calls=%async_computation.1 | async-start | bytes 524288 | tf_op jit(solution)/shard_map/all_to_all | solution.py:484
  44.0 5.1 %collective-permute-start.2 = (bf16[44,40,128]{2,1,0:T(8,128)(2,1)S(1)}, bf16[44,40,128]{2,1,0:T(8,128)(2,1)S(1)}, u32[]{:S(2)}, u32[]{:S(2)}) collective-permute-start(bf16[44,40,128]{2,1,0:T(8,128)(2,1)S(1)} %get-tuple-element.24), channel_id=1, source_target_pairs={{0,64},{64,128},{128,192},{192,256},{256,320},{320,384},{384,448},... | collective-permute-start | bytes 1351688 | tf_op jit(solution)/shard_map/ppermute | solution.py:455
  49.1 1.9 %collective-permute-start.3 = (bf16[44,40,128]{2,1,0:T(8,128)(2,1)S(1)}, bf16[44,40,128]{2,1,0:T(8,128)(2,1)S(1)}, u32[]{:S(2)}, u32[]{:S(2)}) collective-permute-start(bf16[44,40,128]{2,1,0:T(8,128)(2,1)S(1)} %get-tuple-element.25), channel_id=1, source_target_pairs={{64,0},{128,64},{192,128},{256,192},{320,256},{384,320},{448,384},... | collective-permute-start | bytes 1351688 | tf_op jit(solution)/shard_map/ppermute | solution.py:455
  51.0 3.4 %collective-permute-done.2.refs_7_ = bf16[44,40,128]{2,1,0:T(8,128)(2,1)S(1)} collective-permute-done((bf16[44,40,128]{2,1,0:T(8,128)(2,1)S(1)}, bf16[44,40,128]{2,1,0:T(8,128)(2,1)S(1)}, u32[]{:S(2)}, u32[]{:S(2)}) %collective-permute-start.2) | collective-permute-done | bytes 450592 | tf_op jit(solution)/shard_map/ppermute | solution.py:455
  54.4 4.8 %collective-permute-done.3.refs_8_ = bf16[44,40,128]{2,1,0:T(8,128)(2,1)S(1)} collective-permute-done((bf16[44,40,128]{2,1,0:T(8,128)(2,1)S(1)}, bf16[44,40,128]{2,1,0:T(8,128)(2,1)S(1)}, u32[]{:S(2)}, u32[]{:S(2)}) %collective-permute-start.3) | collective-permute-done | bytes 450592 | tf_op jit(solution)/shard_map/ppermute | solution.py:455
  60.5 1.3 collective-permute-start.5
  61.8 4.7 %collective-permute-start.4 = (bf16[14,40,128]{2,1,0:T(8,128)(2,1)}, bf16[14,40,128]{2,1,0:T(8,128)(2,1)}, u32[]{:S(2)}, u32[]{:S(2)}) collective-permute-start(bf16[14,40,128]{2,1,0:T(8,128)(2,1)} %shard_map.102), channel_id=1, source_target_pairs={{0,1},{1,2},{2,3},{3,4},{4,5},{5,6},{6,7},{8,9},{9,10},{10,11},{11... | collective-permute-start | bytes 430088 | tf_op jit(solution)/shard_map/ppermute | solution.py:455
  66.4 1.6 %shard_map.105 = (f32[2,8,40,128]{3,2,1,0:T(8,128)S(1)}, f32[2,40,128]{2,1,0:T(8,128)S(1)}, bf16[2,4,40,128]{3,2,1,0:T(8,128)(2,1)S(1)}, bf16[2,4,40,128]{3,2,1,0:T(8,128)(2,1)S(1)}) custom-call(bf16[64,16,128]{2,1,0:T(8,128)(2,1)} %all-to-all-done.1.arrived), custom_call_target="tpu_custom_call" | custom-call | tf_op jit(solution)/shard_map/pallas_call | solution.py:236
  68.0 1.9 %collective-permute-start.6 = (bf16[2,4,40,128]{3,2,1,0:T(8,128)(2,1)S(1)}, bf16[2,4,40,128]{3,2,1,0:T(8,128)(2,1)S(1)}, u32[]{:S(2)}, u32[]{:S(2)}) collective-permute-start(bf16[2,4,40,128]{3,2,1,0:T(8,128)(2,1)S(1)} %get-tuple-element.28), channel_id=1, source_target_pairs={{0,64},{64,128},{128,192},{192,256},{256,320},{320,384},{384,448},... | collective-permute-start | bytes 245768 | tf_op jit(solution)/shard_map/ppermute | solution.py:455
  69.9 2.4 %collective-permute-start.7 = (bf16[2,4,40,128]{3,2,1,0:T(8,128)(2,1)S(1)}, bf16[2,4,40,128]{3,2,1,0:T(8,128)(2,1)S(1)}, u32[]{:S(2)}, u32[]{:S(2)}) collective-permute-start(bf16[2,4,40,128]{3,2,1,0:T(8,128)(2,1)S(1)} %get-tuple-element.29), channel_id=1, source_target_pairs={{64,0},{128,64},{192,128},{256,192},{320,256},{384,320},{448,384},... | collective-permute-start | bytes 245768 | tf_op jit(solution)/shard_map/ppermute | solution.py:455
  73.0 2.7 %collective-permute-done.7.refs_14_ = bf16[2,4,40,128]{3,2,1,0:T(8,128)(2,1)S(1)} collective-permute-done((bf16[2,4,40,128]{3,2,1,0:T(8,128)(2,1)S(1)}, bf16[2,4,40,128]{3,2,1,0:T(8,128)(2,1)S(1)}, u32[]{:S(2)}, u32[]{:S(2)}) %collective-permute-start.7) | collective-permute-done | bytes 81952 | tf_op jit(solution)/shard_map/ppermute | solution.py:455
  76.6 3.2 %shard_map.106.adj.refs_0_ = f32[2,8,32,128]{3,2,1,0:T(8,128)S(1)} custom-call(f32[2,8,32,128]{3,2,1,0:T(8,128)S(1)} %copy-done.3, f32[6,8,32,128]{3,2,1,0:T(8,128)S(1)} %copy-done.1, f32[2,8,32,128]{3,2,1,0:T(8,128)S(1)} %copy-done.4, f32[2,8,32,128]{3,2,1,0:T(8,128)S(1)} %copy-done.6, f32[2,8,32,128]{3,2,1,0:T(8,128)S(1)} %copy-done.8, ...), custom_call_target="tpu_custom_call" | custom-call | tf_op jit(solution)/shard_map/pallas_call | solution.py:436
  80.8 11.7 %all-to-all-start.2 = ((bf16[64,8,128]{2,1,0:T(8,128)(2,1)}), bf16[64,8,128]{2,1,0:T(8,128)(2,1)S(1)}, u32[]{:S(2)}, u32[]{:S(2)}) async-start(bf16[64,8,128]{2,1,0:T(8,128)(2,1)} %bitcast.7), calls=%async_computation.2 | async-start | bytes 262144 | tf_op jit(solution)/shard_map/all_to_all | solution.py:490
  92.5 2.9 %collective-permute-start.8 = (bf16[8,8,128]{2,1,0:T(8,128)(2,1)S(1)}, bf16[8,8,128]{2,1,0:T(8,128)(2,1)S(1)}, u32[]{:S(2)}, u32[]{:S(2)}) collective-permute-start(bf16[8,8,128]{2,1,0:T(8,128)(2,1)S(1)} %get-tuple-element.30), channel_id=1, source_target_pairs={{0,8},{8,16},{16,24},{24,32},{32,40},{40,48},{48,56},{1,9},{9,17},... | collective-permute-start | bytes 49160 | tf_op jit(solution)/shard_map/ppermute | solution.py:455
  95.5 1.3 collective-permute-start.9
  96.8 3.5 %collective-permute-done.9.refs_2_.refs_12_ = bf16[8,8,128]{2,1,0:T(8,128)(2,1)S(1)} collective-permute-done((bf16[8,8,128]{2,1,0:T(8,128)(2,1)S(1)}, bf16[8,8,128]{2,1,0:T(8,128)(2,1)S(1)}, u32[]{:S(2)}, u32[]{:S(2)}) %collective-permute-start.9) | collective-permute-done | bytes 16416 | tf_op jit(solution)/shard_map/ppermute | solution.py:455
  100.3 3.8 %all-to-all-done.2 = bf16[64,8,128]{2,1,0:T(8,128)(2,1)S(1)} async-done(((bf16[64,8,128]{2,1,0:T(8,128)(2,1)}), bf16[64,8,128]{2,1,0:T(8,128)(2,1)S(1)}, u32[]{:S(2)}, u32[]{:S(2)}) %all-to-all-start.2) | async-done | bytes 131104 | tf_op jit(solution)/shard_map/all_to_all | solution.py:490
  105.2 1.7 %shard_map.110 = bf16[64,16,128]{2,1,0:T(8,128)(2,1)} custom-call(bf16[512,128]{1,0:T(8,128)(2,1)S(1)} %bitcast.13, bf16[4,256,256]{2,1,0:T(8,128)(2,1)S(1)} %bitcast.10, bf16[4,256,256]{2,1,0:T(8,128)(2,1)S(1)} %bitcast.12), custom_call_target="tpu_custom_call" | custom-call | tf_op jit(solution)/shard_map/pallas_call | solution.py:152
  106.8 8.5 %all-to-all-start.3 = ((bf16[64,16,128]{2,1,0:T(8,128)(2,1)}), bf16[64,16,128]{2,1,0:T(8,128)(2,1)S(1)}, u32[]{:S(2)}, u32[]{:S(2)}) async-start(bf16[64,16,128]{2,1,0:T(8,128)(2,1)} %shard_map.110), calls=%async_computation.3 | async-start | bytes 524288 | tf_op jit(solution)/shard_map/all_to_all | solution.py:495
  115.4 1.4 collective-permute-start.11
  116.9 4.0 %collective-permute-start.10 = (bf16[2,40,128]{2,1,0:T(8,128)(2,1)S(1)}, bf16[2,40,128]{2,1,0:T(8,128)(2,1)S(1)}, u32[]{:S(2)}, u32[]{:S(2)}) collective-permute-start(bf16[2,40,128]{2,1,0:T(8,128)(2,1)S(1)} %shard_map.109), channel_id=1, source_target_pairs={{0,1},{1,2},{2,3},{3,4},{4,5},{5,6},{6,7},{8,9},{9,10},{10,11},{11... | collective-permute-start | bytes 61448 | tf_op jit(solution)/shard_map/ppermute | solution.py:455
  120.9 2.3 %collective-permute-done.11.refs_4_.refs_14_ = bf16[2,40,128]{2,1,0:T(8,128)(2,1)S(1)} collective-permute-done((bf16[2,40,128]{2,1,0:T(8,128)(2,1)S(1)}, bf16[2,40,128]{2,1,0:T(8,128)(2,1)S(1)}, u32[]{:S(2)}, u32[]{:S(2)}) %collective-permute-start.11) | collective-permute-done | bytes 20512 | tf_op jit(solution)/shard_map/ppermute | solution.py:455
  123.1 6.2 %all-to-all-done.3.arrived = bf16[64,16,128]{2,1,0:T(8,128)(2,1)S(1)} async-done(((bf16[64,16,128]{2,1,0:T(8,128)(2,1)}), bf16[64,16,128]{2,1,0:T(8,128)(2,1)S(1)}, u32[]{:S(2)}, u32[]{:S(2)}) %all-to-all-start.3) | async-done | bytes 262176 | tf_op jit(solution)/shard_map/all_to_all | solution.py:495
  130.0 5.1 %collective-permute-start.12 = (bf16[2,8,40,128]{3,2,1,0:T(8,128)(2,1)S(1)}, bf16[2,8,40,128]{3,2,1,0:T(8,128)(2,1)S(1)}, u32[]{:S(2)}, u32[]{:S(2)}) collective-permute-start(bf16[2,8,40,128]{3,2,1,0:T(8,128)(2,1)S(1)} %get-tuple-element.37), channel_id=1, source_target_pairs={{0,64},{64,128},{128,192},{192,256},{256,320},{320,384},{384,448},... | collective-permute-start | bytes 491528 | tf_op jit(solution)/shard_map/ppermute | solution.py:455
  135.1 1.9 %collective-permute-start.13 = (bf16[2,8,40,128]{3,2,1,0:T(8,128)(2,1)S(1)}, bf16[2,8,40,128]{3,2,1,0:T(8,128)(2,1)S(1)}, u32[]{:S(2)}, u32[]{:S(2)}) collective-permute-start(bf16[2,8,40,128]{3,2,1,0:T(8,128)(2,1)S(1)} %get-tuple-element.38), channel_id=1, source_target_pairs={{64,0},{128,64},{192,128},{256,192},{320,256},{384,320},{448,384},... | collective-permute-start | bytes 491528 | tf_op jit(solution)/shard_map/ppermute | solution.py:455
  137.3 4.4 %collective-permute-done.13.refs_18_ = bf16[2,8,40,128]{3,2,1,0:T(8,128)(2,1)S(1)} collective-permute-done((bf16[2,8,40,128]{3,2,1,0:T(8,128)(2,1)S(1)}, bf16[2,8,40,128]{3,2,1,0:T(8,128)(2,1)S(1)}, u32[]{:S(2)}, u32[]{:S(2)}) %collective-permute-start.13) | collective-permute-done | bytes 163872 | tf_op jit(solution)/shard_map/ppermute | solution.py:455
  141.8 4.0 %shard_map.112 = f32[2,8,32,128]{3,2,1,0:T(8,128)} custom-call(f32[2,8,32,128]{3,2,1,0:T(8,128)S(1)} %shard_map.106.adj.refs_0_, f32[6,8,32,128]{3,2,1,0:T(8,128)S(1)} %copy-done.1, f32[2,8,32,128]{3,2,1,0:T(8,128)S(1)} %copy-done.4, f32[2,8,32,128]{3,2,1,0:T(8,128)S(1)} %copy-done.6, f32[2,8,32,128]{3,2,1,0:T(8,128)S(1)} %copy-done.8, ...), custom_call_target="tpu_custom_call" | custom-call | tf_op jit(solution)/shard_map/pallas_call | solution.py:436
  (65 shorter events, 11.8 us)
Async XLA Ops:
  1.6 18.2 %copy-start.3 = (f32[2,8,32,128]{3,2,1,0:T(8,128)S(1)}, f32[2,8,32,128]{3,2,1,0:T(8,128)}, u32[]{:S(2)}) copy-start(f32[2,8,32,128]{3,2,1,0:T(8,128)} %refs_0_.7) | copy-start | bytes 786436
  1.6 18.2 %copy-start.4 = (f32[2,8,32,128]{3,2,1,0:T(8,128)S(1)}, f32[2,8,32,128]{3,2,1,0:T(8,128)}, u32[]{:S(2)}) copy-start(f32[2,8,32,128]{3,2,1,0:T(8,128)} %refs_2_.9) | copy-start | bytes 786436
  2.7 28.7 %all-to-all-start = ((bf16[64,8,128]{2,1,0:T(8,128)(2,1)}), bf16[64,8,128]{2,1,0:T(8,128)(2,1)S(1)}, u32[]{:S(2)}, u32[]{:S(2)}) async-start(bf16[64,8,128]{2,1,0:T(8,128)(2,1)} %bitcast.3), calls=%async_computation | async-start | bytes 262144 | tf_op jit(solution)/shard_map/all_to_all | solution.py:478
  22.9 8.5 %copy-start.9 = (bf16[1,1,1,4,256,256]{5,4,3,2,1,0:T(8,128)(2,1)S(1)}, bf16[1,1,1,4,256,256]{5,4,3,2,1,0:T(8,128)(2,1)}, u32[]{:S(2)}) copy-start(bf16[1,1,1,4,256,256]{5,4,3,2,1,0:T(8,128)(2,1)} %param.18) | copy-start | bytes 1572868
  22.9 8.5 %copy-start.10 = (bf16[1,1,1,4,256,256]{5,4,3,2,1,0:T(8,128)(2,1)S(1)}, bf16[1,1,1,4,256,256]{5,4,3,2,1,0:T(8,128)(2,1)}, u32[]{:S(2)}) copy-start(bf16[1,1,1,4,256,256]{5,4,3,2,1,0:T(8,128)(2,1)} %param.19) | copy-start | bytes 1572868
  22.9 20.9 %collective-permute-start = (bf16[56,8,128]{2,1,0:T(8,128)(2,1)S(1)}, bf16[56,8,128]{2,1,0:T(8,128)(2,1)S(1)}, u32[]{:S(2)}, u32[]{:S(2)}) collective-permute-start(bf16[56,8,128]{2,1,0:T(8,128)(2,1)S(1)} %get-tuple-element.22), channel_id=1, source_target_pairs={{0,8},{8,16},{16,24},{24,32},{32,40},{40,48},{48,56},{1,9},{9,17},... | collective-permute-start | bytes 344072 | tf_op jit(solution)/shard_map/ppermute | solution.py:455
  26.0 17.8 %collective-permute-start.1 = (bf16[56,8,128]{2,1,0:T(8,128)(2,1)S(1)}, bf16[56,8,128]{2,1,0:T(8,128)(2,1)S(1)}, u32[]{:S(2)}, u32[]{:S(2)}) collective-permute-start(bf16[56,8,128]{2,1,0:T(8,128)(2,1)S(1)} %get-tuple-element.23), channel_id=1, source_target_pairs={{8,0},{16,8},{24,16},{32,24},{40,32},{48,40},{56,48},{9,1},{17,9},... | collective-permute-start | bytes 344072 | tf_op jit(solution)/shard_map/ppermute | solution.py:455
  31.4 12.5 %copy-start.1 = (f32[6,8,32,128]{3,2,1,0:T(8,128)S(1)}, f32[6,8,32,128]{3,2,1,0:T(8,128)}, u32[]{:S(2)}) copy-start(f32[6,8,32,128]{3,2,1,0:T(8,128)} %refs_1_.9) | copy-start | bytes 2359300
  33.0 10.8 %copy-start.6 = (f32[2,8,32,128]{3,2,1,0:T(8,128)S(1)}, f32[2,8,32,128]{3,2,1,0:T(8,128)}, u32[]{:S(2)}) copy-start(f32[2,8,32,128]{3,2,1,0:T(8,128)} %refs_3_.9) | copy-start | bytes 786436
  33.0 10.9 %copy-start.8 = (f32[2,8,32,128]{3,2,1,0:T(8,128)S(1)}, f32[2,8,32,128]{3,2,1,0:T(8,128)}, u32[]{:S(2)}) copy-start(f32[2,8,32,128]{3,2,1,0:T(8,128)} %refs_4_.9) | copy-start | bytes 786436
  33.0 33.4 %all-to-all-start.1 = ((bf16[64,16,128]{2,1,0:T(8,128)(2,1)}), bf16[64,16,128]{2,1,0:T(8,128)(2,1)}, u32[]{:S(2)}, u32[]{:S(2)}) async-start(bf16[64,16,128]{2,1,0:T(8,128)(2,1)} %shard_map.104), calls=%async_computation.1 | async-start | bytes 524288 | tf_op jit(solution)/shard_map/all_to_all | solution.py:484
  43.8 15.4 %copy-start.12 = (bf16[56,8,128]{2,1,0:T(8,128)(2,1)}, bf16[56,8,128]{2,1,0:T(8,128)(2,1)S(1)}, u32[]{:S(2)}) copy-start(bf16[56,8,128]{2,1,0:T(8,128)(2,1)S(1)} %collective-permute-done.refs_5_) | copy-start | bytes 344068
  43.9 15.3 %copy-start.15 = (bf16[56,8,128]{2,1,0:T(8,128)(2,1)}, bf16[56,8,128]{2,1,0:T(8,128)(2,1)S(1)}, u32[]{:S(2)}) copy-start(bf16[56,8,128]{2,1,0:T(8,128)(2,1)S(1)} %collective-permute-done.1.refs_6_) | copy-start | bytes 344068
  44.0 10.4 %collective-permute-start.2 = (bf16[44,40,128]{2,1,0:T(8,128)(2,1)S(1)}, bf16[44,40,128]{2,1,0:T(8,128)(2,1)S(1)}, u32[]{:S(2)}, u32[]{:S(2)}) collective-permute-start(bf16[44,40,128]{2,1,0:T(8,128)(2,1)S(1)} %get-tuple-element.24), channel_id=1, source_target_pairs={{0,64},{64,128},{128,192},{192,256},{256,320},{320,384},{384,448},... | collective-permute-start | bytes 1351688 | tf_op jit(solution)/shard_map/ppermute | solution.py:455
  49.1 10.1 %collective-permute-start.3 = (bf16[44,40,128]{2,1,0:T(8,128)(2,1)S(1)}, bf16[44,40,128]{2,1,0:T(8,128)(2,1)S(1)}, u32[]{:S(2)}, u32[]{:S(2)}) collective-permute-start(bf16[44,40,128]{2,1,0:T(8,128)(2,1)S(1)} %get-tuple-element.25), channel_id=1, source_target_pairs={{64,0},{128,64},{192,128},{256,192},{320,256},{384,320},{448,384},... | collective-permute-start | bytes 1351688 | tf_op jit(solution)/shard_map/ppermute | solution.py:455
  60.5 11.9 %collective-permute-start.5 = (bf16[14,40,128]{2,1,0:T(8,128)(2,1)}, bf16[14,40,128]{2,1,0:T(8,128)(2,1)S(1)}, u32[]{:S(2)}, u32[]{:S(2)}) collective-permute-start(bf16[14,40,128]{2,1,0:T(8,128)(2,1)} %shard_map.102), channel_id=1, source_target_pairs={{1,0},{2,1},{3,2},{4,3},{5,4},{6,5},{7,6},{9,8},{10,9},{11,10},{12... | collective-permute-start | bytes 430088 | tf_op jit(solution)/shard_map/ppermute | solution.py:455
  61.8 11.3 %collective-permute-start.4 = (bf16[14,40,128]{2,1,0:T(8,128)(2,1)}, bf16[14,40,128]{2,1,0:T(8,128)(2,1)}, u32[]{:S(2)}, u32[]{:S(2)}) collective-permute-start(bf16[14,40,128]{2,1,0:T(8,128)(2,1)} %shard_map.102), channel_id=1, source_target_pairs={{0,1},{1,2},{2,3},{3,4},{4,5},{5,6},{6,7},{8,9},{9,10},{10,11},{11... | collective-permute-start | bytes 430088 | tf_op jit(solution)/shard_map/ppermute | solution.py:455
  66.4 9.3 %copy-start.13 = (bf16[56,8,128]{2,1,0:T(8,128)(2,1)S(1)}, bf16[56,8,128]{2,1,0:T(8,128)(2,1)}, u32[]{:S(2)}) copy-start(bf16[56,8,128]{2,1,0:T(8,128)(2,1)} %copy-done.12) | copy-start | bytes 344068
  66.4 9.3 %copy-start.16 = (bf16[56,8,128]{2,1,0:T(8,128)(2,1)S(1)}, bf16[56,8,128]{2,1,0:T(8,128)(2,1)}, u32[]{:S(2)}) copy-start(bf16[56,8,128]{2,1,0:T(8,128)(2,1)} %copy-done.15) | copy-start | bytes 344068
  68.0 5.0 %collective-permute-start.6 = (bf16[2,4,40,128]{3,2,1,0:T(8,128)(2,1)S(1)}, bf16[2,4,40,128]{3,2,1,0:T(8,128)(2,1)S(1)}, u32[]{:S(2)}, u32[]{:S(2)}) collective-permute-start(bf16[2,4,40,128]{3,2,1,0:T(8,128)(2,1)S(1)} %get-tuple-element.28), channel_id=1, source_target_pairs={{0,64},{64,128},{128,192},{192,256},{256,320},{320,384},{384,448},... | collective-permute-start | bytes 245768 | tf_op jit(solution)/shard_map/ppermute | solution.py:455
  69.9 5.8 %collective-permute-start.7 = (bf16[2,4,40,128]{3,2,1,0:T(8,128)(2,1)S(1)}, bf16[2,4,40,128]{3,2,1,0:T(8,128)(2,1)S(1)}, u32[]{:S(2)}, u32[]{:S(2)}) collective-permute-start(bf16[2,4,40,128]{3,2,1,0:T(8,128)(2,1)S(1)} %get-tuple-element.29), channel_id=1, source_target_pairs={{64,0},{128,64},{192,128},{256,192},{320,256},{384,320},{448,384},... | collective-permute-start | bytes 245768 | tf_op jit(solution)/shard_map/ppermute | solution.py:455
  80.8 23.3 %all-to-all-start.2 = ((bf16[64,8,128]{2,1,0:T(8,128)(2,1)}), bf16[64,8,128]{2,1,0:T(8,128)(2,1)S(1)}, u32[]{:S(2)}, u32[]{:S(2)}) async-start(bf16[64,8,128]{2,1,0:T(8,128)(2,1)} %bitcast.7), calls=%async_computation.2 | async-start | bytes 262144 | tf_op jit(solution)/shard_map/all_to_all | solution.py:490
  92.5 4.2 %collective-permute-start.8 = (bf16[8,8,128]{2,1,0:T(8,128)(2,1)S(1)}, bf16[8,8,128]{2,1,0:T(8,128)(2,1)S(1)}, u32[]{:S(2)}, u32[]{:S(2)}) collective-permute-start(bf16[8,8,128]{2,1,0:T(8,128)(2,1)S(1)} %get-tuple-element.30), channel_id=1, source_target_pairs={{0,8},{8,16},{16,24},{24,32},{32,40},{40,48},{48,56},{1,9},{9,17},... | collective-permute-start | bytes 49160 | tf_op jit(solution)/shard_map/ppermute | solution.py:455
  95.5 4.8 %collective-permute-start.9 = (bf16[8,8,128]{2,1,0:T(8,128)(2,1)S(1)}, bf16[8,8,128]{2,1,0:T(8,128)(2,1)S(1)}, u32[]{:S(2)}, u32[]{:S(2)}) collective-permute-start(bf16[8,8,128]{2,1,0:T(8,128)(2,1)S(1)} %get-tuple-element.31), channel_id=1, source_target_pairs={{8,0},{16,8},{24,16},{32,24},{40,32},{48,40},{56,48},{9,1},{17,9},... | collective-permute-start | bytes 49160 | tf_op jit(solution)/shard_map/ppermute | solution.py:455
  106.8 22.5 %all-to-all-start.3 = ((bf16[64,16,128]{2,1,0:T(8,128)(2,1)}), bf16[64,16,128]{2,1,0:T(8,128)(2,1)S(1)}, u32[]{:S(2)}, u32[]{:S(2)}) async-start(bf16[64,16,128]{2,1,0:T(8,128)(2,1)} %shard_map.110), calls=%async_computation.3 | async-start | bytes 524288 | tf_op jit(solution)/shard_map/all_to_all | solution.py:495
  115.4 26.3 %copy-start.14 = (bf16[56,8,128]{2,1,0:T(8,128)(2,1)S(1)}, bf16[56,8,128]{2,1,0:T(8,128)(2,1)}, u32[]{:S(2)}) copy-start(bf16[56,8,128]{2,1,0:T(8,128)(2,1)} %copy-done.12) | copy-start | bytes 344068
  115.4 26.3 %copy-start.17 = (bf16[56,8,128]{2,1,0:T(8,128)(2,1)S(1)}, bf16[56,8,128]{2,1,0:T(8,128)(2,1)}, u32[]{:S(2)}) copy-start(bf16[56,8,128]{2,1,0:T(8,128)(2,1)} %copy-done.15) | copy-start | bytes 344068
  115.4 26.3 %copy-start.20 = (bf16[14,40,128]{2,1,0:T(8,128)(2,1)S(1)}, bf16[14,40,128]{2,1,0:T(8,128)(2,1)}, u32[]{:S(2)}) copy-start(bf16[14,40,128]{2,1,0:T(8,128)(2,1)} %copy-done.18) | copy-start | bytes 430084
  115.4 7.7 %collective-permute-start.11 = (bf16[2,40,128]{2,1,0:T(8,128)(2,1)S(1)}, bf16[2,40,128]{2,1,0:T(8,128)(2,1)S(1)}, u32[]{:S(2)}, u32[]{:S(2)}) collective-permute-start(bf16[2,40,128]{2,1,0:T(8,128)(2,1)S(1)} %shard_map.109), channel_id=1, source_target_pairs={{1,0},{2,1},{3,2},{4,3},{5,4},{6,5},{7,6},{9,8},{10,9},{11,10},{12... | collective-permute-start | bytes 61448 | tf_op jit(solution)/shard_map/ppermute | solution.py:455
  116.9 6.3 %collective-permute-start.10 = (bf16[2,40,128]{2,1,0:T(8,128)(2,1)S(1)}, bf16[2,40,128]{2,1,0:T(8,128)(2,1)S(1)}, u32[]{:S(2)}, u32[]{:S(2)}) collective-permute-start(bf16[2,40,128]{2,1,0:T(8,128)(2,1)S(1)} %shard_map.109), channel_id=1, source_target_pairs={{0,1},{1,2},{2,3},{3,4},{4,5},{5,6},{6,7},{8,9},{9,10},{10,11},{11... | collective-permute-start | bytes 61448 | tf_op jit(solution)/shard_map/ppermute | solution.py:455
  130.0 7.4 %collective-permute-start.12 = (bf16[2,8,40,128]{3,2,1,0:T(8,128)(2,1)S(1)}, bf16[2,8,40,128]{3,2,1,0:T(8,128)(2,1)S(1)}, u32[]{:S(2)}, u32[]{:S(2)}) collective-permute-start(bf16[2,8,40,128]{3,2,1,0:T(8,128)(2,1)S(1)} %get-tuple-element.37), channel_id=1, source_target_pairs={{0,64},{64,128},{128,192},{192,256},{256,320},{320,384},{384,448},... | collective-permute-start | bytes 491528 | tf_op jit(solution)/shard_map/ppermute | solution.py:455
  135.1 6.6 %collective-permute-start.13 = (bf16[2,8,40,128]{3,2,1,0:T(8,128)(2,1)S(1)}, bf16[2,8,40,128]{3,2,1,0:T(8,128)(2,1)S(1)}, u32[]{:S(2)}, u32[]{:S(2)}) collective-permute-start(bf16[2,8,40,128]{3,2,1,0:T(8,128)(2,1)S(1)} %get-tuple-element.38), channel_id=1, source_target_pairs={{64,0},{128,64},{192,128},{256,192},{320,256},{384,320},{448,384},... | collective-permute-start | bytes 491528 | tf_op jit(solution)/shard_map/ppermute | solution.py:455
  (10 other events, 8.6 us)

commit v3 on v2

--- a/solution.py
+++ b/solution.py
@@ -20,13 +20,25 @@
     return lax.broadcasted_iota(jnp.int32, shape, dim)
 
 
-def call(body, out_shape, scratch=(), limit=32):
+def call(body, out_shape, scratch=(), far=None):
+    specs, limit = {}, 32
+    if far is not None:
+        limit = 58 if far[-1] else 32
+        specs["in_specs"] = [pl.BlockSpec(memory_space=pl.ANY if f else pltpu.VMEM) for f in far]
     return pl.pallas_call(
         body,
         out_shape=out_shape,
         scratch_shapes=list(scratch),
         compiler_params=pltpu.CompilerParams(vmem_limit_bytes=limit * 1024 * 1024),
+        **specs,
     )
+
+
+def start_copies(pairs, sems):
+    copies = [pltpu.make_async_copy(a, b, sems.at[i]) for i, (a, b) in enumerate(pairs)]
+    for copy in copies:
+        copy.start()
+    return copies
 
 
 def dot(a, b):
@@ -58,7 +70,11 @@
     return jnp.concatenate([main, tile], axis=0)
 
 
-def panels_body(adj, perf, owner, slot, out, sc):
+def panels_body(perf, owner, slot, adj, out, sc, *near):
+    far = len(near) > 0
+    if far:
+        near, sems = near
+        (copy,) = start_copies([(adj, near)], sems)
     own = owner[...].astype(F32)
     i0, i1 = iota((64, 64), 0), iota((64, 64), 1)
     wide = jnp.broadcast_to(own, (64, 64))
@@ -71,6 +87,9 @@
     pick = jnp.where(row_code == (iota((SLOTS, 256), 1) + 1).astype(F32), 1.0, 0.0)
     lane = iota((SLOTS, 128), 1)
     meta = jnp.where(lane == 0, slot_code, jnp.where(lane == 1, row_code, 0.0))
+    if far:
+        copy.wait()
+        adj = near
     for c in range(2):
         picked = dot(pick, adj[c].reshape(NZ * NY, NX))
         for k in range(2):
@@ -82,12 +101,14 @@
     out[...] = sc[...].astype(BF16)
 
 
-def panels(adj, perf, owner, slot):
+def panels(adj, perf, owner, slot, far=False):
+    near = [pltpu.VMEM(adj.shape, F32), pltpu.SemaphoreType.DMA((1,))] if far else []
     return call(
         panels_body,
         jax.ShapeDtypeStruct((512, 128), BF16),
-        [pltpu.VMEM((512, 128), F32)],
-    )(adj, perf, owner, slot)
+        [pltpu.VMEM((512, 128), F32), *near],
+        (False, False, False, far),
+    )(perf, owner, slot, adj)
 
 
 def owner_body(arrived, well, cross, out, sx, rq):
@@ -219,8 +240,7 @@
             )
             if ins:
                 adj, ylo, yhi, xlo, xhi = ins
-                cols = columns(xlo, xhi, c)
-                cols = pltpu.roll(cols, 128 - 8 * z0, 1) if z0 else cols
+                cols = pltpu.roll(columns(xlo, xhi, 0), -8 * (8 * c + z0) % 128, 1)
                 packed = jnp.where(lane_group() < 4, cols, packed)
                 for h in range(2):
                     tiles = y_tiles(ylo, yhi, 4 * c + z0 // 2 + h)
@@ -254,13 +274,22 @@
 
 
 def ysend_body(*refs):
-    ins, (up, down) = refs[:-2], refs[-2:]
+    high = 24
+    if len(refs) == 3:
+        ins, (up, down) = refs[:1], refs[1:]
+    else:
+        far, (up, down), ins, sems = refs[:5], refs[5:7], refs[7:12], refs[12]
+        high = 8
+        pairs = [(a.at[:, :, 0:8], b.at[:, :, 0:8]) for a, b in zip(far, ins)]
+        pairs += [(a.at[:, :, 24:32], b.at[:, :, 8:16]) for a, b in zip(far, ins)]
+        for copy in start_copies(pairs, sems):
+            copy.wait()
     low = iota((8, 128), 0) < 4
     for f, (ref, i) in enumerate(fields_of(ins)):
         for h in range(4):
             z = 2 * h
             up[4 * f + h] = jnp.where(
-                low, pltpu.roll(ref[i, z, 24:32], 4, 0), ref[i, z + 1, 24:32]
+                low, pltpu.roll(ref[i, z, high : high + 8], 4, 0), ref[i, z + 1, high : high + 8]
             ).astype(BF16)
             down[4 * f + h] = jnp.where(
                 low, ref[i, z, 0:8], pltpu.roll(ref[i, z + 1, 0:8], 4, 0)
@@ -269,7 +298,11 @@
 
 def ysend(*ins):
     shape = jax.ShapeDtypeStruct((56 if len(ins) > 1 else 8, 8, 128), BF16)
-    return call(ysend_body, (shape, shape))(*ins)
+    near = []
+    if len(ins) > 1:
+        near = [pltpu.VMEM((a.shape[0], NZ, 16, NX), F32) for a in ins]
+        near += [pltpu.SemaphoreType.DMA((2 * len(ins),))]
+    return call(ysend_body, (shape, shape), near, [len(ins) > 1] * len(ins))(*ins)
 
 
 def block_planes(ref, i, f, ylo, yhi):
@@ -285,17 +318,27 @@
 
 
 def zsend_body(*refs):
-    ins, (ylo, yhi, up, down) = refs[:-4], refs[-4:]
+    ins, (ylo, yhi, xlo, xhi, up, down) = refs[:-6], refs[-6:]
+    group = lane_group()
     for f, (ref, i) in enumerate(fields_of(ins)):
         planes = block_planes(ref, i, f, ylo, yhi)
         at, deep = z_slot(f)
         for j in range(deep):
             up[at + j] = planes[NZ - deep + j].astype(BF16)
             down[at + j] = planes[j].astype(BF16)
+    for q in range(4):
+        for out, top in ((up, True), (down, False)):
+            strip = jnp.zeros((EY, 128), F32)
+            for f in range(4 * q, min(4 * q + 4, 14)):
+                to = 4 * (f % 4)
+                came = 8 * (f % 2) + (NZ - z_slot(f)[1] if top else 0)
+                moved = pltpu.roll(columns(xlo, xhi, f // 2), 8 * (to - came) % 128, 1)
+                strip = jnp.where((group >= to) & (group < to + 4), moved, strip)
+            out[44 + q] = strip.astype(BF16)
 
 
 def zsend(*ins):
-    shape = jax.ShapeDtypeStruct((44, EY, NX), BF16)
+    shape = jax.ShapeDtypeStruct((48, EY, NX), BF16)
     return call(zsend_body, (shape, shape))(*ins)
 
 
@@ -306,60 +349,57 @@
     return low + block_planes(ref, i, f, ylo, yhi) + high
 
 
+def join_strips(low, mid, high):
+    group = lane_group()
+    return jnp.where(group < 4, low, jnp.where(group < 12, mid, high))
+
+
+def block_strip(xlo, xhi, f):
+    return pltpu.roll(columns(xlo, xhi, f // 2), 8 * (4 - 8 * (f % 2)) % 128, 1)
+
+
+def field_strip(f, xlo, xhi, zlo, zhi):
+    deep, at = z_slot(f)[1], 4 * (f % 4)
+    low = pltpu.roll(zlo[44 + f // 4].astype(F32), 8 * (4 - deep - at) % 128, 1)
+    high = pltpu.roll(zhi[44 + f // 4].astype(F32), 8 * (12 - at) % 128, 1)
+    return join_strips(low, block_strip(xlo, xhi, f), high)
+
+
 def xsend_body(*refs):
-    if len(refs) == 4:
-        adj, ylo, yhi, out = refs
-        for c in range(2):
-            strip = jnp.zeros((EY, 128), F32)
-            for z, plane in enumerate(block_planes(adj, c, c, ylo, yhi)):
-                strip = to_strip(plane, z, strip)
-            out[c] = strip.astype(BF16)
-        return
-    ins, (ylo, yhi, zlo, zhi, out) = refs[:-5], refs[-5:]
+    ins, (ylo, yhi, out) = refs[:-3], refs[-3:]
+    strip = None
     for f, (ref, i) in enumerate(fields_of(ins)):
-        strip = jnp.zeros((EY, 128), F32)
-        for z, plane in enumerate(field_planes(ref, i, f, ylo, yhi, zlo, zhi)):
-            strip = to_strip(plane, z + (f >= 2), strip)
-        out[f] = strip.astype(BF16)
+        strip = strip if f % 2 else jnp.zeros((EY, 128), F32)
+        for z, plane in enumerate(block_planes(ref, i, f, ylo, yhi)):
+            strip = to_strip(plane, z + 8 * (f % 2), strip)
+        if f % 2:
+            out[f // 2] = strip.astype(BF16)
 
 
 def xsend(*ins):
-    fields = 14 if len(ins) > 3 else 2
-    return call(xsend_body, jax.ShapeDtypeStruct((fields, EY, 128), BF16))(*ins)
+    return call(xsend_body, jax.ShapeDtypeStruct((7 if len(ins) > 3 else 1, EY, 128), BF16))(*ins)
 
 
 def sweeps_body(*refs):
-    ins, ylo, yhi, zlo, zhi, xlo, xhi = refs[:5], *refs[5:11]
+    ins, ylo, yhi, xlo, xhi, zlo, zhi = refs[:5], *refs[5:11]
     out, field, fstrip, buf0, buf1, overs, rhs, rstrip = refs[-8:]
     ws, wx, wlo, whi = refs[-12:-8]
     later = refs[11:-12]
     bufs = (buf0, buf1)
     strips = []
     skip = 4 if later else 0
-    group = lane_group()
     lane = iota((EY, 128), 1)
     column = jnp.bitwise_and(lane, 7)
 
     for c in range(2):
-        ends = [r[c, skip + 3].astype(F32) for r in (wlo, whi)]
         if later:
-            yl, yh, xl, xh = later
             planes = [wlo[c, j].astype(F32) for j in range(4)]
-            planes += block_planes(ins[0], c, c, yl, yh)
+            planes += block_planes(ins[0], c, c, *later[:2])
             planes += [whi[c, j].astype(F32) for j in range(4)]
-            strip = pltpu.roll(columns(xl, xh, c), 32, 1)
-            strip = jnp.where(group < 4, ends[0], strip)
-            strip = jnp.where(group >= 12, pltpu.roll(ends[1], 96, 1), strip)
         else:
             planes = field_planes(ins[0], c, c, ylo, yhi, zlo, zhi)
-            strip = columns(xlo, xhi, c)
         for z, plane in enumerate(planes):
             buf0[c, z] = plane
-        strips.append(strip)
-        side = wx[c]
-        side = jnp.where(group < 4, pltpu.roll(ends[0], (8 - 8 * skip) % 128, 1), side)
-        side = jnp.where(group >= 12, pltpu.roll(ends[1], 96 - 8 * skip, 1), side)
-        rstrip[c] = side + columns(xlo, xhi, 12 + c)
         for e, plane in enumerate(field_planes(ins[4], c, 12 + c, ylo, yhi, zlo, zhi)):
             if e < 3:
                 extra = wlo[c, skip + e].astype(F32)
@@ -371,7 +411,19 @@
     for n, (ref, i) in enumerate(fields_of(ins)[2:12]):
         for e, plane in enumerate(field_planes(ref, i, n + 2, ylo, yhi, zlo, zhi)):
             field[n, e] = plane
-        fstrip[n] = columns(xlo, xhi, n + 2)
+    for n in range(10):
+        fstrip[n] = field_strip(n + 2, xlo, xhi, zlo, zhi)
+    for c in range(2):
+        ends = [r[c, skip + 3].astype(F32) for r in (wlo, whi)]
+        if later:
+            strip = join_strips(ends[0], block_strip(*later[2:], c), pltpu.roll(ends[1], 96, 1))
+        else:
+            strip = field_strip(c, xlo, xhi, zlo, zhi)
+        strips.append(strip)
+        side = join_strips(
+            pltpu.roll(ends[0], (8 - 8 * skip) % 128, 1), wx[c], pltpu.roll(ends[1], 96 - 8 * skip, 1)
+        )
+        rstrip[c] = side + field_strip(12 + c, xlo, xhi, zlo, zhi)
 
     def mix(co, inflow):
         return co(6) * inflow[0] + co(8) * inflow[1], co(9) * inflow[0] + co(7) * inflow[1]
@@ -474,12 +526,12 @@
     cross_mats = cross_block.reshape(cross_block.shape[3:])
     fields = (couple, diag_inverse, cross_inverse, source)
     start = (adjoint_start, *fields)
-    sent = panels(adjoint_start, perf, owner, slot)
+    sent = panels(adjoint_start, perf, owner, slot, far=True)
     arrived = lax.all_to_all(sent, ("gy", "gx"), split_axis=0, concat_axis=0, tiled=True)
     ylo, yhi = exchange(*ysend(*start), "gy")
-    zlo, zhi = exchange(*zsend(*start, ylo, yhi), "gz")
-    packed = xsend(*start, ylo, yhi, zlo, zhi)
-    kept = (*fields, ylo, yhi, zlo, zhi, *exchange(packed, packed, "gx"))
+    packed = xsend(*start, ylo, yhi)
+    halo = (ylo, yhi, *exchange(packed, packed, "gx"))
+    kept = (*fields, *halo, *exchange(*zsend(*start, *halo), "gz"))
     answers = owner_work(arrived, well, cross_mats)
     returned = lax.all_to_all(answers, ("gy", "gx"), split_axis=0, concat_axis=0, tiled=True)
     ws, wx, up, down = place(returned)

time: 147 us -> 141 us (0.959)
  local copies, waits for them, and re-layouts: 7.31 us -> 0.74 us
  waiting for transfers between devices: 35.5 us -> 31.6 us
  Pallas kernels: 16.2 us -> 19 us
  starting transfers between devices: 86.4 us -> 88.8 us
    unnamed x48 -> x22, local copies, waits for them, and re-layouts: 7.31 us -> 0.74 us
    ppermute x14, waiting for transfers between devices: 21.4 us -> 16.3 us  [exchange(): return (lax.ppermute(up, axis, forward), lax.ppermute(down, axis, backward))]
    all_to_all x2, starting transfers between devices: 28.8 us -> 31.7 us  [per_device(): lax.all_to_all(sent, ('gy', 'gx'), split_axis=0, concat_axis=0, tiled=True)]
    pallas_call x2, Pallas kernels: 2.04 us -> 3.54 us  [panels(): call(panels_body, jax.ShapeDtypeStruct((512, 128), BF16), [pltpu.VMEM((51...]
  transfers between devices with their start and end apart: 18 -> 18, of which waited for: 10 -> 11; matrix products, arithmetic and copies ran while one was open for 0% -> 0% of each run, Pallas kernels for 3% -> 4%
where the time goes in v3:
time: 141 us
  starting transfers between devices  88.8 us (63%)
  waiting for transfers between devices  31.6 us (22%)
  Pallas kernels  19 us (13%)
    ppermute x14, starting transfers between devices, exchange(): return (lax.ppermute(up, axis, forward), lax.ppermute(down, axis, backward))  39.2 us
    all_to_all x2, starting transfers between devices, per_device(): lax.all_to_all(sent, ('gy', 'gx'), split_axis=0, concat_axis=0, tiled=True)  31.7 us
    all_to_all x2, starting transfers between devices, per_device(): lax.all_to_all(answers, ('gy', 'gx'), split_axis=0, concat_axis=0, tiled=...  17.9 us
    ppermute x14, waiting for transfers between devices, exchange(): return (lax.ppermute(up, axis, forward), lax.ppermute(down, axis, backward))  16.3 us
    all_to_all x2, waiting for transfers between devices, per_device(): lax.all_to_all(sent, ('gy', 'gx'), split_axis=0, concat_axis=0, tiled=True)  9 us
    pallas_call x2, Pallas kernels, sweeps(): call(sweeps_body, jax.ShapeDtypeStruct((2, NZ, NY, NX), F32), [pltpu.VMEM...  8 us
    all_to_all x2, waiting for transfers between devices, per_device(): lax.all_to_all(answers, ('gy', 'gx'), split_axis=0, concat_axis=0, tiled=...  6.32 us
    pallas_call x2, Pallas kernels, panels(): call(panels_body, jax.ShapeDtypeStruct((512, 128), BF16), [pltpu.VMEM((51...  3.54 us
  transfers between devices with their start and end apart: 18, of which 11 were waited for; matrix products, arithmetic and copies ran while one was open for 0% of the time, Pallas kernels for 4%

profile of v3, /device:TPU:1, one launch (start us, length us, event | category | flops | bytes accessed | tf_op | source)
XLA Modules:
  0.0 140.5 jit_solution(14492866499433988685)
XLA Ops:
  0.0 2.5 %shard_map.103 = bf16[512,128]{1,0:T(8,128)(2,1)} custom-call(s32[1,64]{1,0:T(1,128)} %bitcast.15, s32[1,64]{1,0:T(1,128)} %bitcast.17, s32[1,64]{1,0:T(1,128)} %bitcast.19, f32[2,8,32,128]{3,2,1,0:T(8,128)} %refs_0_.7), custom_call_target="tpu_custom_call" | custom-call | tf_op jit(solution)/shard_map/pallas_call | solution.py:106
  2.5 17.1 %all-to-all-start = ((bf16[64,8,128]{2,1,0:T(8,128)(2,1)}), bf16[64,8,128]{2,1,0:T(8,128)(2,1)S(1)}, u32[]{:S(2)}, u32[]{:S(2)}) async-start(bf16[64,8,128]{2,1,0:T(8,128)(2,1)} %bitcast.21), calls=%async_computation | async-start | bytes 262144 | tf_op jit(solution)/shard_map/all_to_all | solution.py:530
  19.7 2.1 %shard_map.100 = (bf16[56,8,128]{2,1,0:T(8,128)(2,1)}, bf16[56,8,128]{2,1,0:T(8,128)(2,1)}) custom-call(f32[2,8,32,128]{3,2,1,0:T(8,128)} %refs_0_.7, f32[6,8,32,128]{3,2,1,0:T(8,128)} %refs_1_.9, f32[2,8,32,128]{3,2,1,0:T(8,128)} %refs_2_.9, f32[2,8,32,128]{3,2,1,0:T(8,128)} %refs_3_.9, f32[2,8,32,128]{3,2,1,0:T(8,128)} %refs_4_.9), custom_call_target="tpu_custom_call" | custom-call | tf_op jit(solution)/shard_map/pallas_call | solution.py:305
  21.8 2.9 %collective-permute-start = (bf16[56,8,128]{2,1,0:T(8,128)(2,1)}, bf16[56,8,128]{2,1,0:T(8,128)(2,1)S(1)}, u32[]{:S(2)}, u32[]{:S(2)}) collective-permute-start(bf16[56,8,128]{2,1,0:T(8,128)(2,1)} %get-tuple-element.22), channel_id=1, source_target_pairs={{0,8},{8,16},{16,24},{24,32},{32,40},{40,48},{48,56},{1,9},{9,17},... | collective-permute-start | bytes 344072 | tf_op jit(solution)/shard_map/ppermute | solution.py:507
  24.8 1.3 collective-permute-start.1
  26.1 5.2 %all-to-all-done = bf16[64,8,128]{2,1,0:T(8,128)(2,1)S(1)} async-done(((bf16[64,8,128]{2,1,0:T(8,128)(2,1)}), bf16[64,8,128]{2,1,0:T(8,128)(2,1)S(1)}, u32[]{:S(2)}, u32[]{:S(2)}) %all-to-all-start) | async-done | bytes 131104 | tf_op jit(solution)/shard_map/all_to_all | solution.py:530
  32.9 9.4 %all-to-all-start.1 = ((bf16[64,16,128]{2,1,0:T(8,128)(2,1)}), bf16[64,16,128]{2,1,0:T(8,128)(2,1)S(1)}, u32[]{:S(2)}, u32[]{:S(2)}) async-start(bf16[64,16,128]{2,1,0:T(8,128)(2,1)} %copy-done.7), calls=%async_computation.1 | async-start | bytes 524288 | tf_op jit(solution)/shard_map/all_to_all | solution.py:536
  42.8 1.3 collective-permute-start.3
  44.1 4.0 %collective-permute-start.2 = (bf16[7,40,128]{2,1,0:T(8,128)(2,1)S(1)}, bf16[7,40,128]{2,1,0:T(8,128)(2,1)S(1)}, u32[]{:S(2)}, u32[]{:S(2)}) collective-permute-start(bf16[7,40,128]{2,1,0:T(8,128)(2,1)S(1)} %shard_map.101), channel_id=1, source_target_pairs={{0,1},{1,2},{2,3},{3,4},{4,5},{5,6},{6,7},{8,9},{9,10},{10,11},{11... | collective-permute-start | bytes 215048 | tf_op jit(solution)/shard_map/ppermute | solution.py:507
  48.1 1.5 %collective-permute-done.3.refs_8_ = bf16[7,40,128]{2,1,0:T(8,128)(2,1)S(1)} collective-permute-done((bf16[7,40,128]{2,1,0:T(8,128)(2,1)S(1)}, bf16[7,40,128]{2,1,0:T(8,128)(2,1)S(1)}, u32[]{:S(2)}, u32[]{:S(2)}) %collective-permute-start.3) | collective-permute-done | bytes 71712 | tf_op jit(solution)/shard_map/ppermute | solution.py:507
  51.1 5.7 %collective-permute-start.4 = (bf16[48,40,128]{2,1,0:T(8,128)(2,1)}, bf16[48,40,128]{2,1,0:T(8,128)(2,1)}, u32[]{:S(2)}, u32[]{:S(2)}) collective-permute-start(bf16[48,40,128]{2,1,0:T(8,128)(2,1)} %get-tuple-element.24), channel_id=1, source_target_pairs={{0,64},{64,128},{128,192},{192,256},{256,320},{320,384},{384,448},... | collective-permute-start | bytes 1474568 | tf_op jit(solution)/shard_map/ppermute | solution.py:507
  56.8 1.9 %collective-permute-start.5 = (bf16[48,40,128]{2,1,0:T(8,128)(2,1)}, bf16[48,40,128]{2,1,0:T(8,128)(2,1)}, u32[]{:S(2)}, u32[]{:S(2)}) collective-permute-start(bf16[48,40,128]{2,1,0:T(8,128)(2,1)} %get-tuple-element.25), channel_id=1, source_target_pairs={{64,0},{128,64},{192,128},{256,192},{320,256},{384,320},{448,384},... | collective-permute-start | bytes 1474568 | tf_op jit(solution)/shard_map/ppermute | solution.py:507
  59.3 3.6 %collective-permute-start.6 = (bf16[2,4,40,128]{3,2,1,0:T(8,128)(2,1)S(1)}, bf16[2,4,40,128]{3,2,1,0:T(8,128)(2,1)S(1)}, u32[]{:S(2)}, u32[]{:S(2)}) collective-permute-start(bf16[2,4,40,128]{3,2,1,0:T(8,128)(2,1)S(1)} %get-tuple-element.28), channel_id=1, source_target_pairs={{0,64},{64,128},{128,192},{192,256},{256,320},{320,384},{384,448},... | collective-permute-start | bytes 245768 | tf_op jit(solution)/shard_map/ppermute | solution.py:507
  63.0 1.9 %collective-permute-start.7 = (bf16[2,4,40,128]{3,2,1,0:T(8,128)(2,1)S(1)}, bf16[2,4,40,128]{3,2,1,0:T(8,128)(2,1)S(1)}, u32[]{:S(2)}, u32[]{:S(2)}) collective-permute-start(bf16[2,4,40,128]{3,2,1,0:T(8,128)(2,1)S(1)} %get-tuple-element.29), channel_id=1, source_target_pairs={{64,0},{128,64},{192,128},{256,192},{320,256},{384,320},{448,384},... | collective-permute-start | bytes 245768 | tf_op jit(solution)/shard_map/ppermute | solution.py:507
  64.9 2.3 %collective-permute-done.5.refs_10_ = bf16[48,40,128]{2,1,0:T(8,128)(2,1)} collective-permute-done((bf16[48,40,128]{2,1,0:T(8,128)(2,1)}, bf16[48,40,128]{2,1,0:T(8,128)(2,1)}, u32[]{:S(2)}, u32[]{:S(2)}) %collective-permute-start.5) | collective-permute-done | bytes 491552 | tf_op jit(solution)/shard_map/ppermute | solution.py:507
  67.3 1.5 %collective-permute-done.7.refs_14_ = bf16[2,4,40,128]{3,2,1,0:T(8,128)(2,1)S(1)} collective-permute-done((bf16[2,4,40,128]{3,2,1,0:T(8,128)(2,1)S(1)}, bf16[2,4,40,128]{3,2,1,0:T(8,128)(2,1)S(1)}, u32[]{:S(2)}, u32[]{:S(2)}) %collective-permute-start.7) | collective-permute-done | bytes 81952 | tf_op jit(solution)/shard_map/ppermute | solution.py:507
  68.7 3.7 %shard_map.106.adj.refs_0_ = f32[2,8,32,128]{3,2,1,0:T(8,128)S(1)} custom-call(f32[2,8,32,128]{3,2,1,0:T(8,128)S(1)} %copy-done.1, f32[6,8,32,128]{3,2,1,0:T(8,128)S(1)} %copy-done, f32[2,8,32,128]{3,2,1,0:T(8,128)S(1)} %copy-done.2, f32[2,8,32,128]{3,2,1,0:T(8,128)S(1)} %copy-done.3, f32[2,8,32,128]{3,2,1,0:T(8,128)S(1)} %copy-done.4, ...), custom_call_target="tpu_custom_call" | custom-call | tf_op jit(solution)/shard_map/pallas_call | solution.py:488
  73.5 14.5 %all-to-all-start.2 = ((bf16[64,8,128]{2,1,0:T(8,128)(2,1)}), bf16[64,8,128]{2,1,0:T(8,128)(2,1)S(1)}, u32[]{:S(2)}, u32[]{:S(2)}) async-start(bf16[64,8,128]{2,1,0:T(8,128)(2,1)} %bitcast.7), calls=%async_computation.2 | async-start | bytes 262144 | tf_op jit(solution)/shard_map/all_to_all | solution.py:542
  88.0 2.9 %collective-permute-start.8 = (bf16[8,8,128]{2,1,0:T(8,128)(2,1)S(1)}, bf16[8,8,128]{2,1,0:T(8,128)(2,1)S(1)}, u32[]{:S(2)}, u32[]{:S(2)}) collective-permute-start(bf16[8,8,128]{2,1,0:T(8,128)(2,1)S(1)} %get-tuple-element.30), channel_id=1, source_target_pairs={{0,8},{8,16},{16,24},{24,32},{32,40},{40,48},{48,56},{1,9},{9,17},... | collective-permute-start | bytes 49160 | tf_op jit(solution)/shard_map/ppermute | solution.py:507
  90.9 1.3 collective-permute-start.9
  92.3 3.5 %collective-permute-done.9.refs_2_.refs_12_ = bf16[8,8,128]{2,1,0:T(8,128)(2,1)S(1)} collective-permute-done((bf16[8,8,128]{2,1,0:T(8,128)(2,1)S(1)}, bf16[8,8,128]{2,1,0:T(8,128)(2,1)S(1)}, u32[]{:S(2)}, u32[]{:S(2)}) %collective-permute-start.9) | collective-permute-done | bytes 16416 | tf_op jit(solution)/shard_map/ppermute | solution.py:507
  95.8 3.8 %all-to-all-done.2 = bf16[64,8,128]{2,1,0:T(8,128)(2,1)S(1)} async-done(((bf16[64,8,128]{2,1,0:T(8,128)(2,1)}), bf16[64,8,128]{2,1,0:T(8,128)(2,1)S(1)}, u32[]{:S(2)}, u32[]{:S(2)}) %all-to-all-start.2) | async-done | bytes 131104 | tf_op jit(solution)/shard_map/all_to_all | solution.py:542
  99.6 1.7 %shard_map.110 = bf16[64,16,128]{2,1,0:T(8,128)(2,1)} custom-call(bf16[512,128]{1,0:T(8,128)(2,1)S(1)} %bitcast.13, bf16[4,256,256]{2,1,0:T(8,128)(2,1)S(1)} %bitcast.10, bf16[4,256,256]{2,1,0:T(8,128)(2,1)S(1)} %bitcast.12), custom_call_target="tpu_custom_call" | custom-call | tf_op jit(solution)/shard_map/pallas_call | solution.py:173
  101.3 8.5 %all-to-all-start.3 = ((bf16[64,16,128]{2,1,0:T(8,128)(2,1)}), bf16[64,16,128]{2,1,0:T(8,128)(2,1)S(1)}, u32[]{:S(2)}, u32[]{:S(2)}) async-start(bf16[64,16,128]{2,1,0:T(8,128)(2,1)} %shard_map.110), calls=%async_computation.3 | async-start | bytes 524288 | tf_op jit(solution)/shard_map/all_to_all | solution.py:547
  109.8 1.3 collective-permute-start.11
  111.2 4.0 %collective-permute-start.10 = (bf16[1,40,128]{2,1,0:T(8,128)(2,1)S(1)}, bf16[1,40,128]{2,1,0:T(8,128)(2,1)S(1)}, u32[]{:S(2)}, u32[]{:S(2)}) collective-permute-start(bf16[1,40,128]{2,1,0:T(8,128)(2,1)S(1)} %shard_map.109), channel_id=1, source_target_pairs={{0,1},{1,2},{2,3},{3,4},{4,5},{5,6},{6,7},{8,9},{9,10},{10,11},{11... | collective-permute-start | bytes 30728 | tf_op jit(solution)/shard_map/ppermute | solution.py:507
  115.1 2.4 %collective-permute-done.11.refs_4_.refs_14_ = bf16[1,40,128]{2,1,0:T(8,128)(2,1)S(1)} collective-permute-done((bf16[1,40,128]{2,1,0:T(8,128)(2,1)S(1)}, bf16[1,40,128]{2,1,0:T(8,128)(2,1)S(1)}, u32[]{:S(2)}, u32[]{:S(2)}) %collective-permute-start.11) | collective-permute-done | bytes 10272 | tf_op jit(solution)/shard_map/ppermute | solution.py:507
  117.5 6.3 %all-to-all-done.3.arrived = bf16[64,16,128]{2,1,0:T(8,128)(2,1)S(1)} async-done(((bf16[64,16,128]{2,1,0:T(8,128)(2,1)}), bf16[64,16,128]{2,1,0:T(8,128)(2,1)S(1)}, u32[]{:S(2)}, u32[]{:S(2)}) %all-to-all-start.3) | async-done | bytes 262176 | tf_op jit(solution)/shard_map/all_to_all | solution.py:547
  124.4 5.1 %collective-permute-start.12 = (bf16[2,8,40,128]{3,2,1,0:T(8,128)(2,1)S(1)}, bf16[2,8,40,128]{3,2,1,0:T(8,128)(2,1)S(1)}, u32[]{:S(2)}, u32[]{:S(2)}) collective-permute-start(bf16[2,8,40,128]{3,2,1,0:T(8,128)(2,1)S(1)} %get-tuple-element.37), channel_id=1, source_target_pairs={{0,64},{64,128},{128,192},{192,256},{256,320},{320,384},{384,448},... | collective-permute-start | bytes 491528 | tf_op jit(solution)/shard_map/ppermute | solution.py:507
  129.5 1.9 %collective-permute-start.13 = (bf16[2,8,40,128]{3,2,1,0:T(8,128)(2,1)S(1)}, bf16[2,8,40,128]{3,2,1,0:T(8,128)(2,1)S(1)}, u32[]{:S(2)}, u32[]{:S(2)}) collective-permute-start(bf16[2,8,40,128]{3,2,1,0:T(8,128)(2,1)S(1)} %get-tuple-element.38), channel_id=1, source_target_pairs={{64,0},{128,64},{192,128},{256,192},{320,256},{384,320},{448,384},... | collective-permute-start | bytes 491528 | tf_op jit(solution)/shard_map/ppermute | solution.py:507
  131.8 4.4 %collective-permute-done.13.refs_18_ = bf16[2,8,40,128]{3,2,1,0:T(8,128)(2,1)S(1)} collective-permute-done((bf16[2,8,40,128]{3,2,1,0:T(8,128)(2,1)S(1)}, bf16[2,8,40,128]{3,2,1,0:T(8,128)(2,1)S(1)}, u32[]{:S(2)}, u32[]{:S(2)}) %collective-permute-start.13) | collective-permute-done | bytes 163872 | tf_op jit(solution)/shard_map/ppermute | solution.py:507
  136.2 4.3 %shard_map.112 = f32[2,8,32,128]{3,2,1,0:T(8,128)} custom-call(f32[2,8,32,128]{3,2,1,0:T(8,128)S(1)} %shard_map.106.adj.refs_0_, f32[6,8,32,128]{3,2,1,0:T(8,128)S(1)} %copy-done, f32[2,8,32,128]{3,2,1,0:T(8,128)S(1)} %copy-done.2, f32[2,8,32,128]{3,2,1,0:T(8,128)S(1)} %copy-done.3, f32[2,8,32,128]{3,2,1,0:T(8,128)S(1)} %copy-done.4, ...), custom_call_target="tpu_custom_call" | custom-call | tf_op jit(solution)/shard_map/pallas_call | solution.py:488
  (39 shorter events, 6.2 us)
Async XLA Ops:
  2.5 28.7 %all-to-all-start = ((bf16[64,8,128]{2,1,0:T(8,128)(2,1)}), bf16[64,8,128]{2,1,0:T(8,128)(2,1)S(1)}, u32[]{:S(2)}, u32[]{:S(2)}) async-start(bf16[64,8,128]{2,1,0:T(8,128)(2,1)} %bitcast.21), calls=%async_computation | async-start | bytes 262144 | tf_op jit(solution)/shard_map/all_to_all | solution.py:530
  19.7 11.5 %copy-start.5 = (bf16[1,1,1,4,256,256]{5,4,3,2,1,0:T(8,128)(2,1)S(1)}, bf16[1,1,1,4,256,256]{5,4,3,2,1,0:T(8,128)(2,1)}, u32[]{:S(2)}) copy-start(bf16[1,1,1,4,256,256]{5,4,3,2,1,0:T(8,128)(2,1)} %param.18) | copy-start | bytes 1572868
  19.7 11.5 %copy-start.6 = (bf16[1,1,1,4,256,256]{5,4,3,2,1,0:T(8,128)(2,1)S(1)}, bf16[1,1,1,4,256,256]{5,4,3,2,1,0:T(8,128)(2,1)}, u32[]{:S(2)}) copy-start(bf16[1,1,1,4,256,256]{5,4,3,2,1,0:T(8,128)(2,1)} %param.19) | copy-start | bytes 1572868
  21.8 20.5 %collective-permute-start = (bf16[56,8,128]{2,1,0:T(8,128)(2,1)}, bf16[56,8,128]{2,1,0:T(8,128)(2,1)S(1)}, u32[]{:S(2)}, u32[]{:S(2)}) collective-permute-start(bf16[56,8,128]{2,1,0:T(8,128)(2,1)} %get-tuple-element.22), channel_id=1, source_target_pairs={{0,8},{8,16},{16,24},{24,32},{32,40},{40,48},{48,56},{1,9},{9,17},... | collective-permute-start | bytes 344072 | tf_op jit(solution)/shard_map/ppermute | solution.py:507
  24.8 17.6 %collective-permute-start.1 = (bf16[56,8,128]{2,1,0:T(8,128)(2,1)}, bf16[56,8,128]{2,1,0:T(8,128)(2,1)S(1)}, u32[]{:S(2)}, u32[]{:S(2)}) collective-permute-start(bf16[56,8,128]{2,1,0:T(8,128)(2,1)} %get-tuple-element.23), channel_id=1, source_target_pairs={{8,0},{16,8},{24,16},{32,24},{40,32},{48,40},{56,48},{9,1},{17,9},... | collective-permute-start | bytes 344072 | tf_op jit(solution)/shard_map/ppermute | solution.py:507
  31.2 11.1 %copy-start = (f32[6,8,32,128]{3,2,1,0:T(8,128)S(1)}, f32[6,8,32,128]{3,2,1,0:T(8,128)}, u32[]{:S(2)}) copy-start(f32[6,8,32,128]{3,2,1,0:T(8,128)} %refs_1_.9) | copy-start | bytes 2359300
  31.2 11.1 %copy-start.3 = (f32[2,8,32,128]{3,2,1,0:T(8,128)S(1)}, f32[2,8,32,128]{3,2,1,0:T(8,128)}, u32[]{:S(2)}) copy-start(f32[2,8,32,128]{3,2,1,0:T(8,128)} %refs_3_.9) | copy-start | bytes 786436
  31.2 11.2 %copy-start.4 = (f32[2,8,32,128]{3,2,1,0:T(8,128)S(1)}, f32[2,8,32,128]{3,2,1,0:T(8,128)}, u32[]{:S(2)}) copy-start(f32[2,8,32,128]{3,2,1,0:T(8,128)} %refs_4_.9) | copy-start | bytes 786436
  32.2 0.7 copy-start.7
  32.9 9.5 %copy-start.1 = (f32[2,8,32,128]{3,2,1,0:T(8,128)S(1)}, f32[2,8,32,128]{3,2,1,0:T(8,128)}, u32[]{:S(2)}) copy-start(f32[2,8,32,128]{3,2,1,0:T(8,128)} %refs_0_.7) | copy-start | bytes 786436
  32.9 9.5 %copy-start.2 = (f32[2,8,32,128]{3,2,1,0:T(8,128)S(1)}, f32[2,8,32,128]{3,2,1,0:T(8,128)}, u32[]{:S(2)}) copy-start(f32[2,8,32,128]{3,2,1,0:T(8,128)} %refs_2_.9) | copy-start | bytes 786436
  32.9 25.8 %all-to-all-start.1 = ((bf16[64,16,128]{2,1,0:T(8,128)(2,1)}), bf16[64,16,128]{2,1,0:T(8,128)(2,1)S(1)}, u32[]{:S(2)}, u32[]{:S(2)}) async-start(bf16[64,16,128]{2,1,0:T(8,128)(2,1)} %copy-done.7), calls=%async_computation.1 | async-start | bytes 524288 | tf_op jit(solution)/shard_map/all_to_all | solution.py:536
  42.8 6.8 %collective-permute-start.3 = (bf16[7,40,128]{2,1,0:T(8,128)(2,1)S(1)}, bf16[7,40,128]{2,1,0:T(8,128)(2,1)S(1)}, u32[]{:S(2)}, u32[]{:S(2)}) collective-permute-start(bf16[7,40,128]{2,1,0:T(8,128)(2,1)S(1)} %shard_map.101), channel_id=1, source_target_pairs={{1,0},{2,1},{3,2},{4,3},{5,4},{6,5},{7,6},{9,8},{10,9},{11,10},{12... | collective-permute-start | bytes 215048 | tf_op jit(solution)/shard_map/ppermute | solution.py:507
  44.1 5.9 %collective-permute-start.2 = (bf16[7,40,128]{2,1,0:T(8,128)(2,1)S(1)}, bf16[7,40,128]{2,1,0:T(8,128)(2,1)S(1)}, u32[]{:S(2)}, u32[]{:S(2)}) collective-permute-start(bf16[7,40,128]{2,1,0:T(8,128)(2,1)S(1)} %shard_map.101), channel_id=1, source_target_pairs={{0,1},{1,2},{2,3},{3,4},{4,5},{5,6},{6,7},{8,9},{9,10},{10,11},{11... | collective-permute-start | bytes 215048 | tf_op jit(solution)/shard_map/ppermute | solution.py:507
  51.1 13.8 %collective-permute-start.4 = (bf16[48,40,128]{2,1,0:T(8,128)(2,1)}, bf16[48,40,128]{2,1,0:T(8,128)(2,1)}, u32[]{:S(2)}, u32[]{:S(2)}) collective-permute-start(bf16[48,40,128]{2,1,0:T(8,128)(2,1)} %get-tuple-element.24), channel_id=1, source_target_pairs={{0,64},{64,128},{128,192},{192,256},{256,320},{320,384},{384,448},... | collective-permute-start | bytes 1474568 | tf_op jit(solution)/shard_map/ppermute | solution.py:507
  56.8 10.5 %collective-permute-start.5 = (bf16[48,40,128]{2,1,0:T(8,128)(2,1)}, bf16[48,40,128]{2,1,0:T(8,128)(2,1)}, u32[]{:S(2)}, u32[]{:S(2)}) collective-permute-start(bf16[48,40,128]{2,1,0:T(8,128)(2,1)} %get-tuple-element.25), channel_id=1, source_target_pairs={{64,0},{128,64},{192,128},{256,192},{320,256},{384,320},{448,384},... | collective-permute-start | bytes 1474568 | tf_op jit(solution)/shard_map/ppermute | solution.py:507
  59.3 7.9 %collective-permute-start.6 = (bf16[2,4,40,128]{3,2,1,0:T(8,128)(2,1)S(1)}, bf16[2,4,40,128]{3,2,1,0:T(8,128)(2,1)S(1)}, u32[]{:S(2)}, u32[]{:S(2)}) collective-permute-start(bf16[2,4,40,128]{3,2,1,0:T(8,128)(2,1)S(1)} %get-tuple-element.28), channel_id=1, source_target_pairs={{0,64},{64,128},{128,192},{192,256},{256,320},{320,384},{384,448},... | collective-permute-start | bytes 245768 | tf_op jit(solution)/shard_map/ppermute | solution.py:507
  63.0 5.8 %collective-permute-start.7 = (bf16[2,4,40,128]{3,2,1,0:T(8,128)(2,1)S(1)}, bf16[2,4,40,128]{3,2,1,0:T(8,128)(2,1)S(1)}, u32[]{:S(2)}, u32[]{:S(2)}) collective-permute-start(bf16[2,4,40,128]{3,2,1,0:T(8,128)(2,1)S(1)} %get-tuple-element.29), channel_id=1, source_target_pairs={{64,0},{128,64},{192,128},{256,192},{320,256},{384,320},{448,384},... | collective-permute-start | bytes 245768 | tf_op jit(solution)/shard_map/ppermute | solution.py:507
  68.7 3.7 %copy-start.8 = (s32[1,1,1,64]{3,2,1,0:T(1,128)S(1)}, s32[1,1,1,64]{3,2,1,0:T(1,128)}, u32[]{:S(2)}) copy-start(s32[1,1,1,64]{3,2,1,0:T(1,128)} %param.15) | copy-start | bytes 772
  68.7 3.7 %copy-start.9 = (s32[1,1,1,64,1]{3,4,2,1,0:T(1,128)S(1)}, s32[1,1,1,64,1]{3,4,2,1,0:T(1,128)}, u32[]{:S(2)}) copy-start(s32[1,1,1,64,1]{3,4,2,1,0:T(1,128)} %param.16) | copy-start | bytes 772
  68.7 3.7 %copy-start.10 = (s32[1,1,1,64]{3,2,1,0:T(1,128)S(1)}, s32[1,1,1,64]{3,2,1,0:T(1,128)}, u32[]{:S(2)}) copy-start(s32[1,1,1,64]{3,2,1,0:T(1,128)} %param.17) | copy-start | bytes 772
  73.5 26.1 %all-to-all-start.2 = ((bf16[64,8,128]{2,1,0:T(8,128)(2,1)}), bf16[64,8,128]{2,1,0:T(8,128)(2,1)S(1)}, u32[]{:S(2)}, u32[]{:S(2)}) async-start(bf16[64,8,128]{2,1,0:T(8,128)(2,1)} %bitcast.7), calls=%async_computation.2 | async-start | bytes 262144 | tf_op jit(solution)/shard_map/all_to_all | solution.py:542
  88.0 4.2 %collective-permute-start.8 = (bf16[8,8,128]{2,1,0:T(8,128)(2,1)S(1)}, bf16[8,8,128]{2,1,0:T(8,128)(2,1)S(1)}, u32[]{:S(2)}, u32[]{:S(2)}) collective-permute-start(bf16[8,8,128]{2,1,0:T(8,128)(2,1)S(1)} %get-tuple-element.30), channel_id=1, source_target_pairs={{0,8},{8,16},{16,24},{24,32},{32,40},{40,48},{48,56},{1,9},{9,17},... | collective-permute-start | bytes 49160 | tf_op jit(solution)/shard_map/ppermute | solution.py:507
  90.9 4.8 %collective-permute-start.9 = (bf16[8,8,128]{2,1,0:T(8,128)(2,1)S(1)}, bf16[8,8,128]{2,1,0:T(8,128)(2,1)S(1)}, u32[]{:S(2)}, u32[]{:S(2)}) collective-permute-start(bf16[8,8,128]{2,1,0:T(8,128)(2,1)S(1)} %get-tuple-element.31), channel_id=1, source_target_pairs={{8,0},{16,8},{24,16},{32,24},{40,32},{48,40},{56,48},{9,1},{17,9},... | collective-permute-start | bytes 49160 | tf_op jit(solution)/shard_map/ppermute | solution.py:507
  101.3 22.6 %all-to-all-start.3 = ((bf16[64,16,128]{2,1,0:T(8,128)(2,1)}), bf16[64,16,128]{2,1,0:T(8,128)(2,1)S(1)}, u32[]{:S(2)}, u32[]{:S(2)}) async-start(bf16[64,16,128]{2,1,0:T(8,128)(2,1)} %shard_map.110), calls=%async_computation.3 | async-start | bytes 524288 | tf_op jit(solution)/shard_map/all_to_all | solution.py:547
  109.8 7.7 %collective-permute-start.11 = (bf16[1,40,128]{2,1,0:T(8,128)(2,1)S(1)}, bf16[1,40,128]{2,1,0:T(8,128)(2,1)S(1)}, u32[]{:S(2)}, u32[]{:S(2)}) collective-permute-start(bf16[1,40,128]{2,1,0:T(8,128)(2,1)S(1)} %shard_map.109), channel_id=1, source_target_pairs={{1,0},{2,1},{3,2},{4,3},{5,4},{6,5},{7,6},{9,8},{10,9},{11,10},{12... | collective-permute-start | bytes 30728 | tf_op jit(solution)/shard_map/ppermute | solution.py:507
  111.2 6.4 %collective-permute-start.10 = (bf16[1,40,128]{2,1,0:T(8,128)(2,1)S(1)}, bf16[1,40,128]{2,1,0:T(8,128)(2,1)S(1)}, u32[]{:S(2)}, u32[]{:S(2)}) collective-permute-start(bf16[1,40,128]{2,1,0:T(8,128)(2,1)S(1)} %shard_map.109), channel_id=1, source_target_pairs={{0,1},{1,2},{2,3},{3,4},{4,5},{5,6},{6,7},{8,9},{9,10},{10,11},{11... | collective-permute-start | bytes 30728 | tf_op jit(solution)/shard_map/ppermute | solution.py:507
  124.4 7.4 %collective-permute-start.12 = (bf16[2,8,40,128]{3,2,1,0:T(8,128)(2,1)S(1)}, bf16[2,8,40,128]{3,2,1,0:T(8,128)(2,1)S(1)}, u32[]{:S(2)}, u32[]{:S(2)}) collective-permute-start(bf16[2,8,40,128]{3,2,1,0:T(8,128)(2,1)S(1)} %get-tuple-element.37), channel_id=1, source_target_pairs={{0,64},{64,128},{128,192},{192,256},{256,320},{320,384},{384,448},... | collective-permute-start | bytes 491528 | tf_op jit(solution)/shard_map/ppermute | solution.py:507
  129.5 6.6 %collective-permute-start.13 = (bf16[2,8,40,128]{3,2,1,0:T(8,128)(2,1)S(1)}, bf16[2,8,40,128]{3,2,1,0:T(8,128)(2,1)S(1)}, u32[]{:S(2)}, u32[]{:S(2)}) collective-permute-start(bf16[2,8,40,128]{3,2,1,0:T(8,128)(2,1)S(1)} %get-tuple-element.38), channel_id=1, source_target_pairs={{64,0},{128,64},{192,128},{256,192},{320,256},{384,320},{448,384},... | collective-permute-start | bytes 491528 | tf_op jit(solution)/shard_map/ppermute | solution.py:507

commit v4 on v3

v4 whole, which is shorter than its diff:
```python
import functools

import jax
import jax.numpy as jnp
from jax import lax
from jax.experimental import pallas as pl
from jax.experimental.pallas import tpu as pltpu
from jax.sharding import PartitionSpec as P

SWEEPS = 4
F32 = jnp.float32
BF16 = jnp.bfloat16
NZ, NY, NX = 8, 32, 128
EZ, EY = 16, 48
OWNERS = 64
SLOTS = 128
CZ = 14


def iota(shape, dim):
    return lax.broadcasted_iota(jnp.int32, shape, dim)


def call(body, out_shape, scratch=(), far=None):
    specs, limit = {}, 32
    if far is not None:
        limit = 58 if all(far) else 32
        specs["in_specs"] = [pl.BlockSpec(memory_space=pl.ANY if f else pltpu.VMEM) for f in far]
    return pl.pallas_call(
        body,
        out_shape=out_shape,
        scratch_shapes=list(scratch),
        compiler_params=pltpu.CompilerParams(vmem_limit_bytes=limit * 1024 * 1024),
        **specs,
    )


def start_copies(pairs, sems):
    copies = [pltpu.make_async_copy(a, b, sems.at[i]) for i, (a, b) in enumerate(pairs)]
    for copy in copies:
        copy.start()
    return copies


def dot(a, b):
    return jnp.dot(a.astype(BF16), b.astype(BF16), preferred_element_type=F32)


def lane_group():
    return lax.shift_right_logical(iota((EY, 128), 1), 4)


def columns(xlo, xhi, index):
    low = jnp.bitwise_and(iota((EY, 128), 1), 15) < 8
    return jnp.where(low, xlo[index].astype(F32), xhi[index].astype(F32))


def to_strip(plane, g, strip):
    return jnp.where(lane_group() == g, pltpu.roll(plane, 16 * g + 8, 1), strip)


def swap(strip):
    return pltpu.roll(strip, 64, 1)


def by_half(low, high):
    return jnp.where(lane_group() < 4, low, high)


def tall(main, above, below):
    return jnp.concatenate([main, above, below], axis=0)


def panels_body(perf, owner, slot, adj, out, sc, *near):
    far = len(near) > 0
    if far:
        near, sems = near
        (copy,) = start_copies([(adj, near)], sems)
    own = owner[...].astype(F32)
    i0, i1 = iota((64, 64), 0), iota((64, 64), 1)
    wide = jnp.broadcast_to(own, (64, 64))
    down = jnp.sum(jnp.where(i0 == i1, wide, 0.0), axis=1, keepdims=True)
    rank = jnp.sum(jnp.where((down == wide) & (i0 < i1), 1.0, 0.0), axis=0, keepdims=True)
    dest = rank * float(OWNERS) + own
    hit = iota((SLOTS, 64), 0).astype(F32) == dest
    row_code = jnp.sum(jnp.where(hit, perf[...].astype(F32) + 1.0, 0.0), axis=1, keepdims=True)
    slot_code = jnp.sum(jnp.where(hit, slot[...].astype(F32) + 1.0, 0.0), axis=1, keepdims=True)
    pick = jnp.where(row_code == (iota((SLOTS, 256), 1) + 1).astype(F32), 1.0, 0.0)
    lane = iota((SLOTS, 128), 1)
    meta = jnp.where(lane == 0, slot_code, jnp.where(lane == 1, row_code, 0.0))
    if far:
        copy.wait()
        adj = near
    for c in range(2):
        picked = dot(pick, adj[c, :, 0:NY].reshape(NZ * NY, NX))
        for k in range(2):
            sc[pl.ds(2 * c + k, 64, stride=8), :] = picked[k * 64 : (k + 1) * 64]
    zero = jnp.zeros((64, 128), F32)
    for k in range(2):
        sc[pl.ds(4 + k, 64, stride=8), :] = meta[k * 64 : (k + 1) * 64]
        sc[pl.ds(6 + k, 64, stride=8), :] = zero
    out[...] = sc[...].astype(BF16)


def panels(adj, perf, owner, slot, far=False):
    near = [pltpu.VMEM(adj.shape, F32), pltpu.SemaphoreType.DMA((1,))] if far else []
    return call(
        panels_body,
        jax.ShapeDtypeStruct((512, 128), BF16),
        [pltpu.VMEM((512, 128), F32), *near],
        (False, False, False, far),
    )(perf, owner, slot, adj)


def owner_body(arrived, well, cross, *refs):
    out, sx, rq = refs[-3:]
    sx[...] = arrived[...].astype(F32)

    def rows(i):
        return jnp.concatenate(
            [sx[pl.ds(i, 64, stride=8), :], sx[pl.ds(i + 1, 64, stride=8), :]], axis=0
        )

    meta = rows(4)
    ident, row_code = meta[:, 0:1], meta[:, 1:2]
    panel = jnp.concatenate([rows(0), rows(2)], axis=1)
    i0, i1 = iota((SLOTS, SLOTS), 0), iota((SLOTS, SLOTS), 1)
    across = jnp.sum(jnp.where(i0 == i1, ident, 0.0), axis=0, keepdims=True)
    same = jnp.where(ident == across, 1.0, 0.0)
    totals = dot(same, panel).astype(BF16).astype(F32)
    mixed = jnp.zeros((SLOTS, 256), F32)
    for w in range(4):
        mine = ident == float(w + 1)
        mixed = mixed + dot(jnp.where(mine, panel, 0.0), well[w])
        mixed = mixed + dot(jnp.where(mine, totals, 0.0), cross[w])
    mixed = mixed.astype(BF16).astype(F32)
    tag = jnp.where(iota((SLOTS, 128), 1) == 96, row_code, 0.0)
    for k in range(2):
        part = slice(k * 64, (k + 1) * 64)
        for c in range(2):
            rq[pl.ds(2 * c + k, 64, stride=8), :] = mixed[part, c * 128 : (c + 1) * 128]
        rq[pl.ds(4 + k, 64, stride=8), :] = tag[part]
        rq[pl.ds(6 + k, 64, stride=8), :] = jnp.zeros((64, 128), F32)
    full = rq[...].reshape(64, 8, 128)
    sub, lane = iota((64, 8, 128), 1), iota((64, 8, 128), 2)

    def from_y(v, step):
        gap = jnp.zeros((8, 8, 128), F32)
        return jnp.concatenate([gap, v[:-8]] if step < 0 else [v[8:], gap], axis=0)

    def from_x(v, step):
        v = v.reshape(8, 8, 8, 128)
        gap = jnp.zeros((8, 1, 8, 128), F32)
        v = jnp.concatenate([gap, v[:, :-1]] if step < 0 else [v[:, 1:], gap], axis=1)
        return v.reshape(64, 8, 128)

    def turn(v, by):
        return pltpu.roll(v, by, 2)

    def half(v):
        return pltpu.roll(v, 4, 1)

    below, above = from_y(full, -1), from_y(full, 1)
    edge = jnp.where(lane >= 121, from_x(full, -1), jnp.where(lane < 7, from_x(full, 1), 0.0))
    edges = edge + turn(from_y(edge, -1), 32) + turn(from_y(edge, 1), 64)
    tags = jnp.where((sub >= 4) & (lane == 96), full, 0.0)
    tags = tags + turn(from_y(tags, -1), 1) + turn(from_y(tags, 1), 2)
    tags = tags + turn(from_x(tags, -1), 3) + turn(from_x(tags, 1), 6)
    first = jnp.where(sub < 4, full, half(below))
    second = jnp.where(sub < 4, above, half(jnp.where(sub < 4, edges, 0.0)) + tags)
    out[...] = jnp.concatenate([first, second], axis=1).astype(BF16)


def owner_work(arrived, well, cross, *after):
    return call(
        owner_body,
        jax.ShapeDtypeStruct((64, 16, 128), BF16),
        [pltpu.VMEM((512, 128), F32), pltpu.VMEM((512, 128), F32)],
        [False] * 3 + [True] * len(after),
    )(arrived, well, cross, *after)


def place_body(arrived, *refs):
    ins, (ws, wx, up, down, sx) = refs[:-5], refs[-5:]
    sx[...] = arrived[...].reshape(1024, 128).astype(F32)

    def rows(i):
        return jnp.concatenate(
            [sx[pl.ds(i, 64, stride=16), :], sx[pl.ds(i + 1, 64, stride=16), :]], axis=0
        )

    def both(i):
        return jnp.concatenate([rows(i), rows(i + 2)], axis=1)

    codes = rows(12).T

    def code(n):
        return codes[96 + n : 97 + n, :]

    def place(want, n, values):
        return dot(jnp.where(want == code(n), 1.0, 0.0), values)

    lane = jnp.bitwise_and(iota((SLOTS, 256), 1), 127)

    def sides(by):
        v = jnp.concatenate(
            [pltpu.roll(rows(12), by, 1) if by else rows(12), pltpu.roll(rows(14), by, 1) if by else rows(14)],
            axis=1,
        )
        return jnp.where(lane >= 121, v, 0.0), jnp.where(lane < 7, v, 0.0)

    own = (iota((256, SLOTS), 0) + 1).astype(F32)
    g = iota((64, SLOTS), 0)
    j = jnp.bitwise_and(g, 7)
    high = ((g - j) * 4 + j + 1).astype(F32)
    low = high + 24.0
    main = place(own, 0, both(0))
    above, below = place(high, 2, both(8)), place(low, 1, both(4))
    minus, plus = sides(0)
    side = place(own, 3, minus) + place(own, 6, plus)
    minus, plus = sides(96)
    side_below = place(low, 4, minus) + place(low, 7, plus)
    minus, plus = sides(64)
    side_above = place(high, 5, minus) + place(high, 8, plus)
    for c in range(2):
        part = slice(c * 128, (c + 1) * 128)

        def planes(v, v_above, v_below):
            v = v[:, part].reshape(8, 32, 128)
            v_above, v_below = (u[:, part].reshape(8, 8, 128) for u in (v_above, v_below))
            return [tall(v[z], v_above[z], v_below[z]) for z in range(NZ)]

        strip = jnp.zeros((EY, 128), F32)
        for z, plane in enumerate(planes(side, side_above, side_below)):
            strip = to_strip(plane, z, strip)
        wx[c] = strip
        mine = planes(main, above, below)
        for z in range(NZ):
            ws[c, z] = mine[z]
        first, strip = 4 if ins else 0, swap(strip)
        cols = ins[1][c] if ins else jnp.zeros((EY, 128), F32)
        for j in range(first):
            up[c, j] = ins[0][c, 4 + j].astype(BF16)
            down[c, j] = ins[0][c, j].astype(BF16)
        for j in range(3):
            up[c, first + j] = mine[5 + j].astype(BF16)
            down[c, first + j] = mine[j].astype(BF16)
        up[c, first + 3] = by_half(strip, cols).astype(BF16)
        down[c, first + 3] = by_half(cols, strip).astype(BF16)


def place(arrived, *ins):
    sent = jax.ShapeDtypeStruct((2, 8 if ins else 4, EY, 128), BF16)
    return call(
        place_body,
        (
            jax.ShapeDtypeStruct((2, NZ, EY, 128), F32),
            jax.ShapeDtypeStruct((2, EY, 128), F32),
            sent,
            sent,
        ),
        [pltpu.VMEM((1024, 128), F32)],
    )(arrived, *ins)


def fields_of(refs):
    adj, couple, diag, cross, source = refs
    out = [(adj, 0), (adj, 1)] + [(couple, i) for i in range(6)]
    return out + [(r, i) for r in (diag, cross, source) for i in range(2)]


def ysend_body(*refs):
    far, (up, down), near, sems = refs[:5], refs[6:8], refs[8:13], refs[13]
    pairs = [(a.at[:, :, 0:8], b.at[:, :, 0:8]) for a, b in zip(far, near)]
    pairs += [(a.at[:, :, 24:32], b.at[:, :, 8:16]) for a, b in zip(far, near)]
    for copy in start_copies(pairs, sems):
        copy.wait()
    for f, (ref, i) in enumerate(fields_of(near)):
        down[8 * f : 8 * f + 8] = ref[i, :, 0:8].astype(BF16)
        up[8 * f : 8 * f + 8] = ref[i, :, 8:16].astype(BF16)


def ysend(after, *ins):
    shape = jax.ShapeDtypeStruct((112, 8, 128), BF16)
    near = [pltpu.VMEM((a.shape[0], NZ, 16, NX), F32) for a in ins]
    near += [pltpu.SemaphoreType.DMA((2 * len(ins),))]
    return call(ysend_body, (shape, shape), near, [True] * 6)(*ins, after)


def block_planes(ref, i, f, ylo, yhi):
    return [
        tall(ref[i, z], yhi[8 * f + z].astype(F32), ylo[8 * f + z].astype(F32)) for z in range(NZ)
    ]


def xsend_body(*refs):
    ins, (ylo, yhi, _, out) = refs[:-4], refs[-4:]
    for f, (ref, i) in enumerate(fields_of(ins)):
        strip = jnp.zeros((EY, 128), F32)
        for z, plane in enumerate(block_planes(ref, i, f, ylo, yhi)):
            strip = to_strip(plane, z, strip)
        out[f] = strip.astype(BF16)


def xsend(after, *ins):
    shape = jax.ShapeDtypeStruct((14, EY, 128), BF16)
    return call(xsend_body, shape, far=[False] * len(ins) + [True])(*ins, after)


def z_slot(f):
    return (4 * f, 4) if f < 2 else (3 * f + 2, 3)


def zsend_body(*refs):
    ins, (ylo, yhi, xlo, xhi, _, up, down) = refs[:-7], refs[-7:]
    for f, (ref, i) in enumerate(fields_of(ins)):
        planes = block_planes(ref, i, f, ylo, yhi)
        at, deep = z_slot(f)
        for j in range(deep):
            up[at + j] = planes[NZ - deep + j].astype(BF16)
            down[at + j] = planes[j].astype(BF16)
    for q in range(7):
        even, odd = columns(xlo, xhi, 2 * q), swap(columns(xlo, xhi, 2 * q + 1))
        up[44 + q] = by_half(odd, even).astype(BF16)
        down[44 + q] = by_half(even, odd).astype(BF16)


def zsend(after, *ins):
    shape = jax.ShapeDtypeStruct((51, EY, NX), BF16)
    return call(zsend_body, (shape, shape), far=[False] * len(ins) + [True])(*ins, after)


def field_planes(ref, i, f, ylo, yhi, zlo, zhi):
    at, deep = z_slot(f)
    low = [zlo[at + j].astype(F32) for j in range(deep)]
    high = [zhi[at + j].astype(F32) for j in range(deep)]
    return low + block_planes(ref, i, f, ylo, yhi) + high


def field_strip(f, xlo, xhi, zlo, zhi):
    low, high = zlo[44 + f // 2].astype(F32), zhi[44 + f // 2].astype(F32)
    far = swap(by_half(low, high)) if f % 2 else by_half(high, low)
    return jnp.concatenate([columns(xlo, xhi, f), far], axis=1)


def half_group(z):
    return (0, z - 4) if 4 <= z < 12 else (1, (z - 12) % 16)


def sweeps_body(final, *refs):
    ins, ylo, yhi, xlo, xhi, zlo, zhi = refs[:5], *refs[5:11]
    field, fstrip, buf0, buf1, overs, rhs, rstrip = refs[-7:]
    if final:
        near, out = refs[11], refs[-8]
        ws, wx, wlo, whi = refs[12:16]
    else:
        out, out_strip = refs[-9:-7]
        ws, wx, wlo, whi = refs[11:15]
    bufs = (buf0, buf1)
    strips = []
    skip = 4 if final else 0
    lane = iota((EY, 128), 1)
    column = jnp.bitwise_and(iota((EY, 256), 1), 15)

    for c in range(2):
        if final:
            planes = [wlo[c, j].astype(F32) for j in range(4)]
            planes += [ins[0][c, z] for z in range(NZ)]
            planes += [whi[c, j].astype(F32) for j in range(4)]
        else:
            planes = field_planes(ins[0], c, c, ylo, yhi, zlo, zhi)
        for z, plane in enumerate(planes):
            buf0[c, z] = plane
        for e, plane in enumerate(field_planes(ins[4], c, 12 + c, ylo, yhi, zlo, zhi)):
            if e < 3:
                extra = wlo[c, skip + e].astype(F32)
            elif e >= 11:
                extra = whi[c, skip + e - 11].astype(F32)
            else:
                extra = ws[c, e - 3]
            rhs[c, e] = plane + extra
    for n, (ref, i) in enumerate(fields_of(ins)[2:12]):
        for e, plane in enumerate(field_planes(ref, i, n + 2, ylo, yhi, zlo, zhi)):
            field[n, e] = plane
        fstrip[n] = field_strip(n + 2, xlo, xhi, zlo, zhi)
    for c in range(2):
        low, high = wlo[c, skip + 3].astype(F32), whi[c, skip + 3].astype(F32)
        if final:
            strips.append(jnp.concatenate([near[c], by_half(high, low)], axis=1))
        else:
            strips.append(field_strip(c, xlo, xhi, zlo, zhi))
        side = jnp.concatenate([wx[c], swap(by_half(low, high))], axis=1)
        rstrip[c] = side + field_strip(12 + c, xlo, xhi, zlo, zhi)

    def mix(co, inflow):
        return co(6) * inflow[0] + co(8) * inflow[1], co(9) * inflow[0] + co(7) * inflow[1]

    for s in range(SWEEPS):
        last = s == SWEEPS - 1
        src, dst = bufs[s % 2], bufs[1 - s % 2]
        rows = NY if last and final else EY
        layers = range(1 + s, EZ - 1 - s)
        edges = []
        for c in range(2):
            edge = [jnp.zeros((EY, 128), F32)] * 2
            for z in layers:
                h, g = half_group(z)
                overs[c, z] = pltpu.roll(strips[c][:, 128 * h : 128 * h + 128], 120 - 16 * g, 1)
                if not (last and final):
                    edge[h] = to_strip(src[c, z], g, edge[h])
            edges.append(jnp.concatenate(edge, axis=1))

        for z in layers:

            def co(n):
                return field[n, z - 1, 0:rows]

            inflow = []
            for c in range(2):
                here, over = src[c, z], overs[c, z]
                right = pltpu.roll(jnp.where(lane == 0, over, here), 127, 1)
                left = pltpu.roll(jnp.where(lane == 127, over, here), 1, 1)
                total = rhs[c, z - 1, 0:rows]
                total = total + co(0) * src[c, z + 1, 0:rows]
                total = total + co(1) * src[c, z - 1, 0:rows]
                total = total + co(2) * pltpu.roll(here, EY - 1, 0)[0:rows]
                total = total + co(3) * pltpu.roll(here, 1, 0)[0:rows]
                total = total + co(4) * right[0:rows]
                total = total + co(5) * left[0:rows]
                inflow.append(total)
            for c, new in enumerate(mix(co, inflow)):
                if last:
                    out[c, z - 4] = new
                else:
                    dst[c, z] = new
        if last and final:
            break

        def co(n):
            return fstrip[n]

        inflow = []
        for c in range(2):
            here, edge = strips[c], edges[c]
            right = pltpu.roll(jnp.where(column == 8, edge, here), 255, 1)
            left = pltpu.roll(jnp.where(column == 7, edge, here), 1, 1)
            total = rstrip[c]
            total = total + co(0) * pltpu.roll(here, 240, 1) + co(1) * pltpu.roll(here, 16, 1)
            total = total + co(2) * pltpu.roll(here, EY - 1, 0) + co(3) * pltpu.roll(here, 1, 0)
            total = total + co(4) * right + co(5) * left
            inflow.append(total)
        strips = list(mix(co, inflow))
    if not final:
        for c in range(2):
            out_strip[c] = strips[c][:, 0:128]


def sweeps(final, *ins):
    shape = jax.ShapeDtypeStruct((2, NZ, NY if final else EY, NX), F32)
    return call(
        functools.partial(sweeps_body, final),
        shape if final else (shape, jax.ShapeDtypeStruct((2, EY, 128), F32)),
        [
            pltpu.VMEM((10, CZ, EY, 128), F32),
            pltpu.VMEM((10, EY, 256), F32),
            pltpu.VMEM((2, EZ, EY, 128), F32),
            pltpu.VMEM((2, EZ, EY, 128), F32),
            pltpu.VMEM((2, EZ, EY, 128), F32),
            pltpu.VMEM((2, CZ, EY, 128), F32),
            pltpu.VMEM((2, EY, 256), F32),
        ],
    )(*ins)


def exchange(up, down, axis):
    count = lax.axis_size(axis)
    forward = [(i, i + 1) for i in range(count - 1)]
    backward = [(i + 1, i) for i in range(count - 1)]
    return lax.ppermute(up, axis, forward), lax.ppermute(down, axis, backward)


def per_device(
    source,
    adjoint_start,
    couple,
    diag_inverse,
    cross_inverse,
    perf_row,
    well_owner,
    well_slot,
    well_block,
    cross_block,
):
    perf = perf_row.reshape(1, -1)
    owner = well_owner.reshape(1, -1)
    slot = well_slot.reshape(1, -1)
    well = well_block.reshape(well_block.shape[3:])
    cross_mats = cross_block.reshape(cross_block.shape[3:])
    fields = (couple, diag_inverse, cross_inverse, source)
    start = (adjoint_start, *fields)
    sent = panels(adjoint_start, perf, owner, slot, far=True)
    arrived = lax.all_to_all(sent, ("gy", "gx"), split_axis=0, concat_axis=0, tiled=True)
    ylo, yhi = exchange(*ysend(sent, *start), "gy")
    answers = owner_work(arrived, well, cross_mats)
    answers, ylo, yhi = lax.optimization_barrier((answers, ylo, yhi))
    packed = xsend(answers, *start, ylo, yhi)
    halo = (ylo, yhi, *exchange(packed, packed, "gx"))
    returned = lax.all_to_all(answers, ("gy", "gx"), split_axis=0, concat_axis=0, tiled=True)
    kept = (*fields, *halo, *exchange(*zsend(returned, *start, *halo), "gz"))
    ws, wx, up, down = place(returned)
    adjoint, strip = sweeps(False, *start[:1], *kept, ws, wx, *exchange(up, down, "gz"))

    sent = panels(adjoint, perf, owner, slot)
    arrived = lax.all_to_all(sent, ("gy", "gx"), split_axis=0, concat_axis=0, tiled=True)
    answers = owner_work(arrived, well, cross_mats)
    returned = lax.all_to_all(answers, ("gy", "gx"), split_axis=0, concat_axis=0, tiled=True)
    ws, wx, up, down = place(returned, adjoint, strip)
    return sweeps(True, adjoint, *kept, strip, ws, wx, *exchange(up, down, "gz"))


def solution(mesh):
    placed = (
        P(None, "gz", "gy", "gx"),
        P(None, "gz", "gy", "gx"),
        P(None, "gz", "gy", "gx"),
        P(None, "gz", "gy", "gx"),
        P(None, "gz", "gy", "gx"),
        P("gz", "gy", "gx", None),
        P("gz", "gy", "gx", None, None),
        P("gz", "gy", "gx", None),
        P("gz", "gy", "gx", None, None, None),
        P("gz", "gy", "gx", None, None, None),
    )
    return jax.shard_map(
        per_device, mesh=mesh, in_specs=placed, out_specs=P(None, "gz", "gy", "gx"), check_vma=False
    )
```

time: 141 us -> 139 us (0.986)
  blocking collectives: 0 us -> 39.2 us
  starting transfers between devices: 88.8 us -> 61 us
  waiting for transfers between devices: 31.6 us -> 21.2 us
  Pallas kernels: 19 us -> 14.9 us
    all_to_all x0 -> x2, blocking collectives: none -> 39.2 us  [the longest x1 21.6 us: per_device(): lax.all_to_all(sent, ('gy', 'gx'), split_axis=0, concat_axis=0, tiled=True)]
    all_to_all x2 -> x1, starting transfers between devices: 31.7 us -> 17.1 us  [per_device(): lax.all_to_all(sent, ('gy', 'gx'), split_axis=0, concat_axis=0, tiled=True)]
    ppermute x14 -> x10, starting transfers between devices: 39.2 us -> 31.6 us  [exchange(): return (lax.ppermute(up, axis, forward), lax.ppermute(down, axis, backward))]
    all_to_all x2 -> x1, starting transfers between devices: 17.9 us -> 12.2 us  [per_device(): lax.all_to_all(answers, ('gy', 'gx'), split_axis=0, concat_axis=0, tiled=...]
    all_to_all x2 -> x1, waiting for transfers between devices: 9 us -> 5.07 us  [per_device(): lax.all_to_all(sent, ('gy', 'gx'), split_axis=0, concat_axis=0, tiled=True)]
    all_to_all x2 -> x1, waiting for transfers between devices: 6.32 us -> 2.7 us  [per_device(): lax.all_to_all(answers, ('gy', 'gx'), split_axis=0, concat_axis=0, tiled=...]
    ppermute x14 -> x10, waiting for transfers between devices: 16.3 us -> 13.5 us  [exchange(): return (lax.ppermute(up, axis, forward), lax.ppermute(down, axis, backward))]
    pallas_call x7 -> x5, Pallas kernels: 11.7 us -> 9.59 us  [the longest x2 6.78 us: sweeps(): call(functools.partial(sweeps_body, final), shape if final else (shape, j...]
  transfers between devices with their start and end apart: 18 -> 12, of which waited for: 11 -> 7; matrix products, arithmetic and copies ran while one was open for 0% -> 0% of each run, Pallas kernels for 4% -> 4%
where the time goes in v4:
time: 139 us; the launch traced here: 138 us
  starting transfers between devices  61 us (44%)
  blocking collectives  39.2 us (28%)
  waiting for transfers between devices  21.2 us (15%)
  Pallas kernels  14.9 us (11%)
  local copies, waits for them, and re-layouts  1.67 us (1%)
    ppermute x10, starting transfers between devices, exchange(): return (lax.ppermute(up, axis, forward), lax.ppermute(down, axis, backward))  31.6 us
    all_to_all x1, blocking collectives, per_device(): lax.all_to_all(sent, ('gy', 'gx'), split_axis=0, concat_axis=0, tiled=True)  21.6 us
    all_to_all x1, blocking collectives, per_device(): lax.all_to_all(answers, ('gy', 'gx'), split_axis=0, concat_axis=0, tiled=...  17.6 us
    all_to_all x1, starting transfers between devices, per_device(): lax.all_to_all(sent, ('gy', 'gx'), split_axis=0, concat_axis=0, tiled=True)  17.1 us
    ppermute x10, waiting for transfers between devices, exchange(): return (lax.ppermute(up, axis, forward), lax.ppermute(down, axis, backward))  13.5 us
    all_to_all x1, starting transfers between devices, per_device(): lax.all_to_all(answers, ('gy', 'gx'), split_axis=0, concat_axis=0, tiled=...  12.2 us
    pallas_call x2, Pallas kernels, sweeps(): call(functools.partial(sweeps_body, final), shape if final else (shape, j...  6.78 us
    all_to_all x1, waiting for transfers between devices, per_device(): lax.all_to_all(sent, ('gy', 'gx'), split_axis=0, concat_axis=0, tiled=True)  5.07 us
  transfers between devices with their start and end apart: 12, of which 7 were waited for; matrix products, arithmetic and copies ran while one was open for 0% of the time, Pallas kernels for 4%

profile of v4, /device:TPU:1, one launch (start us, length us, event | category | flops | bytes accessed | tf_op | source)
XLA Modules:
  0.0 138.2 jit_solution(1335141154312417417)
XLA Ops:
  0.0 0.6 copy-done.9
  0.7 0.9 copy-done.1
  1.6 1.1 shard_map.100.refs_5_
  2.8 17.1 %all-to-all-start = ((bf16[64,8,128]{2,1,0:T(8,128)(2,1)}), bf16[64,8,128]{2,1,0:T(8,128)(2,1)S(1)}, u32[]{:S(2)}, u32[]{:S(2)}) async-start(bf16[64,8,128]{2,1,0:T(8,128)(2,1)} %bitcast.3), calls=%async_computation | async-start | bytes 262144 | tf_op jit(solution)/shard_map/all_to_all | solution.py:502
  19.9 2.2 %shard_map.102 = (bf16[112,8,128]{2,1,0:T(8,128)(2,1)}, bf16[112,8,128]{2,1,0:T(8,128)(2,1)}) custom-call(f32[2,8,32,128]{3,2,1,0:T(8,128)} %refs_0_.7, f32[6,8,32,128]{3,2,1,0:T(8,128)} %refs_1_.9, f32[2,8,32,128]{3,2,1,0:T(8,128)} %refs_2_.9, f32[2,8,32,128]{3,2,1,0:T(8,128)} %refs_3_.9, f32[2,8,32,128]{3,2,1,0:T(8,128)} %refs_4_.9, ...), custom_call_target="tpu_custom_call" | custom-call | tf_op jit(solution)/shard_map/pallas_call | solution.py:287
  22.1 2.9 %collective-permute-start = (bf16[112,8,128]{2,1,0:T(8,128)(2,1)}, bf16[112,8,128]{2,1,0:T(8,128)(2,1)S(1)}, u32[]{:S(2)}, u32[]{:S(2)}) collective-permute-start(bf16[112,8,128]{2,1,0:T(8,128)(2,1)} %get-tuple-element.22), channel_id=1, source_target_pairs={{0,8},{8,16},{16,24},{24,32},{32,40},{40,48},{48,56},{1,9},{9,17},... | collective-permute-start | bytes 688136 | tf_op jit(solution)/shard_map/ppermute | solution.py:479
  25.1 1.3 collective-permute-start.1
  26.4 5.1 %all-to-all-done = bf16[64,8,128]{2,1,0:T(8,128)(2,1)S(1)} async-done(((bf16[64,8,128]{2,1,0:T(8,128)(2,1)}), bf16[64,8,128]{2,1,0:T(8,128)(2,1)S(1)}, u32[]{:S(2)}, u32[]{:S(2)}) %all-to-all-start) | async-done | bytes 131104 | tf_op jit(solution)/shard_map/all_to_all | solution.py:502
  31.5 1.7 %shard_map.101.refs_7_ = bf16[64,16,128]{2,1,0:T(8,128)(2,1)} custom-call(bf16[512,128]{1,0:T(8,128)(2,1)S(1)} %bitcast.14, bf16[4,256,256]{2,1,0:T(8,128)(2,1)S(1)} %bitcast.9, bf16[4,256,256]{2,1,0:T(8,128)(2,1)S(1)} %bitcast.11), custom_call_target="tpu_custom_call" | custom-call | tf_op jit(solution)/shard_map/pallas_call | solution.py:175
  33.2 12.2 %all-to-all-start.1 = ((bf16[64,16,128]{2,1,0:T(8,128)(2,1)}), bf16[64,16,128]{2,1,0:T(8,128)(2,1)S(1)}, u32[]{:S(2)}, u32[]{:S(2)}) async-start(bf16[64,16,128]{2,1,0:T(8,128)(2,1)} %shard_map.101.refs_7_), calls=%async_computation.1 | async-start | bytes 524288 | tf_op jit(solution)/shard_map/all_to_all | solution.py:508
  45.4 0.4 shard_map.103
  45.9 1.3 collective-permute-start.3
  47.2 4.0 %collective-permute-start.2 = (bf16[14,48,128]{2,1,0:T(8,128)(2,1)S(1)}, bf16[14,48,128]{2,1,0:T(8,128)(2,1)S(1)}, u32[]{:S(2)}, u32[]{:S(2)}) collective-permute-start(bf16[14,48,128]{2,1,0:T(8,128)(2,1)S(1)} %shard_map.103), channel_id=1, source_target_pairs={{0,1},{1,2},{2,3},{3,4},{4,5},{5,6},{6,7},{8,9},{9,10},{10,11},{11... | collective-permute-start | bytes 516104 | tf_op jit(solution)/shard_map/ppermute | solution.py:479
  51.2 4.0 %collective-permute-done.3.refs_8_ = bf16[14,48,128]{2,1,0:T(8,128)(2,1)S(1)} collective-permute-done((bf16[14,48,128]{2,1,0:T(8,128)(2,1)S(1)}, bf16[14,48,128]{2,1,0:T(8,128)(2,1)S(1)}, u32[]{:S(2)}, u32[]{:S(2)}) %collective-permute-start.3) | collective-permute-done | bytes 172064 | tf_op jit(solution)/shard_map/ppermute | solution.py:479
  55.2 2.7 %all-to-all-done.1.refs_9_.arrived = bf16[64,16,128]{2,1,0:T(8,128)(2,1)S(1)} async-done(((bf16[64,16,128]{2,1,0:T(8,128)(2,1)}), bf16[64,16,128]{2,1,0:T(8,128)(2,1)S(1)}, u32[]{:S(2)}, u32[]{:S(2)}) %all-to-all-start.1) | async-done | bytes 262176 | tf_op jit(solution)/shard_map/all_to_all | solution.py:508
  58.1 6.9 %collective-permute-start.4 = (bf16[51,48,128]{2,1,0:T(8,128)(2,1)S(1)}, bf16[51,48,128]{2,1,0:T(8,128)(2,1)S(1)}, u32[]{:S(2)}, u32[]{:S(2)}) collective-permute-start(bf16[51,48,128]{2,1,0:T(8,128)(2,1)S(1)} %get-tuple-element.27), channel_id=1, source_target_pairs={{0,64},{64,128},{128,192},{192,256},{256,320},{320,384},{384,448},... | collective-permute-start | bytes 1880072 | tf_op jit(solution)/shard_map/ppermute | solution.py:479
  65.0 1.9 %collective-permute-start.5 = (bf16[51,48,128]{2,1,0:T(8,128)(2,1)S(1)}, bf16[51,48,128]{2,1,0:T(8,128)(2,1)S(1)}, u32[]{:S(2)}, u32[]{:S(2)}) collective-permute-start(bf16[51,48,128]{2,1,0:T(8,128)(2,1)S(1)} %get-tuple-element.28), channel_id=1, source_target_pairs={{64,0},{128,64},{192,128},{256,192},{320,256},{384,320},{448,384},... | collective-permute-start | bytes 1880072 | tf_op jit(solution)/shard_map/ppermute | solution.py:479
  67.0 0.6 shard_map.105
  67.6 3.6 %collective-permute-start.6 = (bf16[2,4,48,128]{3,2,1,0:T(8,128)(2,1)S(1)}, bf16[2,4,48,128]{3,2,1,0:T(8,128)(2,1)S(1)}, u32[]{:S(2)}, u32[]{:S(2)}) collective-permute-start(bf16[2,4,48,128]{3,2,1,0:T(8,128)(2,1)S(1)} %get-tuple-element.31), channel_id=1, source_target_pairs={{0,64},{64,128},{128,192},{192,256},{256,320},{320,384},{384,448},... | collective-permute-start | bytes 294920 | tf_op jit(solution)/shard_map/ppermute | solution.py:479
  71.2 1.9 %collective-permute-start.7 = (bf16[2,4,48,128]{3,2,1,0:T(8,128)(2,1)S(1)}, bf16[2,4,48,128]{3,2,1,0:T(8,128)(2,1)S(1)}, u32[]{:S(2)}, u32[]{:S(2)}) collective-permute-start(bf16[2,4,48,128]{3,2,1,0:T(8,128)(2,1)S(1)} %get-tuple-element.32), channel_id=1, source_target_pairs={{64,0},{128,64},{192,128},{256,192},{320,256},{384,320},{448,384},... | collective-permute-start | bytes 294920 | tf_op jit(solution)/shard_map/ppermute | solution.py:479
  73.3 4.4 %collective-permute-done.7.refs_14_ = bf16[2,4,48,128]{3,2,1,0:T(8,128)(2,1)S(1)} collective-permute-done((bf16[2,4,48,128]{3,2,1,0:T(8,128)(2,1)S(1)}, bf16[2,4,48,128]{3,2,1,0:T(8,128)(2,1)S(1)}, u32[]{:S(2)}, u32[]{:S(2)}) %collective-permute-start.7) | collective-permute-done | bytes 98336 | tf_op jit(solution)/shard_map/ppermute | solution.py:479
  77.7 3.3 %shard_map.106 = (f32[2,8,48,128]{3,2,1,0:T(8,128)S(1)}, f32[2,48,128]{2,1,0:T(8,128)S(1)}) custom-call(f32[2,8,32,128]{3,2,1,0:T(8,128)S(1)} %copy-done.2, f32[6,8,32,128]{3,2,1,0:T(8,128)S(1)} %copy-done, f32[2,8,32,128]{3,2,1,0:T(8,128)S(1)} %copy-done.3, f32[2,8,32,128]{3,2,1,0:T(8,128)S(1)} %copy-done.4, f32[2,8,32,128]{3,2,1,0:T(8,128)S(1)} %copy-done.5, ...), custom_call_target="tpu_custom_call" | custom-call | tf_op jit(solution)/shard_map/pallas_call | solution.py:460
  81.0 0.4 shard_map.107
  81.3 21.6 %all_to_all.32 = bf16[64,8,128]{2,1,0:T(8,128)(2,1)S(1)} all-to-all(bf16[64,8,128]{2,1,0:T(8,128)(2,1)S(1)} %bitcast.13), channel_id=1, replica_groups=mesh['gz'=8,'gy'=8,'gx'=8] {'gy','gx'}, dimensions={0} | all-to-all | bytes 262144 | tf_op jit(solution)/shard_map/all_to_all | solution.py:514
  102.9 1.0 shard_map.108
  103.9 17.6 %all_to_all.33.arrived = bf16[64,16,128]{2,1,0:T(8,128)(2,1)S(1)} all-to-all(bf16[64,16,128]{2,1,0:T(8,128)(2,1)S(1)} %shard_map.108), channel_id=1, replica_groups=mesh['gz'=8,'gy'=8,'gx'=8] {'gy','gx'}, dimensions={0} | all-to-all | bytes 524288 | tf_op jit(solution)/shard_map/all_to_all | solution.py:516
  121.5 0.6 shard_map.109
  122.1 5.6 %collective-permute-start.8 = (bf16[2,8,48,128]{3,2,1,0:T(8,128)(2,1)S(1)}, bf16[2,8,48,128]{3,2,1,0:T(8,128)(2,1)S(1)}, u32[]{:S(2)}, u32[]{:S(2)}) collective-permute-start(bf16[2,8,48,128]{3,2,1,0:T(8,128)(2,1)S(1)} %get-tuple-element.37), channel_id=1, source_target_pairs={{0,64},{64,128},{128,192},{192,256},{256,320},{320,384},{384,448},... | collective-permute-start | bytes 589832 | tf_op jit(solution)/shard_map/ppermute | solution.py:479
  127.7 2.1 %collective-permute-start.9 = (bf16[2,8,48,128]{3,2,1,0:T(8,128)(2,1)S(1)}, bf16[2,8,48,128]{3,2,1,0:T(8,128)(2,1)S(1)}, u32[]{:S(2)}, u32[]{:S(2)}) collective-permute-start(bf16[2,8,48,128]{3,2,1,0:T(8,128)(2,1)S(1)} %get-tuple-element.38), channel_id=1, source_target_pairs={{64,0},{128,64},{192,128},{256,192},{320,256},{384,320},{448,384},... | collective-permute-start | bytes 589832 | tf_op jit(solution)/shard_map/ppermute | solution.py:479
  129.8 0.5 collective-permute-done.8.refs_14_
  130.3 4.4 %collective-permute-done.9.refs_15_ = bf16[2,8,48,128]{3,2,1,0:T(8,128)(2,1)S(1)} collective-permute-done((bf16[2,8,48,128]{3,2,1,0:T(8,128)(2,1)S(1)}, bf16[2,8,48,128]{3,2,1,0:T(8,128)(2,1)S(1)}, u32[]{:S(2)}, u32[]{:S(2)}) %collective-permute-start.9) | collective-permute-done | bytes 196640 | tf_op jit(solution)/shard_map/ppermute | solution.py:479
  134.7 3.5 %shard_map.110 = f32[2,8,32,128]{3,2,1,0:T(8,128)} custom-call(f32[2,8,48,128]{3,2,1,0:T(8,128)S(1)} %get-tuple-element.33.adj.refs_0_, f32[6,8,32,128]{3,2,1,0:T(8,128)S(1)} %copy-done, f32[2,8,32,128]{3,2,1,0:T(8,128)S(1)} %copy-done.3, f32[2,8,32,128]{3,2,1,0:T(8,128)S(1)} %copy-done.4, f32[2,8,32,128]{3,2,1,0:T(8,128)S(1)} %copy-done.5, ...), custom_call_target="tpu_custom_call" | custom-call | tf_op jit(solution)/shard_map/pallas_call | solution.py:460
  (29 shorter events, 0.4 us)
Async XLA Ops:
  0.0 0.7 copy-start.9
  0.0 0.7 copy-start.10
  0.0 0.7 copy-start.11
  0.7 0.9 copy-start.1
  2.8 28.7 %all-to-all-start = ((bf16[64,8,128]{2,1,0:T(8,128)(2,1)}), bf16[64,8,128]{2,1,0:T(8,128)(2,1)S(1)}, u32[]{:S(2)}, u32[]{:S(2)}) async-start(bf16[64,8,128]{2,1,0:T(8,128)(2,1)} %bitcast.3), calls=%async_computation | async-start | bytes 262144 | tf_op jit(solution)/shard_map/all_to_all | solution.py:502
  19.9 11.6 %copy-start.6 = (bf16[1,1,1,4,256,256]{5,4,3,2,1,0:T(8,128)(2,1)S(1)}, bf16[1,1,1,4,256,256]{5,4,3,2,1,0:T(8,128)(2,1)}, u32[]{:S(2)}) copy-start(bf16[1,1,1,4,256,256]{5,4,3,2,1,0:T(8,128)(2,1)} %param.18) | copy-start | bytes 1572868
  19.9 11.5 %copy-start.7 = (bf16[1,1,1,4,256,256]{5,4,3,2,1,0:T(8,128)(2,1)S(1)}, bf16[1,1,1,4,256,256]{5,4,3,2,1,0:T(8,128)(2,1)}, u32[]{:S(2)}) copy-start(bf16[1,1,1,4,256,256]{5,4,3,2,1,0:T(8,128)(2,1)} %param.19) | copy-start | bytes 1572868
  22.1 11.0 %collective-permute-start = (bf16[112,8,128]{2,1,0:T(8,128)(2,1)}, bf16[112,8,128]{2,1,0:T(8,128)(2,1)S(1)}, u32[]{:S(2)}, u32[]{:S(2)}) collective-permute-start(bf16[112,8,128]{2,1,0:T(8,128)(2,1)} %get-tuple-element.22), channel_id=1, source_target_pairs={{0,8},{8,16},{16,24},{24,32},{32,40},{40,48},{48,56},{1,9},{9,17},... | collective-permute-start | bytes 688136 | tf_op jit(solution)/shard_map/ppermute | solution.py:479
  25.1 8.1 %collective-permute-start.1 = (bf16[112,8,128]{2,1,0:T(8,128)(2,1)}, bf16[112,8,128]{2,1,0:T(8,128)(2,1)S(1)}, u32[]{:S(2)}, u32[]{:S(2)}) collective-permute-start(bf16[112,8,128]{2,1,0:T(8,128)(2,1)} %get-tuple-element.23), channel_id=1, source_target_pairs={{8,0},{16,8},{24,16},{32,24},{40,32},{48,40},{56,48},{9,1},{17,9},... | collective-permute-start | bytes 688136 | tf_op jit(solution)/shard_map/ppermute | solution.py:479
  31.5 13.9 %copy-start = (f32[6,8,32,128]{3,2,1,0:T(8,128)S(1)}, f32[6,8,32,128]{3,2,1,0:T(8,128)}, u32[]{:S(2)}) copy-start(f32[6,8,32,128]{3,2,1,0:T(8,128)} %refs_1_.9) | copy-start | bytes 2359300
  31.5 13.9 %copy-start.4 = (f32[2,8,32,128]{3,2,1,0:T(8,128)S(1)}, f32[2,8,32,128]{3,2,1,0:T(8,128)}, u32[]{:S(2)}) copy-start(f32[2,8,32,128]{3,2,1,0:T(8,128)} %refs_3_.9) | copy-start | bytes 786436
  31.5 13.9 %copy-start.5 = (f32[2,8,32,128]{3,2,1,0:T(8,128)S(1)}, f32[2,8,32,128]{3,2,1,0:T(8,128)}, u32[]{:S(2)}) copy-start(f32[2,8,32,128]{3,2,1,0:T(8,128)} %refs_4_.9) | copy-start | bytes 786436
  33.1 12.3 %copy-start.2 = (f32[2,8,32,128]{3,2,1,0:T(8,128)S(1)}, f32[2,8,32,128]{3,2,1,0:T(8,128)}, u32[]{:S(2)}) copy-start(f32[2,8,32,128]{3,2,1,0:T(8,128)} %refs_0_.7) | copy-start | bytes 786436
  33.1 12.3 %copy-start.3 = (f32[2,8,32,128]{3,2,1,0:T(8,128)S(1)}, f32[2,8,32,128]{3,2,1,0:T(8,128)}, u32[]{:S(2)}) copy-start(f32[2,8,32,128]{3,2,1,0:T(8,128)} %refs_2_.9) | copy-start | bytes 786436
  33.2 24.8 %all-to-all-start.1 = ((bf16[64,16,128]{2,1,0:T(8,128)(2,1)}), bf16[64,16,128]{2,1,0:T(8,128)(2,1)S(1)}, u32[]{:S(2)}, u32[]{:S(2)}) async-start(bf16[64,16,128]{2,1,0:T(8,128)(2,1)} %shard_map.101.refs_7_), calls=%async_computation.1 | async-start | bytes 524288 | tf_op jit(solution)/shard_map/all_to_all | solution.py:508
  45.9 9.3 %collective-permute-start.3 = (bf16[14,48,128]{2,1,0:T(8,128)(2,1)S(1)}, bf16[14,48,128]{2,1,0:T(8,128)(2,1)S(1)}, u32[]{:S(2)}, u32[]{:S(2)}) collective-permute-start(bf16[14,48,128]{2,1,0:T(8,128)(2,1)S(1)} %shard_map.103), channel_id=1, source_target_pairs={{1,0},{2,1},{3,2},{4,3},{5,4},{6,5},{7,6},{9,8},{10,9},{11,10},{12... | collective-permute-start | bytes 516104 | tf_op jit(solution)/shard_map/ppermute | solution.py:479
  47.2 8.0 %collective-permute-start.2 = (bf16[14,48,128]{2,1,0:T(8,128)(2,1)S(1)}, bf16[14,48,128]{2,1,0:T(8,128)(2,1)S(1)}, u32[]{:S(2)}, u32[]{:S(2)}) collective-permute-start(bf16[14,48,128]{2,1,0:T(8,128)(2,1)S(1)} %shard_map.103), channel_id=1, source_target_pairs={{0,1},{1,2},{2,3},{3,4},{4,5},{5,6},{6,7},{8,9},{9,10},{10,11},{11... | collective-permute-start | bytes 516104 | tf_op jit(solution)/shard_map/ppermute | solution.py:479
  58.1 19.6 %collective-permute-start.4 = (bf16[51,48,128]{2,1,0:T(8,128)(2,1)S(1)}, bf16[51,48,128]{2,1,0:T(8,128)(2,1)S(1)}, u32[]{:S(2)}, u32[]{:S(2)}) collective-permute-start(bf16[51,48,128]{2,1,0:T(8,128)(2,1)S(1)} %get-tuple-element.27), channel_id=1, source_target_pairs={{0,64},{64,128},{128,192},{192,256},{256,320},{320,384},{384,448},... | collective-permute-start | bytes 1880072 | tf_op jit(solution)/shard_map/ppermute | solution.py:479
  65.0 12.7 %collective-permute-start.5 = (bf16[51,48,128]{2,1,0:T(8,128)(2,1)S(1)}, bf16[51,48,128]{2,1,0:T(8,128)(2,1)S(1)}, u32[]{:S(2)}, u32[]{:S(2)}) collective-permute-start(bf16[51,48,128]{2,1,0:T(8,128)(2,1)S(1)} %get-tuple-element.28), channel_id=1, source_target_pairs={{64,0},{128,64},{192,128},{256,192},{320,256},{384,320},{448,384},... | collective-permute-start | bytes 1880072 | tf_op jit(solution)/shard_map/ppermute | solution.py:479
  67.6 5.7 %collective-permute-start.6 = (bf16[2,4,48,128]{3,2,1,0:T(8,128)(2,1)S(1)}, bf16[2,4,48,128]{3,2,1,0:T(8,128)(2,1)S(1)}, u32[]{:S(2)}, u32[]{:S(2)}) collective-permute-start(bf16[2,4,48,128]{3,2,1,0:T(8,128)(2,1)S(1)} %get-tuple-element.31), channel_id=1, source_target_pairs={{0,64},{64,128},{128,192},{192,256},{256,320},{320,384},{384,448},... | collective-permute-start | bytes 294920 | tf_op jit(solution)/shard_map/ppermute | solution.py:479
  71.2 6.5 %collective-permute-start.7 = (bf16[2,4,48,128]{3,2,1,0:T(8,128)(2,1)S(1)}, bf16[2,4,48,128]{3,2,1,0:T(8,128)(2,1)S(1)}, u32[]{:S(2)}, u32[]{:S(2)}) collective-permute-start(bf16[2,4,48,128]{3,2,1,0:T(8,128)(2,1)S(1)} %get-tuple-element.32), channel_id=1, source_target_pairs={{64,0},{128,64},{192,128},{256,192},{320,256},{384,320},{448,384},... | collective-permute-start | bytes 294920 | tf_op jit(solution)/shard_map/ppermute | solution.py:479
  81.0 21.9 %copy-start.8 = (bf16[1,1,1,4,256,256]{5,4,3,2,1,0:T(8,128)(2,1)S(1)}, bf16[1,1,1,4,256,256]{5,4,3,2,1,0:T(8,128)(2,1)}, u32[]{:S(2)}) copy-start(bf16[1,1,1,4,256,256]{5,4,3,2,1,0:T(8,128)(2,1)} %param.19) | copy-start | bytes 1572868
  122.1 8.2 %collective-permute-start.8 = (bf16[2,8,48,128]{3,2,1,0:T(8,128)(2,1)S(1)}, bf16[2,8,48,128]{3,2,1,0:T(8,128)(2,1)S(1)}, u32[]{:S(2)}, u32[]{:S(2)}) collective-permute-start(bf16[2,8,48,128]{3,2,1,0:T(8,128)(2,1)S(1)} %get-tuple-element.37), channel_id=1, source_target_pairs={{0,64},{64,128},{128,192},{192,256},{256,320},{320,384},{384,448},... | collective-permute-start | bytes 589832 | tf_op jit(solution)/shard_map/ppermute | solution.py:479
  127.7 7.0 %collective-permute-start.9 = (bf16[2,8,48,128]{3,2,1,0:T(8,128)(2,1)S(1)}, bf16[2,8,48,128]{3,2,1,0:T(8,128)(2,1)S(1)}, u32[]{:S(2)}, u32[]{:S(2)}) collective-permute-start(bf16[2,8,48,128]{3,2,1,0:T(8,128)(2,1)S(1)} %get-tuple-element.38), channel_id=1, source_target_pairs={{64,0},{128,64},{192,128},{256,192},{320,256},{384,320},{448,384},... | collective-permute-start | bytes 589832 | tf_op jit(solution)/shard_map/ppermute | solution.py:479

commit v5 on v4

--- a/solution.py
+++ b/solution.py
@@ -50,9 +50,15 @@
     return lax.shift_right_logical(iota((EY, 128), 1), 4)
 
 
+def first_eight():
+    return jnp.bitwise_and(iota((EY, 128), 1), 15) < 8
+
+
 def columns(xlo, xhi, index):
-    low = jnp.bitwise_and(iota((EY, 128), 1), 15) < 8
-    return jnp.where(low, xlo[index].astype(F32), xhi[index].astype(F32))
+    below, above = xlo[index // 2].astype(F32), xhi[index // 2].astype(F32)
+    if index % 2:
+        below, above = pltpu.roll(below, 120, 1), pltpu.roll(above, 8, 1)
+    return jnp.where(first_eight(), below, above)
 
 
 def to_strip(plane, g, strip):
@@ -294,17 +300,22 @@
 
 
 def xsend_body(*refs):
-    ins, (ylo, yhi, _, out) = refs[:-4], refs[-4:]
+    ins, (ylo, yhi, _, up, down) = refs[:-5], refs[-5:]
+    strips = []
     for f, (ref, i) in enumerate(fields_of(ins)):
         strip = jnp.zeros((EY, 128), F32)
         for z, plane in enumerate(block_planes(ref, i, f, ylo, yhi)):
             strip = to_strip(plane, z, strip)
-        out[f] = strip.astype(BF16)
+        strips.append(strip)
+        if f % 2:
+            even, odd = strips[f - 1], strip
+            up[f // 2] = jnp.where(first_eight(), even, pltpu.roll(odd, 8, 1)).astype(BF16)
+            down[f // 2] = jnp.where(first_eight(), pltpu.roll(odd, 120, 1), even).astype(BF16)
 
 
 def xsend(after, *ins):
-    shape = jax.ShapeDtypeStruct((14, EY, 128), BF16)
-    return call(xsend_body, shape, far=[False] * len(ins) + [True])(*ins, after)
+    shape = jax.ShapeDtypeStruct((7, EY, 128), BF16)
+    return call(xsend_body, (shape, shape), far=[False] * len(ins) + [True])(*ins, after)
 
 
 def z_slot(f):
@@ -503,8 +514,7 @@
     ylo, yhi = exchange(*ysend(sent, *start), "gy")
     answers = owner_work(arrived, well, cross_mats)
     answers, ylo, yhi = lax.optimization_barrier((answers, ylo, yhi))
-    packed = xsend(answers, *start, ylo, yhi)
-    halo = (ylo, yhi, *exchange(packed, packed, "gx"))
+    halo = (ylo, yhi, *exchange(*xsend(answers, *start, ylo, yhi), "gx"))
     returned = lax.all_to_all(answers, ("gy", "gx"), split_axis=0, concat_axis=0, tiled=True)
     kept = (*fields, *halo, *exchange(*zsend(returned, *start, *halo), "gz"))
     ws, wx, up, down = place(returned)

time: 139 us -> 138 us (level)
  blocking collectives: 39.2 us -> 37.5 us
    all_to_all x1, blocking collectives: 21.6 us -> 19.9 us  [per_device(): lax.all_to_all(sent, ('gy', 'gx'), split_axis=0, concat_axis=0, tiled=True)]
  transfers between devices with their start and end apart: 12 -> 12, of which waited for: 7 -> 8; matrix products, arithmetic and copies ran while one was open for 0% -> 0% of each run, Pallas kernels for 4% -> 4%
where the time goes in v5:
time: 138 us
  starting transfers between devices  61.1 us (44%)
  blocking collectives  37.5 us (27%)
  waiting for transfers between devices  21.8 us (16%)
  Pallas kernels  15.4 us (11%)
  local copies, waits for them, and re-layouts  1.67 us (1%)
    ppermute x10, starting transfers between devices, exchange(): return (lax.ppermute(up, axis, forward), lax.ppermute(down, axis, backward))  31.8 us
    all_to_all x1, blocking collectives, per_device(): lax.all_to_all(sent, ('gy', 'gx'), split_axis=0, concat_axis=0, tiled=True)  19.9 us
    all_to_all x1, blocking collectives, per_device(): lax.all_to_all(answers, ('gy', 'gx'), split_axis=0, concat_axis=0, tiled=...  17.6 us
    all_to_all x1, starting transfers between devices, per_device(): lax.all_to_all(sent, ('gy', 'gx'), split_axis=0, concat_axis=0, tiled=True)  17.1 us
    ppermute x10, waiting for transfers between devices, exchange(): return (lax.ppermute(up, axis, forward), lax.ppermute(down, axis, backward))  14 us
    all_to_all x1, starting transfers between devices, per_device(): lax.all_to_all(answers, ('gy', 'gx'), split_axis=0, concat_axis=0, tiled=...  12.2 us
    pallas_call x2, Pallas kernels, sweeps(): call(functools.partial(sweeps_body, final), shape if final else (shape, j...  6.82 us
    all_to_all x1, waiting for transfers between devices, per_device(): lax.all_to_all(sent, ('gy', 'gx'), split_axis=0, concat_axis=0, tiled=True)  5.08 us
  transfers between devices with their start and end apart: 12, of which 8 were waited for; matrix products, arithmetic and copies ran while one was open for 0% of the time, Pallas kernels for 4%

profile of v5, /device:TPU:1, one launch (start us, length us, event | category | flops | bytes accessed | tf_op | source)
XLA Modules:
  0.0 137.8 jit_solution(9271598470723833304)
XLA Ops:
  0.0 0.6 copy-done.9
  0.7 0.9 copy-done.1
  1.6 1.1 shard_map.100.refs_5_
  2.8 17.1 %all-to-all-start = ((bf16[64,8,128]{2,1,0:T(8,128)(2,1)}), bf16[64,8,128]{2,1,0:T(8,128)(2,1)S(1)}, u32[]{:S(2)}, u32[]{:S(2)}) async-start(bf16[64,8,128]{2,1,0:T(8,128)(2,1)} %bitcast.3), calls=%async_computation | async-start | bytes 262144 | tf_op jit(solution)/shard_map/all_to_all | solution.py:513
  19.9 2.2 %shard_map.102 = (bf16[112,8,128]{2,1,0:T(8,128)(2,1)}, bf16[112,8,128]{2,1,0:T(8,128)(2,1)}) custom-call(f32[2,8,32,128]{3,2,1,0:T(8,128)} %refs_0_.7, f32[6,8,32,128]{3,2,1,0:T(8,128)} %refs_1_.9, f32[2,8,32,128]{3,2,1,0:T(8,128)} %refs_2_.9, f32[2,8,32,128]{3,2,1,0:T(8,128)} %refs_3_.9, f32[2,8,32,128]{3,2,1,0:T(8,128)} %refs_4_.9, ...), custom_call_target="tpu_custom_call" | custom-call | tf_op jit(solution)/shard_map/pallas_call | solution.py:293
  22.1 2.9 %collective-permute-start = (bf16[112,8,128]{2,1,0:T(8,128)(2,1)}, bf16[112,8,128]{2,1,0:T(8,128)(2,1)S(1)}, u32[]{:S(2)}, u32[]{:S(2)}) collective-permute-start(bf16[112,8,128]{2,1,0:T(8,128)(2,1)} %get-tuple-element.24), channel_id=1, source_target_pairs={{0,8},{8,16},{16,24},{24,32},{32,40},{40,48},{48,56},{1,9},{9,17},... | collective-permute-start | bytes 688136 | tf_op jit(solution)/shard_map/ppermute | solution.py:490
  25.1 1.3 collective-permute-start.1
  26.4 5.1 %all-to-all-done = bf16[64,8,128]{2,1,0:T(8,128)(2,1)S(1)} async-done(((bf16[64,8,128]{2,1,0:T(8,128)(2,1)}), bf16[64,8,128]{2,1,0:T(8,128)(2,1)S(1)}, u32[]{:S(2)}, u32[]{:S(2)}) %all-to-all-start) | async-done | bytes 131104 | tf_op jit(solution)/shard_map/all_to_all | solution.py:513
  31.5 1.7 %shard_map.101.refs_7_ = bf16[64,16,128]{2,1,0:T(8,128)(2,1)} custom-call(bf16[512,128]{1,0:T(8,128)(2,1)S(1)} %bitcast.14, bf16[4,256,256]{2,1,0:T(8,128)(2,1)S(1)} %bitcast.9, bf16[4,256,256]{2,1,0:T(8,128)(2,1)S(1)} %bitcast.11), custom_call_target="tpu_custom_call" | custom-call | tf_op jit(solution)/shard_map/pallas_call | solution.py:181
  33.2 12.2 %all-to-all-start.1 = ((bf16[64,16,128]{2,1,0:T(8,128)(2,1)}), bf16[64,16,128]{2,1,0:T(8,128)(2,1)S(1)}, u32[]{:S(2)}, u32[]{:S(2)}) async-start(bf16[64,16,128]{2,1,0:T(8,128)(2,1)} %shard_map.101.refs_7_), calls=%async_computation.1 | async-start | bytes 524288 | tf_op jit(solution)/shard_map/all_to_all | solution.py:518
  45.4 0.9 shard_map.103
  46.3 2.9 %collective-permute-start.2 = (bf16[7,48,128]{2,1,0:T(8,128)(2,1)S(1)}, bf16[7,48,128]{2,1,0:T(8,128)(2,1)S(1)}, u32[]{:S(2)}, u32[]{:S(2)}) collective-permute-start(bf16[7,48,128]{2,1,0:T(8,128)(2,1)S(1)} %get-tuple-element.29), channel_id=1, source_target_pairs={{0,1},{1,2},{2,3},{3,4},{4,5},{5,6},{6,7},{8,9},{9,10},{10,11},{11... | collective-permute-start | bytes 258056 | tf_op jit(solution)/shard_map/ppermute | solution.py:490
  49.3 1.3 collective-permute-start.3
  50.6 1.9 %collective-permute-done.2.refs_7_ = bf16[7,48,128]{2,1,0:T(8,128)(2,1)S(1)} collective-permute-done((bf16[7,48,128]{2,1,0:T(8,128)(2,1)S(1)}, bf16[7,48,128]{2,1,0:T(8,128)(2,1)S(1)}, u32[]{:S(2)}, u32[]{:S(2)}) %collective-permute-start.2) | collective-permute-done | bytes 86048 | tf_op jit(solution)/shard_map/ppermute | solution.py:490
  52.5 2.6 %collective-permute-done.3.refs_8_ = bf16[7,48,128]{2,1,0:T(8,128)(2,1)S(1)} collective-permute-done((bf16[7,48,128]{2,1,0:T(8,128)(2,1)S(1)}, bf16[7,48,128]{2,1,0:T(8,128)(2,1)S(1)}, u32[]{:S(2)}, u32[]{:S(2)}) %collective-permute-start.3) | collective-permute-done | bytes 86048 | tf_op jit(solution)/shard_map/ppermute | solution.py:490
  55.1 2.8 %all-to-all-done.1.refs_9_.arrived = bf16[64,16,128]{2,1,0:T(8,128)(2,1)S(1)} async-done(((bf16[64,16,128]{2,1,0:T(8,128)(2,1)}), bf16[64,16,128]{2,1,0:T(8,128)(2,1)S(1)}, u32[]{:S(2)}, u32[]{:S(2)}) %all-to-all-start.1) | async-done | bytes 262176 | tf_op jit(solution)/shard_map/all_to_all | solution.py:518
  58.1 8.1 %collective-permute-start.4 = (bf16[51,48,128]{2,1,0:T(8,128)(2,1)S(1)}, bf16[51,48,128]{2,1,0:T(8,128)(2,1)S(1)}, u32[]{:S(2)}, u32[]{:S(2)}) collective-permute-start(bf16[51,48,128]{2,1,0:T(8,128)(2,1)S(1)} %get-tuple-element.31), channel_id=1, source_target_pairs={{0,64},{64,128},{128,192},{192,256},{256,320},{320,384},{384,448},... | collective-permute-start | bytes 1880072 | tf_op jit(solution)/shard_map/ppermute | solution.py:490
  66.3 1.9 %collective-permute-start.5 = (bf16[51,48,128]{2,1,0:T(8,128)(2,1)S(1)}, bf16[51,48,128]{2,1,0:T(8,128)(2,1)S(1)}, u32[]{:S(2)}, u32[]{:S(2)}) collective-permute-start(bf16[51,48,128]{2,1,0:T(8,128)(2,1)S(1)} %get-tuple-element.32), channel_id=1, source_target_pairs={{64,0},{128,64},{192,128},{256,192},{320,256},{384,320},{448,384},... | collective-permute-start | bytes 1880072 | tf_op jit(solution)/shard_map/ppermute | solution.py:490
  68.2 0.6 shard_map.105
  68.8 3.6 %collective-permute-start.6 = (bf16[2,4,48,128]{3,2,1,0:T(8,128)(2,1)S(1)}, bf16[2,4,48,128]{3,2,1,0:T(8,128)(2,1)S(1)}, u32[]{:S(2)}, u32[]{:S(2)}) collective-permute-start(bf16[2,4,48,128]{3,2,1,0:T(8,128)(2,1)S(1)} %get-tuple-element.35), channel_id=1, source_target_pairs={{0,64},{64,128},{128,192},{192,256},{256,320},{320,384},{384,448},... | collective-permute-start | bytes 294920 | tf_op jit(solution)/shard_map/ppermute | solution.py:490
  72.5 1.9 %collective-permute-start.7 = (bf16[2,4,48,128]{3,2,1,0:T(8,128)(2,1)S(1)}, bf16[2,4,48,128]{3,2,1,0:T(8,128)(2,1)S(1)}, u32[]{:S(2)}, u32[]{:S(2)}) collective-permute-start(bf16[2,4,48,128]{3,2,1,0:T(8,128)(2,1)S(1)} %get-tuple-element.36), channel_id=1, source_target_pairs={{64,0},{128,64},{192,128},{256,192},{320,256},{384,320},{448,384},... | collective-permute-start | bytes 294920 | tf_op jit(solution)/shard_map/ppermute | solution.py:490
  74.5 4.4 %collective-permute-done.7.refs_14_ = bf16[2,4,48,128]{3,2,1,0:T(8,128)(2,1)S(1)} collective-permute-done((bf16[2,4,48,128]{3,2,1,0:T(8,128)(2,1)S(1)}, bf16[2,4,48,128]{3,2,1,0:T(8,128)(2,1)S(1)}, u32[]{:S(2)}, u32[]{:S(2)}) %collective-permute-start.7) | collective-permute-done | bytes 98336 | tf_op jit(solution)/shard_map/ppermute | solution.py:490
  78.9 3.3 %shard_map.106 = (f32[2,8,48,128]{3,2,1,0:T(8,128)S(1)}, f32[2,48,128]{2,1,0:T(8,128)S(1)}) custom-call(f32[2,8,32,128]{3,2,1,0:T(8,128)S(1)} %copy-done.2, f32[6,8,32,128]{3,2,1,0:T(8,128)S(1)} %copy-done, f32[2,8,32,128]{3,2,1,0:T(8,128)S(1)} %copy-done.3, f32[2,8,32,128]{3,2,1,0:T(8,128)S(1)} %copy-done.4, f32[2,8,32,128]{3,2,1,0:T(8,128)S(1)} %copy-done.5, ...), custom_call_target="tpu_custom_call" | custom-call | tf_op jit(solution)/shard_map/pallas_call | solution.py:471
  82.6 19.9 %all_to_all.32 = bf16[64,8,128]{2,1,0:T(8,128)(2,1)S(1)} all-to-all(bf16[64,8,128]{2,1,0:T(8,128)(2,1)S(1)} %bitcast.13), channel_id=1, replica_groups=mesh['gz'=8,'gy'=8,'gx'=8] {'gy','gx'}, dimensions={0} | all-to-all | bytes 262144 | tf_op jit(solution)/shard_map/all_to_all | solution.py:524
  102.5 1.0 shard_map.108
  103.5 17.6 %all_to_all.33.arrived = bf16[64,16,128]{2,1,0:T(8,128)(2,1)S(1)} all-to-all(bf16[64,16,128]{2,1,0:T(8,128)(2,1)S(1)} %shard_map.108), channel_id=1, replica_groups=mesh['gz'=8,'gy'=8,'gx'=8] {'gy','gx'}, dimensions={0} | all-to-all | bytes 524288 | tf_op jit(solution)/shard_map/all_to_all | solution.py:526
  121.0 0.6 shard_map.109
  121.7 5.6 %collective-permute-start.8 = (bf16[2,8,48,128]{3,2,1,0:T(8,128)(2,1)S(1)}, bf16[2,8,48,128]{3,2,1,0:T(8,128)(2,1)S(1)}, u32[]{:S(2)}, u32[]{:S(2)}) collective-permute-start(bf16[2,8,48,128]{3,2,1,0:T(8,128)(2,1)S(1)} %get-tuple-element.41), channel_id=1, source_target_pairs={{0,64},{64,128},{128,192},{192,256},{256,320},{320,384},{384,448},... | collective-permute-start | bytes 589832 | tf_op jit(solution)/shard_map/ppermute | solution.py:490
  127.3 2.1 %collective-permute-start.9 = (bf16[2,8,48,128]{3,2,1,0:T(8,128)(2,1)S(1)}, bf16[2,8,48,128]{3,2,1,0:T(8,128)(2,1)S(1)}, u32[]{:S(2)}, u32[]{:S(2)}) collective-permute-start(bf16[2,8,48,128]{3,2,1,0:T(8,128)(2,1)S(1)} %get-tuple-element.42), channel_id=1, source_target_pairs={{64,0},{128,64},{192,128},{256,192},{320,256},{384,320},{448,384},... | collective-permute-start | bytes 589832 | tf_op jit(solution)/shard_map/ppermute | solution.py:490
  129.4 0.5 collective-permute-done.8.refs_14_
  129.9 4.4 %collective-permute-done.9.refs_15_ = bf16[2,8,48,128]{3,2,1,0:T(8,128)(2,1)S(1)} collective-permute-done((bf16[2,8,48,128]{3,2,1,0:T(8,128)(2,1)S(1)}, bf16[2,8,48,128]{3,2,1,0:T(8,128)(2,1)S(1)}, u32[]{:S(2)}, u32[]{:S(2)}) %collective-permute-start.9) | collective-permute-done | bytes 196640 | tf_op jit(solution)/shard_map/ppermute | solution.py:490
  134.3 3.5 %shard_map.110 = f32[2,8,32,128]{3,2,1,0:T(8,128)} custom-call(f32[2,8,48,128]{3,2,1,0:T(8,128)S(1)} %get-tuple-element.37.adj.refs_0_, f32[6,8,32,128]{3,2,1,0:T(8,128)S(1)} %copy-done, f32[2,8,32,128]{3,2,1,0:T(8,128)S(1)} %copy-done.3, f32[2,8,32,128]{3,2,1,0:T(8,128)S(1)} %copy-done.4, f32[2,8,32,128]{3,2,1,0:T(8,128)S(1)} %copy-done.5, ...), custom_call_target="tpu_custom_call" | custom-call | tf_op jit(solution)/shard_map/pallas_call | solution.py:471
  (29 shorter events, 0.8 us)
Async XLA Ops:
  0.0 0.7 copy-start.9
  0.0 0.7 copy-start.10
  0.0 0.7 copy-start.11
  0.7 0.9 copy-start.1
  2.8 28.7 %all-to-all-start = ((bf16[64,8,128]{2,1,0:T(8,128)(2,1)}), bf16[64,8,128]{2,1,0:T(8,128)(2,1)S(1)}, u32[]{:S(2)}, u32[]{:S(2)}) async-start(bf16[64,8,128]{2,1,0:T(8,128)(2,1)} %bitcast.3), calls=%async_computation | async-start | bytes 262144 | tf_op jit(solution)/shard_map/all_to_all | solution.py:513
  19.9 11.6 %copy-start.6 = (bf16[1,1,1,4,256,256]{5,4,3,2,1,0:T(8,128)(2,1)S(1)}, bf16[1,1,1,4,256,256]{5,4,3,2,1,0:T(8,128)(2,1)}, u32[]{:S(2)}) copy-start(bf16[1,1,1,4,256,256]{5,4,3,2,1,0:T(8,128)(2,1)} %param.18) | copy-start | bytes 1572868
  19.9 11.5 %copy-start.7 = (bf16[1,1,1,4,256,256]{5,4,3,2,1,0:T(8,128)(2,1)S(1)}, bf16[1,1,1,4,256,256]{5,4,3,2,1,0:T(8,128)(2,1)}, u32[]{:S(2)}) copy-start(bf16[1,1,1,4,256,256]{5,4,3,2,1,0:T(8,128)(2,1)} %param.19) | copy-start | bytes 1572868
  22.1 11.0 %collective-permute-start = (bf16[112,8,128]{2,1,0:T(8,128)(2,1)}, bf16[112,8,128]{2,1,0:T(8,128)(2,1)S(1)}, u32[]{:S(2)}, u32[]{:S(2)}) collective-permute-start(bf16[112,8,128]{2,1,0:T(8,128)(2,1)} %get-tuple-element.24), channel_id=1, source_target_pairs={{0,8},{8,16},{16,24},{24,32},{32,40},{40,48},{48,56},{1,9},{9,17},... | collective-permute-start | bytes 688136 | tf_op jit(solution)/shard_map/ppermute | solution.py:490
  25.1 8.1 %collective-permute-start.1 = (bf16[112,8,128]{2,1,0:T(8,128)(2,1)}, bf16[112,8,128]{2,1,0:T(8,128)(2,1)S(1)}, u32[]{:S(2)}, u32[]{:S(2)}) collective-permute-start(bf16[112,8,128]{2,1,0:T(8,128)(2,1)} %get-tuple-element.25), channel_id=1, source_target_pairs={{8,0},{16,8},{24,16},{32,24},{40,32},{48,40},{56,48},{9,1},{17,9},... | collective-permute-start | bytes 688136 | tf_op jit(solution)/shard_map/ppermute | solution.py:490
  31.5 13.9 %copy-start = (f32[6,8,32,128]{3,2,1,0:T(8,128)S(1)}, f32[6,8,32,128]{3,2,1,0:T(8,128)}, u32[]{:S(2)}) copy-start(f32[6,8,32,128]{3,2,1,0:T(8,128)} %refs_1_.9) | copy-start | bytes 2359300
  31.5 13.9 %copy-start.4 = (f32[2,8,32,128]{3,2,1,0:T(8,128)S(1)}, f32[2,8,32,128]{3,2,1,0:T(8,128)}, u32[]{:S(2)}) copy-start(f32[2,8,32,128]{3,2,1,0:T(8,128)} %refs_3_.9) | copy-start | bytes 786436
  31.5 13.9 %copy-start.5 = (f32[2,8,32,128]{3,2,1,0:T(8,128)S(1)}, f32[2,8,32,128]{3,2,1,0:T(8,128)}, u32[]{:S(2)}) copy-start(f32[2,8,32,128]{3,2,1,0:T(8,128)} %refs_4_.9) | copy-start | bytes 786436
  33.1 12.3 %copy-start.2 = (f32[2,8,32,128]{3,2,1,0:T(8,128)S(1)}, f32[2,8,32,128]{3,2,1,0:T(8,128)}, u32[]{:S(2)}) copy-start(f32[2,8,32,128]{3,2,1,0:T(8,128)} %refs_0_.7) | copy-start | bytes 786436
  33.1 12.3 %copy-start.3 = (f32[2,8,32,128]{3,2,1,0:T(8,128)S(1)}, f32[2,8,32,128]{3,2,1,0:T(8,128)}, u32[]{:S(2)}) copy-start(f32[2,8,32,128]{3,2,1,0:T(8,128)} %refs_2_.9) | copy-start | bytes 786436
  33.2 24.7 %all-to-all-start.1 = ((bf16[64,16,128]{2,1,0:T(8,128)(2,1)}), bf16[64,16,128]{2,1,0:T(8,128)(2,1)S(1)}, u32[]{:S(2)}, u32[]{:S(2)}) async-start(bf16[64,16,128]{2,1,0:T(8,128)(2,1)} %shard_map.101.refs_7_), calls=%async_computation.1 | async-start | bytes 524288 | tf_op jit(solution)/shard_map/all_to_all | solution.py:518
  46.3 6.2 %collective-permute-start.2 = (bf16[7,48,128]{2,1,0:T(8,128)(2,1)S(1)}, bf16[7,48,128]{2,1,0:T(8,128)(2,1)S(1)}, u32[]{:S(2)}, u32[]{:S(2)}) collective-permute-start(bf16[7,48,128]{2,1,0:T(8,128)(2,1)S(1)} %get-tuple-element.29), channel_id=1, source_target_pairs={{0,1},{1,2},{2,3},{3,4},{4,5},{5,6},{6,7},{8,9},{9,10},{10,11},{11... | collective-permute-start | bytes 258056 | tf_op jit(solution)/shard_map/ppermute | solution.py:490
  49.3 5.9 %collective-permute-start.3 = (bf16[7,48,128]{2,1,0:T(8,128)(2,1)S(1)}, bf16[7,48,128]{2,1,0:T(8,128)(2,1)S(1)}, u32[]{:S(2)}, u32[]{:S(2)}) collective-permute-start(bf16[7,48,128]{2,1,0:T(8,128)(2,1)S(1)} %get-tuple-element.30), channel_id=1, source_target_pairs={{1,0},{2,1},{3,2},{4,3},{5,4},{6,5},{7,6},{9,8},{10,9},{11,10},{12... | collective-permute-start | bytes 258056 | tf_op jit(solution)/shard_map/ppermute | solution.py:490
  58.1 20.8 %collective-permute-start.4 = (bf16[51,48,128]{2,1,0:T(8,128)(2,1)S(1)}, bf16[51,48,128]{2,1,0:T(8,128)(2,1)S(1)}, u32[]{:S(2)}, u32[]{:S(2)}) collective-permute-start(bf16[51,48,128]{2,1,0:T(8,128)(2,1)S(1)} %get-tuple-element.31), channel_id=1, source_target_pairs={{0,64},{64,128},{128,192},{192,256},{256,320},{320,384},{384,448},... | collective-permute-start | bytes 1880072 | tf_op jit(solution)/shard_map/ppermute | solution.py:490
  66.3 12.7 %collective-permute-start.5 = (bf16[51,48,128]{2,1,0:T(8,128)(2,1)S(1)}, bf16[51,48,128]{2,1,0:T(8,128)(2,1)S(1)}, u32[]{:S(2)}, u32[]{:S(2)}) collective-permute-start(bf16[51,48,128]{2,1,0:T(8,128)(2,1)S(1)} %get-tuple-element.32), channel_id=1, source_target_pairs={{64,0},{128,64},{192,128},{256,192},{320,256},{384,320},{448,384},... | collective-permute-start | bytes 1880072 | tf_op jit(solution)/shard_map/ppermute | solution.py:490
  68.8 5.7 %collective-permute-start.6 = (bf16[2,4,48,128]{3,2,1,0:T(8,128)(2,1)S(1)}, bf16[2,4,48,128]{3,2,1,0:T(8,128)(2,1)S(1)}, u32[]{:S(2)}, u32[]{:S(2)}) collective-permute-start(bf16[2,4,48,128]{3,2,1,0:T(8,128)(2,1)S(1)} %get-tuple-element.35), channel_id=1, source_target_pairs={{0,64},{64,128},{128,192},{192,256},{256,320},{320,384},{384,448},... | collective-permute-start | bytes 294920 | tf_op jit(solution)/shard_map/ppermute | solution.py:490
  72.5 6.5 %collective-permute-start.7 = (bf16[2,4,48,128]{3,2,1,0:T(8,128)(2,1)S(1)}, bf16[2,4,48,128]{3,2,1,0:T(8,128)(2,1)S(1)}, u32[]{:S(2)}, u32[]{:S(2)}) collective-permute-start(bf16[2,4,48,128]{3,2,1,0:T(8,128)(2,1)S(1)} %get-tuple-element.36), channel_id=1, source_target_pairs={{64,0},{128,64},{192,128},{256,192},{320,256},{384,320},{448,384},... | collective-permute-start | bytes 294920 | tf_op jit(solution)/shard_map/ppermute | solution.py:490
  82.2 20.3 %copy-start.8 = (bf16[1,1,1,4,256,256]{5,4,3,2,1,0:T(8,128)(2,1)S(1)}, bf16[1,1,1,4,256,256]{5,4,3,2,1,0:T(8,128)(2,1)}, u32[]{:S(2)}) copy-start(bf16[1,1,1,4,256,256]{5,4,3,2,1,0:T(8,128)(2,1)} %param.19) | copy-start | bytes 1572868
  121.7 8.2 %collective-permute-start.8 = (bf16[2,8,48,128]{3,2,1,0:T(8,128)(2,1)S(1)}, bf16[2,8,48,128]{3,2,1,0:T(8,128)(2,1)S(1)}, u32[]{:S(2)}, u32[]{:S(2)}) collective-permute-start(bf16[2,8,48,128]{3,2,1,0:T(8,128)(2,1)S(1)} %get-tuple-element.41), channel_id=1, source_target_pairs={{0,64},{64,128},{128,192},{192,256},{256,320},{320,384},{384,448},... | collective-permute-start | bytes 589832 | tf_op jit(solution)/shard_map/ppermute | solution.py:490
  127.3 7.0 %collective-permute-start.9 = (bf16[2,8,48,128]{3,2,1,0:T(8,128)(2,1)S(1)}, bf16[2,8,48,128]{3,2,1,0:T(8,128)(2,1)S(1)}, u32[]{:S(2)}, u32[]{:S(2)}) collective-permute-start(bf16[2,8,48,128]{3,2,1,0:T(8,128)(2,1)S(1)} %get-tuple-element.42), channel_id=1, source_target_pairs={{64,0},{128,64},{192,128},{256,192},{320,256},{384,320},{448,384},... | collective-permute-start | bytes 589832 | tf_op jit(solution)/shard_map/ppermute | solution.py:490
